TPU v7x, 32 devices: a whole 2x2x4 slice. The times are simulated.
32 devices in a mesh: region: 4 (over y, x), dom: 8 (over z, core).
Axes of the slice: x: 2, y: 2, z: 4, core: 2. Of those that a mesh axis runs over, the one named last changes fastest.
Arguments:
- theta: float32 [64, 32768], P(None, ('region', 'dom')), may hold values from -6 to 6
- salt: float32 [64, 32768], P(None, ('region', 'dom')), may hold values from -6 to 6
- ssh: float32 [32768], P(('region', 'dom')), may hold values from -6 to 6
- depth: int32 [32768], P(('region', 'dom')), may hold values from 0 to 64, as said below
- neighbors: int32 [6, 32768], P(None, ('region', 'dom')), may hold values from 0 to 4095, as said below
- send_list: int32 [16384], P(('region', 'dom')), may hold values from 0 to 1023, as said below
- weights: float32 [6, 32768], P(None, ('region', 'dom')), may hold values from 0.01 to 0.15
- kappa: float32 [63, 32768], P(None, ('region', 'dom')), may hold values from 0.05 to 5
Outputs:
- theta_next: float32 [64, 32768], P(None, ('region', 'dom'))
- salt_next: float32 [64, 32768], P(None, ('region', 'dom'))
- ssh_next: float32 [32768], P(('region', 'dom'))
Inputs may be any that keep to these rules, and one draw needn't show every extreme that they name: `neighbors`: entries index a partition's extended list: 0 to 1023 the rim from the partition before, 1024 to 2047 its own cells, then 1024 cells of the partition after, then 512 cells from the region group below and 512 from the one above. A neighbour lies at most 1024 positions away along the partition's ordering unless it is a region boundary cell. `send_list`: each partition's 512 entries are distinct local positions of its own cells. `depth`: the share of land cells differs from partition to partition.
All inputs are finite; a program needn't handle non-finite values.
Results may differ from a plain program's by a relative error of at most 0.0003.
Values sent between devices are 32-bit elements; how exact they have to be, the bound alone decides.
No kernel may reach another device: no remote copies, remote signals or barrier semaphores. Data moves between devices by JAX's collectives and lax.ppermute only.
A program may use at most 128 MiB of HBM per device.

v0:
```python
import math

import jax
import jax.numpy as jnp
from jax import lax
from jax.sharding import PartitionSpec as P

HALO = 1024
SUB = 4


def shifted(value, axis, steps):
    count = lax.axis_size(axis)
    pairs = [(source, (source + steps) % count) for source in range(count)]
    return lax.ppermute(value, axis, pairs)


def extended_2(block, sides, width):
    for axis, dim in sides:
        count = lax.axis_size(axis)
        forward = [(i, i + 1) for i in range(count - 1)]
        backward = [(target, source) for source, target in forward]
        low = lax.ppermute(
            lax.slice_in_dim(block, block.shape[dim] - width, None, axis=dim), axis, forward
        )
        high = lax.ppermute(lax.slice_in_dim(block, 0, width, axis=dim), axis, backward)
        block = jnp.concatenate([low, block, high], axis=dim)
    return block


def column_solve(rhs, coupling):
    levels = rhs.shape[1]
    ratios = []
    scaled = []
    for level_index in range(levels):
        if level_index > 0:
            below_coupling = coupling[level_index - 1]
        else:
            below_coupling = jnp.zeros_like(coupling[0])
        if level_index < levels - 1:
            above_coupling = coupling[level_index]
        else:
            above_coupling = jnp.zeros_like(coupling[0])
        diagonal = 1.0 + below_coupling + above_coupling
        if level_index > 0:
            pivot_value = diagonal - below_coupling * ratios[-1]
            solved_value = (rhs[:, level_index] + below_coupling * scaled[-1]) / pivot_value
        else:
            pivot_value = diagonal
            solved_value = rhs[:, 0] / pivot_value
        ratios.append(above_coupling / pivot_value)
        scaled.append(solved_value)
    column_value = scaled[-1]
    results = [column_value]
    for level_index in range(levels - 2, -1, -1):
        column_value = scaled[level_index] + ratios[level_index] * column_value
        results.append(column_value)
    return jnp.stack(results[::-1], 1)


def band_window(extended, start, block_size, cell_count):
    ext_width = extended.shape[1]
    banded = lax.dynamic_slice_in_dim(extended, start, block_size + 2 * HALO, 1)
    region_part = lax.slice_in_dim(extended, cell_count + 2 * HALO, ext_width, axis=1)
    return jnp.concatenate([banded, region_part], 1)


def window_positions(index_rows, start, block_size, cell_count):
    return jnp.where(
        index_rows >= cell_count + 2 * HALO,
        index_rows - cell_count + block_size,
        index_rows - start,
    )


def region_columns(picked):
    below_rows = shifted(picked, "region", 1)
    above_rows = shifted(picked, "region", -1)
    return (below_rows, above_rows)


def surface_extended(surface, send_table):
    widened = extended_2(surface, (("dom", 0),), HALO)
    picked = jnp.dot(
        surface[None],
        send_table,
        precision=lax.Precision.HIGHEST,
        preferred_element_type=jnp.float32,
    )[0]
    below_rows = shifted(picked, "region", 1)
    above_rows = shifted(picked, "region", -1)
    return jnp.concatenate([widened, below_rows, above_rows], 0)


def body(theta, salt, ssh, depth, neighbors, send_list, weights, kappa):
    levels = theta.shape[0]
    cell_count = theta.shape[1]
    block_size = math.gcd(cell_count, 128)
    block_count = cell_count // block_size
    window_width = block_size + 2 * HALO + 2 * send_list.shape[0]
    window_ids = jnp.arange(window_width, dtype=jnp.int32)[:, None]
    block_starts = jnp.arange(block_count, dtype=jnp.int32) * block_size
    neighbor_blocks = jnp.transpose(neighbors.reshape(6, block_count, block_size), (1, 0, 2))
    weight_blocks = jnp.transpose(weights.reshape(6, block_count, block_size), (1, 0, 2))
    weight_total = jnp.sum(weights, axis=0)
    depth_float = depth.astype(jnp.float32)
    level_col = jnp.arange(levels, dtype=jnp.int32)[:, None].astype(jnp.float32)
    own_mask = (level_col < depth_float[None, :]).astype(jnp.float32)
    forcing = jnp.sum(own_mask * (0.2 * theta - 0.15 * salt), axis=0) / math.sqrt(levels)
    tracers = jnp.concatenate([theta, salt], 0)
    send_table = (jnp.arange(cell_count, dtype=jnp.int32)[:, None] == send_list[None, :]).astype(
        jnp.float32
    )
    stacked = jnp.concatenate([theta, salt, depth_float[None], ssh[None]], 0)
    widened = extended_2(stacked, (("dom", 1),), HALO)
    picked = jnp.dot(
        stacked, send_table, precision=lax.Precision.HIGHEST, preferred_element_type=jnp.float32
    )
    below_rows, above_rows = region_columns(picked)
    extended = jnp.concatenate([widened, below_rows, above_rows], 1)

    def surface_band(inputs):
        start, index_rows, weight_rows = inputs
        local = window_positions(index_rows, start, block_size, cell_count)
        band = jnp.zeros((window_width, block_size), jnp.float32)
        for slot_index in range(6):
            band = (
                band
                + (window_ids == local[slot_index][None, :]).astype(jnp.float32)
                * weight_rows[slot_index][None, :]
            )
        return band

    bands = lax.map(surface_band, (block_starts, neighbor_blocks, weight_blocks))

    def subcycle(surface, surface_ext):
        row_ext = surface_ext[None]

        def apply_band(inputs):
            start, band = inputs
            window = band_window(row_ext, start, block_size, cell_count)
            return jnp.dot(
                window, band, precision=lax.Precision.HIGHEST, preferred_element_type=jnp.float32
            )[0]

        gathered = lax.map(apply_band, (block_starts, bands)).reshape(cell_count)
        return surface + (gathered - weight_total * surface) + 0.25 * forcing

    first_surface = extended[2 * levels + 1]
    surface = subcycle(ssh, first_surface)
    for cycle_index in range(SUB - 1):
        surface = subcycle(surface, surface_extended(surface, send_table))
    column_ext = extended[: 2 * levels + 1]
    row_count = column_ext.shape[0]

    def gather_block(inputs):
        start, index_rows = inputs
        window = band_window(column_ext, start, block_size, cell_count)
        local = window_positions(index_rows, start, block_size, cell_count).reshape(
            1, 6 * block_size
        )
        table = (window_ids == local).astype(jnp.float32)
        return jnp.dot(
            window, table, precision=lax.Precision.HIGHEST, preferred_element_type=jnp.float32
        )

    gathered_all = lax.map(gather_block, (block_starts, neighbor_blocks))
    gathered_all = gathered_all.reshape(block_count, row_count, 6, block_size)
    gathered_all = jnp.transpose(gathered_all, (2, 1, 0, 3)).reshape(6, row_count, cell_count)
    both_masks = jnp.concatenate([own_mask, own_mask], 0)
    accumulated = jnp.zeros_like(tracers)
    for slot_index in range(6):
        beside = gathered_all[slot_index]
        beside_mask = (level_col < beside[2 * levels][None, :]).astype(jnp.float32)
        beside_masks = jnp.concatenate([beside_mask, beside_mask], 0)
        accumulated = accumulated + weights[slot_index] * beside_masks * (
            beside[: 2 * levels] - tracers
        )
    stepped = tracers + both_masks * accumulated
    coupling = kappa * own_mask[:-1] * own_mask[1:]
    solved = column_solve(stepped.reshape(2, levels, cell_count), coupling)
    return (solved[0], solved[1], surface)


def solution(mesh):
    in_specs = (
        P(None, ("region", "dom")),
        P(None, ("region", "dom")),
        P(("region", "dom")),
        P(("region", "dom")),
        P(None, ("region", "dom")),
        P(("region", "dom")),
        P(None, ("region", "dom")),
        P(None, ("region", "dom")),
    )
    out_specs = (P(None, ("region", "dom")), P(None, ("region", "dom")), P(("region", "dom")))
    return jax.shard_map(body, mesh=mesh, in_specs=in_specs, out_specs=out_specs, check_vma=False)
```

profile of v0, /device:TPU:0, one launch (start us, length us, event | category | flops | bytes accessed | tf_op | source)
XLA Modules:
  0.0 427.9 jit_solution(2502049548954455131)
XLA Ops:
  2.4 3.2 collective-permute-start
  6.9 2.6 fusion.44
  12.8 32.7 %while.76 = (s32[]{:T(128)}, f32[8,3200,128]{2,1,0:T(8,128)}, s32[8,6,128]{2,1,0:T(8,128)}, s32[8]{0:T(128)S(1)}, f32[8,6,128]{2,1,0:T(8,128)S(1)}, /*index=5*/s32[]{:T(128)}) while((s32[]{:T(128)}, f32[8,3200,128]{2,1,0:T(8,128)}, s32[8,6,128]{2,1,0:T(8,128)}, s32[8]{0:T(128)S(1)}, f32[8,6,128]{2,1,0:T(8,128)S(1)}, ...), condition=%wide.region_3.4_spmd.clone.clone, body=%wide.region_2.3_spmd.clone.clone.sunk | while | flops 6966274 | bytes 1669225 | solution.py:134
  52.5 137.0 %while.75 = (s32[]{:T(128)}, f32[8,129,768]{2,0,1:T(8,128)}, s32[8]{0:T(128)S(1)}, f32[129,4096]{1,0:T(8,128)S(1)}, s32[8,6,128]{2,1,0:T(8,128)}, /*index=5*/s32[]{:T(128)}, s32[]{:T(128)}, s32[]{:T(128)}) while((s32[]{:T(128)}, f32[8,129,768]{2,0,1:T(8,128)}, s32[8]{0:T(128)S(1)}, f32[129,4096]{1,0:T(8,128)S(1)}, ...), condition=%wide.region_1.0_spmd.clone, body=%wide.region_0.0_spmd.clone.sunk | while | flops 3807238144 | bytes 6944411 | solution.py:167
  56.8 3.7 fusion.272
  61.0 8.7 %dynamic_update_slice.47 = f32[8,129,768]{2,0,1:T(8,128)} dynamic-update-slice(f32[8,129,768]{2,0,1:T(8,128)} %get-tuple-element.1052, f32[1,129,768]{2,0,1:T(1,128)S(1)} %copy.327, s32[]{:T(128)S(6)} %copy.340, s32[]{:T(128)} %constant.184.clone.1..sunk.4, s32[]{:T(128)} %constant.184.clone.1..sunk.4) | dynamic-update-slice | bytes 792580 | tf_op jit(solution)/shard_map/while/body/jit(dynamic_update_index_in_dim)/dynamic_update_slice | solution.py:167
  74.0 3.7 fusion.272
  78.1 8.7 %dynamic_update_slice.47 = f32[8,129,768]{2,0,1:T(8,128)} dynamic-update-slice(f32[8,129,768]{2,0,1:T(8,128)} %get-tuple-element.1052, f32[1,129,768]{2,0,1:T(1,128)S(1)} %copy.327, s32[]{:T(128)S(6)} %copy.340, s32[]{:T(128)} %constant.184.clone.1..sunk.4, s32[]{:T(128)} %constant.184.clone.1..sunk.4) | dynamic-update-slice | bytes 792580 | tf_op jit(solution)/shard_map/while/body/jit(dynamic_update_index_in_dim)/dynamic_update_slice | solution.py:167
  91.1 3.7 fusion.272
  95.3 8.7 %dynamic_update_slice.47 = f32[8,129,768]{2,0,1:T(8,128)} dynamic-update-slice(f32[8,129,768]{2,0,1:T(8,128)} %get-tuple-element.1052, f32[1,129,768]{2,0,1:T(1,128)S(1)} %copy.327, s32[]{:T(128)S(6)} %copy.340, s32[]{:T(128)} %constant.184.clone.1..sunk.4, s32[]{:T(128)} %constant.184.clone.1..sunk.4) | dynamic-update-slice | bytes 792580 | tf_op jit(solution)/shard_map/while/body/jit(dynamic_update_index_in_dim)/dynamic_update_slice | solution.py:167
  108.2 3.7 fusion.272
  112.4 8.7 %dynamic_update_slice.47 = f32[8,129,768]{2,0,1:T(8,128)} dynamic-update-slice(f32[8,129,768]{2,0,1:T(8,128)} %get-tuple-element.1052, f32[1,129,768]{2,0,1:T(1,128)S(1)} %copy.327, s32[]{:T(128)S(6)} %copy.340, s32[]{:T(128)} %constant.184.clone.1..sunk.4, s32[]{:T(128)} %constant.184.clone.1..sunk.4) | dynamic-update-slice | bytes 792580 | tf_op jit(solution)/shard_map/while/body/jit(dynamic_update_index_in_dim)/dynamic_update_slice | solution.py:167
  125.4 3.7 fusion.272
  129.5 8.7 %dynamic_update_slice.47 = f32[8,129,768]{2,0,1:T(8,128)} dynamic-update-slice(f32[8,129,768]{2,0,1:T(8,128)} %get-tuple-element.1052, f32[1,129,768]{2,0,1:T(1,128)S(1)} %copy.327, s32[]{:T(128)S(6)} %copy.340, s32[]{:T(128)} %constant.184.clone.1..sunk.4, s32[]{:T(128)} %constant.184.clone.1..sunk.4) | dynamic-update-slice | bytes 792580 | tf_op jit(solution)/shard_map/while/body/jit(dynamic_update_index_in_dim)/dynamic_update_slice | solution.py:167
  142.5 3.7 fusion.272
  146.7 8.7 %dynamic_update_slice.47 = f32[8,129,768]{2,0,1:T(8,128)} dynamic-update-slice(f32[8,129,768]{2,0,1:T(8,128)} %get-tuple-element.1052, f32[1,129,768]{2,0,1:T(1,128)S(1)} %copy.327, s32[]{:T(128)S(6)} %copy.340, s32[]{:T(128)} %constant.184.clone.1..sunk.4, s32[]{:T(128)} %constant.184.clone.1..sunk.4) | dynamic-update-slice | bytes 792580 | tf_op jit(solution)/shard_map/while/body/jit(dynamic_update_index_in_dim)/dynamic_update_slice | solution.py:167
  159.6 3.7 fusion.272
  163.8 8.7 %dynamic_update_slice.47 = f32[8,129,768]{2,0,1:T(8,128)} dynamic-update-slice(f32[8,129,768]{2,0,1:T(8,128)} %get-tuple-element.1052, f32[1,129,768]{2,0,1:T(1,128)S(1)} %copy.327, s32[]{:T(128)S(6)} %copy.340, s32[]{:T(128)} %constant.184.clone.1..sunk.4, s32[]{:T(128)} %constant.184.clone.1..sunk.4) | dynamic-update-slice | bytes 792580 | tf_op jit(solution)/shard_map/while/body/jit(dynamic_update_index_in_dim)/dynamic_update_slice | solution.py:167
  176.7 3.7 fusion.272
  180.9 8.7 %dynamic_update_slice.47 = f32[8,129,768]{2,0,1:T(8,128)} dynamic-update-slice(f32[8,129,768]{2,0,1:T(8,128)} %get-tuple-element.1052, f32[1,129,768]{2,0,1:T(1,128)S(1)} %copy.327, s32[]{:T(128)S(6)} %copy.340, s32[]{:T(128)} %constant.184.clone.1..sunk.4, s32[]{:T(128)} %constant.184.clone.1..sunk.4) | dynamic-update-slice | bytes 792580 | tf_op jit(solution)/shard_map/while/body/jit(dynamic_update_index_in_dim)/dynamic_update_slice | solution.py:167
  190.3 3.4 fusion.243
  199.4 47.1 %while.71 = (s32[]{:T(128)}, f32[8,128]{1,0:T(8,128)S(1)}, s32[8]{0:T(128)}, f32[1,4096]{1,0:T(1,128)S(1)}, f32[8,3200,128]{2,1,0:T(8,128)}, /*index=5*/s32[]{:T(128)}, s32[]{:T(128)}, s32[]{:T(128)}) while((s32[]{:T(128)}, f32[8,128]{1,0:T(8,128)S(1)}, s32[8]{0:T(128)}, f32[1,4096]{1,0:T(1,128)S(1)}, f32[8,3200,128]{2,1,0:T(8,128)}, ...), condition=%wide.region_5.6_spmd, body=%wide.region_4.5_spmd.sunk | while | flops 4918405 | bytes 1678487 | solution.py:146
  247.2 4.1 collective-permute-start.4
  255.1 2.4 collective-permute-start.7
  264.9 4.5 %fusion.61 = f32[2,64,1024]{2,0,1:T(2,128)S(1)} fusion(pred[2,64,1024]{2,1,0:T(8,128)(4,1)S(1)} %bitcast.825, f32[2,64,1024]{2,1,0:T(8,128)S(1)} %bitcast.823, f32[2,64,1024]{2,1,0:T(8,128)S(1)} %copy-done.9, f32[2,64,1024]{2,1,0:T(8,128)S(1)} %slice.725, pred[2,64,1024]{2,1,0:T(8,128)(4,1)S(1)} %bitcast.824, pred[2,64,1024]{2,1,0:T(8,128)(4,1)S(1)} %bitcast.827, ...), kind=kLoop, calls=%fused_computation.97 | loop fusion | flops 3276800 | bytes 5529600 | tf_op jit(solution)/shard_map/add | solution.py:179
  283.8 40.2 %while.72 = (s32[]{:T(128)}, f32[8,128]{1,0:T(8,128)S(1)}, s32[8]{0:T(128)S(1)}, f32[1,4096]{1,0:T(1,128)S(1)}, f32[8,3200,128]{2,1,0:T(8,128)}, /*index=5*/s32[]{:T(128)}, s32[]{:T(128)}, s32[]{:T(128)}) while((s32[]{:T(128)}, f32[8,128]{1,0:T(8,128)S(1)}, s32[8]{0:T(128)S(1)}, f32[1,4096]{1,0:T(1,128)S(1)}, f32[8,3200,128]{2,1,0:T(8,128)}, ...), condition=%wide.region_9.10_spmd, body=%wide.region_8.9_spmd.sunk | while | flops 4918405 | bytes 1678487 | solution.py:146
  324.7 3.7 collective-permute-start.8
  330.8 2.6 collective-permute-start.11
  335.0 40.2 %while.73 = (s32[]{:T(128)}, f32[8,128]{1,0:T(8,128)S(1)}, s32[8]{0:T(128)S(1)}, f32[1,4096]{1,0:T(1,128)S(1)}, f32[8,3200,128]{2,1,0:T(8,128)}, /*index=5*/s32[]{:T(128)}, s32[]{:T(128)}, s32[]{:T(128)}) while((s32[]{:T(128)}, f32[8,128]{1,0:T(8,128)S(1)}, s32[8]{0:T(128)S(1)}, f32[1,4096]{1,0:T(1,128)S(1)}, f32[8,3200,128]{2,1,0:T(8,128)}, ...), condition=%wide.region_11.12_spmd, body=%wide.region_10.11_spmd.sunk | while | flops 4918405 | bytes 1678487 | solution.py:146
  375.2 3.7 collective-permute-start.12
  380.9 2.6 collective-permute-start.14
  387.1 40.1 %while.74 = (s32[]{:T(128)}, f32[8,128]{1,0:T(8,128)S(1)}, s32[8]{0:T(128)S(1)}, f32[1,4096]{1,0:T(1,128)S(1)}, f32[8,3200,128]{2,1,0:T(8,128)}, /*index=5*/s32[]{:T(128)}, s32[]{:T(128)}, s32[]{:T(128)}) while((s32[]{:T(128)}, f32[8,128]{1,0:T(8,128)S(1)}, s32[8]{0:T(128)S(1)}, f32[1,4096]{1,0:T(1,128)S(1)}, f32[8,3200,128]{2,1,0:T(8,128)}, ...), condition=%wide.region_13.14_spmd, body=%wide.region_12.13_spmd.sunk | while | flops 4918405 | bytes 1678487 | solution.py:146
  (646 shorter events, 212.9 us)
Async XLA Ops:
  0.6 12.2 %copy-start.17 = (f32[6,1024]{1,0:T(8,128)S(1)}, f32[6,1024]{1,0:T(8,128)}, u32[]{:S(2)}) copy-start(f32[6,1024]{1,0:T(8,128)} %param.26) | copy-start | bytes 73732
  2.4 45.9 %collective-permute-start = (f32[130,1024]{1,0:T(8,128)S(1)}, f32[130,1024]{1,0:T(8,128)}, u32[]{:S(2)}, u32[]{:S(2)}) collective-permute-start(f32[130,1024]{1,0:T(8,128)S(1)} %pad_maximum_fusion), channel_id=1, source_target_pairs={{0,1},{1,2},{2,3},{3,4},{4,5},{5,6},{6,7},{8,9},{9,10},{10,11},{11... | collective-permute-start | bytes 1597448 | tf_op jit(solution)/shard_map/ppermute | solution.py:23
  5.6 43.8 %collective-permute-start.1 = (f32[130,1024]{1,0:T(8,128)S(1)}, f32[130,1024]{1,0:T(8,128)}, u32[]{:S(2)}, u32[]{:S(2)}) collective-permute-start(f32[130,1024]{1,0:T(8,128)S(1)} %pad_maximum_fusion), channel_id=1, source_target_pairs={{1,0},{2,1},{3,2},{4,3},{5,4},{6,5},{7,6},{9,8},{10,9},{11,10},{12... | collective-permute-start | bytes 1597448 | tf_op jit(solution)/shard_map/ppermute | solution.py:26
  9.5 41.0 %collective-permute-start.2 = (f32[130,512]{1,0:T(8,128)}, f32[130,512]{1,0:T(8,128)}, u32[]{:S(2)}, u32[]{:S(2)}) collective-permute-start(f32[130,512]{1,0:T(8,128)} %fusion.44), channel_id=1, source_target_pairs={{0,8},{8,16},{16,24},{24,0},{1,9},{9,17},{17,25},{25,1},{2,10},{10... | collective-permute-start | bytes 798728 | tf_op jit(solution)/shard_map/ppermute | solution.py:15
  11.8 39.7 %collective-permute-start.3 = (f32[130,512]{1,0:T(8,128)}, f32[130,512]{1,0:T(8,128)}, u32[]{:S(2)}, u32[]{:S(2)}) collective-permute-start(f32[130,512]{1,0:T(8,128)} %fusion.44), channel_id=1, source_target_pairs={{0,24},{8,0},{16,8},{24,16},{1,25},{9,1},{17,9},{25,17},{2,26},{10... | collective-permute-start | bytes 798728 | tf_op jit(solution)/shard_map/ppermute | solution.py:15
  12.8 32.7 %copy-start = (f32[64,1024]{1,0:T(8,128)S(1)}, f32[64,1024]{1,0:T(8,128)}, u32[]{:S(2)}) copy-start(f32[64,1024]{1,0:T(8,128)} %param.21) | copy-start | bytes 786436
  12.8 32.7 %copy-start.1 = (f32[64,1024]{1,0:T(8,128)S(1)}, f32[64,1024]{1,0:T(8,128)}, u32[]{:S(2)}) copy-start(f32[64,1024]{1,0:T(8,128)} %param.20) | copy-start | bytes 786436
  199.4 47.2 %copy-start.57 = (f32[1024]{0:T(1024)S(1)}, f32[1024]{0:T(1024)}, u32[]{:S(2)}) copy-start(f32[1024]{0:T(1024)} %fusion.62) | copy-start | bytes 12292
  199.4 47.2 %copy-start.59 = (f32[1024]{0:T(1024)S(1)}, f32[1024]{0:T(1024)}, u32[]{:S(2)}) copy-start(f32[1024]{0:T(1024)} %reduce_sum.18) | copy-start | bytes 12292
  199.4 47.2 %copy-start.115 = (f32[1024]{0:T(1024)S(1)}, f32[1024]{0:T(1024)}, u32[]{:S(2)}) copy-start(f32[1024]{0:T(1024)} %param.22) | copy-start | bytes 12292
  199.4 53.2 %copy-start.116 = (s32[512]{0:T(512)S(1)}, s32[512]{0:T(512)}, u32[]{:S(2)}) copy-start(s32[512]{0:T(512)} %param.25) | copy-start | bytes 6148
  199.4 58.1 %copy-start.6 = (f32[1,128,8,128]{3,2,0,1:T(8,128)S(1)}, f32[1,128,8,128]{3,2,0,1:T(8,128)}, u32[]{:S(2)}) copy-start(f32[1,128,8,128]{3,2,0,1:T(8,128)} %get-tuple-element.713) | copy-start | bytes 1572868
  199.4 59.0 %copy-start.5 = (f32[1,128,8,128]{3,2,0,1:T(8,128)S(1)}, f32[1,128,8,128]{3,2,0,1:T(8,128)}, u32[]{:S(2)}) copy-start(f32[1,128,8,128]{3,2,0,1:T(8,128)} %get-tuple-element.714) | copy-start | bytes 1572868
  246.5 12.0 %copy-start.4 = (f32[1,128,8,128]{3,2,0,1:T(8,128)S(1)}, f32[1,128,8,128]{3,2,0,1:T(8,128)}, u32[]{:S(2)}) copy-start(f32[1,128,8,128]{3,2,0,1:T(8,128)} %get-tuple-element.715) | copy-start | bytes 1572868
  246.5 12.9 %copy-start.3 = (f32[1,128,8,128]{3,2,0,1:T(8,128)S(1)}, f32[1,128,8,128]{3,2,0,1:T(8,128)}, u32[]{:S(2)}) copy-start(f32[1,128,8,128]{3,2,0,1:T(8,128)} %get-tuple-element.716) | copy-start | bytes 1572868
  247.2 33.2 %collective-permute-start.4 = (f32[1024]{0:T(1024)}, f32[1024]{0:T(1024)}, u32[]{:S(2)}, u32[]{:S(2)}) collective-permute-start(f32[1024]{0:T(1024)} %fusion.163), channel_id=1, source_target_pairs={{0,1},{1,2},{2,3},{3,4},{4,5},{5,6},{6,7},{8,9},{9,10},{10,11},{11... | collective-permute-start | bytes 12296 | tf_op jit(solution)/shard_map/ppermute | solution.py:23
  251.3 30.5 %collective-permute-start.5 = (f32[1024]{0:T(1024)}, f32[1024]{0:T(1024)}, u32[]{:S(2)}, u32[]{:S(2)}) collective-permute-start(f32[1024]{0:T(1024)} %fusion.163), channel_id=1, source_target_pairs={{1,0},{2,1},{3,2},{4,3},{5,4},{6,5},{7,6},{9,8},{10,9},{11,10},{12... | collective-permute-start | bytes 12296 | tf_op jit(solution)/shard_map/ppermute | solution.py:26
  254.6 27.9 %collective-permute-start.6 = (f32[512]{0:T(512)}, f32[512]{0:T(512)}, u32[]{:S(2)}, u32[]{:S(2)}) collective-permute-start(f32[512]{0:T(512)} %bitcast.279), channel_id=1, source_target_pairs={{0,8},{8,16},{16,24},{24,0},{1,9},{9,17},{17,25},{25,1},{2,10},{10... | collective-permute-start | bytes 6152 | tf_op jit(solution)/shard_map/ppermute | solution.py:15
  255.1 28.1 %collective-permute-start.7 = (f32[512]{0:T(512)}, f32[512]{0:T(512)}, u32[]{:S(2)}, u32[]{:S(2)}) collective-permute-start(f32[512]{0:T(512)} %bitcast.279), channel_id=1, source_target_pairs={{0,24},{8,0},{16,8},{24,16},{1,25},{9,1},{17,9},{25,17},{2,26},{10... | collective-permute-start | bytes 6152 | tf_op jit(solution)/shard_map/ppermute | solution.py:15
  264.8 6.7 %copy-start.21 = (f32[1,1024]{1,0:T(1,128)S(1)}, f32[1,1024]{1,0:T(1,128)}, u32[]{:S(2)}) copy-start(f32[1,1024]{1,0:T(1,128)} %get-tuple-element.737) | copy-start | bytes 12292
  264.8 6.7 %copy-start.23 = (f32[1,1024]{1,0:T(1,128)S(1)}, f32[1,1024]{1,0:T(1,128)}, u32[]{:S(2)}) copy-start(f32[1,1024]{1,0:T(1,128)} %get-tuple-element.749) | copy-start | bytes 12292
  283.8 40.2 %copy-start.58 = (f32[1024]{0:T(1024)S(1)}, f32[1024]{0:T(1024)}, u32[]{:S(2)}) copy-start(f32[1024]{0:T(1024)} %fusion.62) | copy-start | bytes 12292
  283.8 40.2 %copy-start.60 = (f32[1024]{0:T(1024)S(1)}, f32[1024]{0:T(1024)}, u32[]{:S(2)}) copy-start(f32[1024]{0:T(1024)} %reduce_sum.18) | copy-start | bytes 12292
  283.8 45.9 %copy-start.117 = (s32[512]{0:T(512)S(1)}, s32[512]{0:T(512)}, u32[]{:S(2)}) copy-start(s32[512]{0:T(512)} %param.25) | copy-start | bytes 6148
  324.7 8.7 %collective-permute-start.8 = (f32[1024]{0:T(1024)S(1)}, f32[1024]{0:T(1024)S(1)}, u32[]{:S(2)}, u32[]{:S(2)}) collective-permute-start(f32[1024]{0:T(1024)S(1)} %fusion.161), channel_id=1, source_target_pairs={{0,1},{1,2},{2,3},{3,4},{4,5},{5,6},{6,7},{8,9},{9,10},{10,11},{11... | collective-permute-start | bytes 12296 | tf_op jit(solution)/shard_map/ppermute | solution.py:23
  328.4 5.0 %collective-permute-start.9 = (f32[1024]{0:T(1024)S(1)}, f32[1024]{0:T(1024)S(1)}, u32[]{:S(2)}, u32[]{:S(2)}) collective-permute-start(f32[1024]{0:T(1024)S(1)} %fusion.161), channel_id=1, source_target_pairs={{1,0},{2,1},{3,2},{4,3},{5,4},{6,5},{7,6},{9,8},{10,9},{11,10},{12... | collective-permute-start | bytes 12296 | tf_op jit(solution)/shard_map/ppermute | solution.py:26
  330.4 4.5 %collective-permute-start.10 = (f32[512]{0:T(512)S(1)}, f32[512]{0:T(512)S(1)}, u32[]{:S(2)}, u32[]{:S(2)}) collective-permute-start(f32[512]{0:T(512)S(1)} %bitcast.1309), channel_id=1, source_target_pairs={{0,8},{8,16},{16,24},{24,0},{1,9},{9,17},{17,25},{25,1},{2,10},{10... | collective-permute-start | bytes 6152 | tf_op jit(solution)/shard_map/ppermute | solution.py:15
  330.8 4.2 collective-permute-start.11
  375.2 8.6 %collective-permute-start.12 = (f32[1024]{0:T(1024)S(1)}, f32[1024]{0:T(1024)S(1)}, u32[]{:S(2)}, u32[]{:S(2)}) collective-permute-start(f32[1024]{0:T(1024)S(1)} %fusion.159), channel_id=1, source_target_pairs={{0,1},{1,2},{2,3},{3,4},{4,5},{5,6},{6,7},{8,9},{9,10},{10,11},{11... | collective-permute-start | bytes 12296 | tf_op jit(solution)/shard_map/ppermute | solution.py:23
  378.9 5.4 %collective-permute-start.13 = (f32[1024]{0:T(1024)S(1)}, f32[1024]{0:T(1024)S(1)}, u32[]{:S(2)}, u32[]{:S(2)}) collective-permute-start(f32[1024]{0:T(1024)S(1)} %fusion.159), channel_id=1, source_target_pairs={{1,0},{2,1},{3,2},{4,3},{5,4},{6,5},{7,6},{9,8},{10,9},{11,10},{12... | collective-permute-start | bytes 12296 | tf_op jit(solution)/shard_map/ppermute | solution.py:26
  380.9 4.5 %collective-permute-start.14 = (f32[512]{0:T(512)S(1)}, f32[512]{0:T(512)S(1)}, u32[]{:S(2)}, u32[]{:S(2)}) collective-permute-start(f32[512]{0:T(512)S(1)} %bitcast.1311), channel_id=1, source_target_pairs={{0,8},{8,16},{16,24},{24,0},{1,9},{9,17},{17,25},{25,1},{2,10},{10... | collective-permute-start | bytes 6152 | tf_op jit(solution)/shard_map/ppermute | solution.py:15
  383.6 3.6 collective-permute-start.15
  (104 other events, 393.3 us)
where the time goes:
time: 436 us; the launch traced here: 428 us
  local copies, waits for them, and re-layouts  136 us (31%)
  matrix products  111 us (25%)
  loops' own time  80 us (18%)
  other arithmetic  61.9 us (14%)
  starting transfers between devices  31.9 us (7%)
  waiting for transfers between devices  4.9 us (1%)
    dot_general x32, matrix products, apply_band(): jnp.dot(window, band, precision=lax.Precision.HIGHEST, preferred_element_...  74.8 us
    dynamic_update_slice x16, local copies, waits for them, and re-layouts, body(): gathered_all = lax.map(gather_block, (block_starts, neighbor_blocks))  72.6 us
    another operation x4, loops' own time, subcycle(): gathered = lax.map(apply_band, (block_starts, bands)).reshape(cell_count)  64.1 us
    dynamic_slice x56, local copies, waits for them, and re-layouts, body(): lax.map(surface_band, (block_starts, neighbor_blocks, weight_blocks))  34.3 us
    dot_general x8, matrix products, gather_block(): jnp.dot(window, table, precision=lax.Precision.HIGHEST, preferred_element...  30 us
    select_n x16, other arithmetic, window_positions(): jnp.where(index_rows >= cell_count + 2 * HALO, index_rows - cell_count +...  21.4 us
    dynamic_update_slice x8, other arithmetic, body(): lax.map(surface_band, (block_starts, neighbor_blocks, weight_blocks))  17.2 us
    another operation x1, loops' own time, body(): gathered_all = lax.map(gather_block, (block_starts, neighbor_blocks))  15.8 us
  transfers between devices with their start and end apart: 16, of which 5 were waited for; matrix products, arithmetic and copies ran while one was open for 16% of the time, Pallas kernels for 0%

commit v1 on v0

v1 whole, which is shorter than its diff:
```python
import functools
import math

import jax
import jax.numpy as jnp
from jax import lax
from jax.experimental import pallas as pl
from jax.experimental.pallas import tpu as pltpu
from jax.sharding import PartitionSpec as P

AXES = ("region", "dom")
LANES = 128
TILE = 256
ROW_DEPTH = 128
ROW_INDEX = 129
ROW_WEIGHT = 135
ROW_FORCING = 141
ROW_SURFACE = 142
ROWS = 144
SMALL = 16


def lane_gather(source, lane):
    return jnp.take_along_axis(source, lane, axis=1, mode="promise_in_bounds")


def pick_block(source_rows, positions, blocks):
    lane = positions & (LANES - 1)
    block = positions >> 7
    result = lane_gather(source_rows(0), lane)
    for b in range(1, blocks):
        result = jnp.where(block == b, lane_gather(source_rows(b), lane), result)
    return result


def prepare_kernel(theta, salt, depth8, ssh8, neighbors, weights, send4, message, picked, payload):
    levels, cells = theta.shape
    blocks = cells // LANES
    message[0:levels, :] = theta[...]
    message[levels : 2 * levels, :] = salt[...]
    message[ROW_INDEX : ROW_INDEX + 6, :] = neighbors[...].astype(jnp.float32)
    message[ROW_WEIGHT : ROW_WEIGHT + 6, :] = weights[...]
    message[ROWS - 1 : ROWS, :] = jnp.zeros((1, cells), jnp.float32)
    level = lax.broadcasted_iota(jnp.int32, (levels, LANES), 0)
    for b in range(blocks):
        cols = slice(b * LANES, (b + 1) * LANES)
        depth_row = depth8[b : b + 1, :]
        message[ROW_DEPTH : ROW_DEPTH + 1, cols] = depth_row.astype(jnp.float32)
        message[ROW_SURFACE : ROW_SURFACE + 1, cols] = ssh8[b : b + 1, :]
        term = 0.2 * theta[:, cols] - 0.15 * salt[:, cols]
        total = jnp.sum(jnp.where(level < depth_row, term, 0.0), axis=0, keepdims=True)
        message[ROW_FORCING : ROW_FORCING + 1, cols] = total / math.sqrt(levels)
    send_blocks = send4.shape[0]
    for t in range(send_blocks):
        positions = jnp.broadcast_to(send4[t : t + 1, :], (8, LANES))
        cols = slice(t * LANES, (t + 1) * LANES)
        for r in range(ROWS // 8):
            rows = slice(8 * r, 8 * r + 8)
            picked[rows, cols] = pick_block(
                lambda b: message[rows, b * LANES : (b + 1) * LANES], positions, blocks
            )
    tail = jnp.concatenate(
        [
            picked[ROW_SURFACE : ROW_SURFACE + 1, t * LANES : (t + 1) * LANES]
            for t in range(send_blocks)
        ],
        axis=0,
    )
    head = ssh8[...]

    def send(i, carry):
        payload[i, 0:blocks, :] = head
        payload[i, blocks : blocks + send_blocks, :] = tail
        return carry

    lax.fori_loop(0, payload.shape[0], send, 0)


def banded_step(ext, stat, own, sub):
    total = 0.25 * stat[8 * 13 : 8 * 14, :]
    for e in range(6):
        index = stat[8 * (1 + e) : 8 * (2 + e), :].astype(jnp.int32)
        weight = stat[8 * (7 + e) : 8 * (8 + e), :]
        lane = index & (LANES - 1)
        block = index >> 7
        key = jnp.where(block >= 24, block, block - sub)
        gathered = lane_gather(ext[0:8, :], lane)
        for d in range(1, 17):
            gathered = jnp.where(key == d, lane_gather(ext[d : d + 8, :], lane), gathered)
        for b in range(24, 32):
            row = jnp.broadcast_to(ext[b : b + 1, :], (8, LANES))
            gathered = jnp.where(key == b, lane_gather(row, lane), gathered)
        total = total + weight * (gathered - own)
    return own + total


def listed_step(ext, stat, own):
    total = 0.25 * stat[8 * 13 : 8 * 14, :]
    for e in range(6):
        index = stat[8 * (1 + e) : 8 * (2 + e), :].astype(jnp.int32)
        weight = stat[8 * (7 + e) : 8 * (8 + e), :]
        gathered = pick_block(lambda b: ext[b], index, 32)
        total = total + weight * (gathered - own)
    return own + total


def surface_kernel(
    place, heights, own_small, swap_in, swap_out, below, above, send4, out,
    stat_own, stat_left, stat_right, stat_list, ext_own, ext_left, ext_right, ext_list, *, last
):
    blocks = own_small.shape[1] // LANES
    half = below.shape[1] // LANES
    odd = place[12]
    sub = lax.broadcasted_iota(jnp.int32, (8, LANES), 0)
    for b in range(blocks):
        cols = slice(b * LANES, (b + 1) * LANES)
        rows = pl.ds(b, SMALL, stride=8)
        first = swap_in[:, cols]
        second = swap_out[:, cols]
        stat_own[rows, :] = own_small[:, cols]
        stat_left[rows, :] = jnp.where(odd == 1, first, second)
        stat_right[rows, :] = jnp.where(odd == 1, second, first)
    for b in range(half):
        cols = slice(b * LANES, (b + 1) * LANES)
        stat_list[pl.ds(b, SMALL, stride=8), :] = below[:, cols]
        stat_list[pl.ds(half + b, SMALL, stride=8), :] = above[:, cols]

    def full(n, side):
        value = heights[place[n], 0:8, :]
        if side is None:
            return value
        return jnp.where(place[13 + side] == 1, value, 0.0)

    def listed(n):
        return heights[place[n], 8:12, :]

    own = full(0, None)
    left2, left, right, right2 = full(1, 0), full(2, 1), full(3, 2), full(4, 3)
    ext_own[0:8, :] = left
    ext_own[8:16, :] = own
    ext_own[16:24, :] = right
    ext_own[24:28, :] = listed(6)
    ext_own[28:32, :] = listed(9)
    ext_left[0:8, :] = left2
    ext_left[8:16, :] = left
    ext_left[16:24, :] = own
    ext_left[24:28, :] = listed(5)
    ext_left[28:32, :] = listed(8)
    ext_right[0:8, :] = own
    ext_right[8:16, :] = right
    ext_right[16:24, :] = right2
    ext_right[24:28, :] = listed(7)
    ext_right[28:32, :] = listed(10)
    low = sub < 4
    below_ext = [full(5, 1), full(6, None), full(7, 2)]
    above_ext = [full(8, 1), full(9, None), full(10, 2)]
    for part in range(3):
        for b in range(8):
            ext_list[8 * part + b] = jnp.where(
                low,
                jnp.broadcast_to(below_ext[part][b : b + 1, :], (8, LANES)),
                jnp.broadcast_to(above_ext[part][b : b + 1, :], (8, LANES)),
            )
    own_listed = listed(0)
    tails = [(listed(11), own_listed), (own_listed, listed(17))]
    for part in range(2):
        for b in range(4):
            ext_list[24 + 4 * part + b] = jnp.where(
                low,
                jnp.broadcast_to(tails[part][0][b : b + 1, :], (8, LANES)),
                jnp.broadcast_to(tails[part][1][b : b + 1, :], (8, LANES)),
            )
    own_list = jnp.concatenate([listed(6), listed(9)], axis=0)
    new_own = banded_step(ext_own, stat_own, own, sub)
    new_left = banded_step(ext_left, stat_left, left, sub)
    new_right = banded_step(ext_right, stat_right, right, sub)
    new_list = listed_step(ext_list, stat_list, own_list)
    ext_own[0:8, :] = jnp.where(place[14] == 1, new_left, 0.0)
    ext_own[8:16, :] = new_own
    ext_own[16:24, :] = jnp.where(place[15] == 1, new_right, 0.0)
    ext_own[24:32, :] = new_list
    final = banded_step(ext_own, stat_own, new_own, sub)
    if last:
        out[...] = final
        return
    ext_left[0:8, :] = final
    positions = jnp.concatenate([send4[...], send4[...]], axis=0)
    tail = pick_block(
        lambda b: jnp.broadcast_to(ext_left[b : b + 1, :], (8, LANES)), positions, blocks
    )

    def send(i, carry):
        out[i, 0:8, :] = final
        out[i, 8:12, :] = tail[0:4, :]
        return carry

    lax.fori_loop(0, out.shape[0], send, 0)


def pivot_kernel(kappa, depth8, ratio, lower, inverse, kap):
    levels = inverse.shape[0] // 8
    cells = kappa.shape[1]
    for b in range(cells // LANES):
        cols = slice(b * LANES, (b + 1) * LANES)
        kap[pl.ds(b, levels - 1, stride=8), :] = kappa[:, cols]
    depth = depth8[...]
    before = jnp.zeros((8, LANES), jnp.float32)
    last_ratio = before
    for k in range(levels):
        rows = slice(8 * k, 8 * k + 8)
        if k < levels - 1:
            after = jnp.where(depth > k + 1, kap[rows, :], 0.0)
        else:
            after = jnp.zeros((8, LANES), jnp.float32)
        pivot = 1.0 + before + after - before * last_ratio
        inv = 1.0 / pivot
        last_ratio = after * inv
        inverse[rows, :] = inv
        lower[rows, :] = before * inv
        ratio[rows, :] = last_ratio
        before = after


def tracer_kernel(
    place, own, swap_in, swap_out, below, above, ratio, lower, inverse, theta_next, salt_next,
    rows_ext, merged, star
):
    levels, cells = theta_next.shape
    listed = below.shape[1]
    level = lax.broadcasted_iota(jnp.int32, (levels, LANES), 0).astype(jnp.float32)
    ext_width = 3 * cells + 2 * listed

    def stage(source, width, offset):
        for b in range(width // LANES):
            cols = slice(b * LANES, (b + 1) * LANES)
            target = pl.ds(offset + b * LANES, LANES)
            wet = (level < source[ROW_DEPTH : ROW_DEPTH + 1, cols]).astype(jnp.float32)
            first = source[0:levels, cols] * wet
            second = source[levels : 2 * levels, cols] * wet
            high0 = first.astype(jnp.bfloat16)
            high1 = second.astype(jnp.bfloat16)
            rows_ext[0:levels, target] = (first - high0.astype(jnp.float32)).astype(jnp.bfloat16)
            rows_ext[levels : 2 * levels, target] = (
                second - high1.astype(jnp.float32)
            ).astype(jnp.bfloat16)
            rows_ext[2 * levels : 3 * levels, target] = high0
            rows_ext[3 * levels : 4 * levels, target] = high1
            rows_ext[4 * levels : 5 * levels, target] = wet.astype(jnp.bfloat16)

    inner = pl.multiple_of(place[12] * 0 + jnp.where(place[12] == 1, 0, 2 * cells), LANES)
    outer = pl.multiple_of(jnp.where(place[12] == 1, 2 * cells, 0), LANES)
    stage(own, cells, cells)
    stage(swap_in, cells, inner)
    stage(swap_out, cells, outer)
    stage(below, listed, 3 * cells)
    stage(above, listed, 3 * cells + listed)

    index = [own[ROW_INDEX + e : ROW_INDEX + e + 1, :].astype(jnp.int32) for e in range(6)]
    weight = [own[ROW_WEIGHT + e : ROW_WEIGHT + e + 1, :] for e in range(6)]
    for e in range(5, 0, -1):
        taken = index[e] < 0
        for f in range(e):
            same = jnp.logical_and(index[e] == index[f], jnp.logical_not(taken))
            weight[f] = weight[f] + jnp.where(same, weight[e], 0.0)
            taken = jnp.logical_or(taken, same)
        index[e] = jnp.where(taken, -1, index[e])
    for e in range(6):
        merged[e : e + 1, :] = index[e].astype(jnp.float32)
        merged[8 + e : 9 + e, :] = weight[e]
    line = lax.broadcasted_iota(jnp.int32, (TILE, TILE), 0).astype(jnp.float32).astype(jnp.bfloat16)
    band = (TILE + 2 * cells) // TILE
    region = 2 * listed // TILE

    def block(t, carry):
        start = pl.multiple_of(t * TILE, TILE)
        idx = [merged[e : e + 1, pl.ds(start, TILE)].astype(jnp.int32) for e in range(6)]
        wts = [merged[8 + e : 9 + e, pl.ds(start, TILE)] for e in range(6)]
        highs = [w.astype(jnp.bfloat16) for w in wts]
        lows = [(w - h.astype(jnp.float32)).astype(jnp.bfloat16) for w, h in zip(wts, highs)]
        total = jnp.zeros((5 * levels, TILE), jnp.float32)
        extra = jnp.zeros((3 * levels, TILE), jnp.float32)
        for j in range(band + region):
            if j < band:
                base = start + j * TILE
            else:
                base = 3 * cells + (j - band) * TILE
            base = pl.multiple_of(base, TILE)
            high = jnp.zeros((TILE, TILE), jnp.bfloat16)
            low = jnp.zeros((TILE, TILE), jnp.bfloat16)
            for e in range(6):
                local = idx[e] - base
                local = jnp.where(jnp.logical_and(local >= 0, local < TILE), local, -1)
                local = local.astype(jnp.float32).astype(jnp.bfloat16)
                hit = line == local
                high = jnp.where(hit, highs[e], high)
                low = jnp.where(hit, lows[e], low)
            total = total + jnp.dot(
                rows_ext[:, pl.ds(base, TILE)], high, preferred_element_type=jnp.float32
            )
            extra = extra + jnp.dot(
                rows_ext[2 * levels :, pl.ds(base, TILE)], low, preferred_element_type=jnp.float32
            )
        wet_sum = total[4 * levels :] + extra[2 * levels :]
        for b in range(TILE // LANES):
            cols = slice(b * LANES, (b + 1) * LANES)
            here = pl.ds(start + b * LANES, LANES)
            wet = level < own[ROW_DEPTH : ROW_DEPTH + 1, here]
            for c in range(2):
                value = own[c * levels : (c + 1) * levels, here]
                acc = (
                    total[c * levels : (c + 1) * levels, cols]
                    + total[(2 + c) * levels : (3 + c) * levels, cols]
                    + extra[c * levels : (c + 1) * levels, cols]
                )
                stepped = value + jnp.where(wet, acc - value * wet_sum[:, cols], 0.0)
                star[c, pl.ds(t * (TILE // LANES) + b, levels, stride=8), :] = stepped
        return carry

    lax.fori_loop(0, cells // TILE, block, 0)
    for c in range(2):
        star[c] = star[c] * inverse[...]
    before = [star[0, 0:8, :], star[1, 0:8, :]]
    for k in range(1, levels):
        rows = slice(8 * k, 8 * k + 8)
        factor = lower[rows, :]
        for c in range(2):
            before[c] = star[c, rows, :] + factor * before[c]
            star[c, rows, :] = before[c]
    for k in range(levels - 2, -1, -1):
        rows = slice(8 * k, 8 * k + 8)
        factor = ratio[rows, :]
        for c in range(2):
            before[c] = star[c, rows, :] + factor * before[c]
            star[c, rows, :] = before[c]
    for b in range(cells // LANES):
        cols = slice(b * LANES, (b + 1) * LANES)
        theta_next[:, cols] = star[0, pl.ds(b, levels, stride=8), :]
        salt_next[:, cols] = star[1, pl.ds(b, levels, stride=8), :]


VMEM = pl.BlockSpec(memory_space=pltpu.VMEM)
SMEM = pl.BlockSpec(memory_space=pltpu.SMEM)


def estimate(flops, size):
    return pl.CostEstimate(flops=flops, bytes_accessed=size, transcendentals=0)


def body(regions, doms, theta, salt, ssh, depth, neighbors, send_list, weights, kappa):
    levels, cells = theta.shape
    listed = send_list.shape[0]
    devices = regions * doms
    f32 = jnp.float32
    depth8 = depth.reshape(cells // LANES, LANES)
    ssh8 = ssh.reshape(cells // LANES, LANES)
    send4 = send_list.reshape(listed // LANES, LANES)
    r = lax.axis_index("region")
    q = lax.axis_index("dom")

    def at(dr, dq):
        return ((r + dr) % regions) * doms + jnp.clip(q + dq, 0, doms - 1)

    place = jnp.stack(
        [
            at(0, 0), at(0, -2), at(0, -1), at(0, 1), at(0, 2),
            at(-1, -1), at(-1, 0), at(-1, 1), at(1, -1), at(1, 0), at(1, 1), at(-2, 0),
            q % 2, (q >= 2), (q >= 1), (q < doms - 1), (q < doms - 2), at(2, 0),
        ]
    ).astype(jnp.int32)
    payload_shape = jax.ShapeDtypeStruct((devices, 12, LANES), f32)
    message, picked, payload = pl.pallas_call(
        prepare_kernel,
        out_shape=(
            jax.ShapeDtypeStruct((ROWS, cells), f32),
            jax.ShapeDtypeStruct((ROWS, listed), f32),
            payload_shape,
        ),
        in_specs=[VMEM] * 7,
        out_specs=(VMEM,) * 3,
        name="prepare",
    )(theta, salt, depth8, ssh8, neighbors, weights, send4)

    def device(i, j):
        return (i % regions) * doms + j

    inner = [(device(i, j), device(i, j ^ 1)) for i in range(regions) for j in range(doms)]
    outer = [
        (device(i, j), device(i, j + 1 if j % 2 else j - 1))
        for i in range(regions)
        for j in range(1, doms - 1)
    ]
    upward = [(device(i, j), device(i + 1, j)) for i in range(regions) for j in range(doms)]
    downward = [(target, source) for source, target in upward]
    below = lax.ppermute(picked, AXES, upward)
    above = lax.ppermute(picked, AXES, downward)
    swap_in = lax.ppermute(message, AXES, inner)
    swap_out = lax.ppermute(message, AXES, outer)
    heights = lax.all_to_all(payload, AXES, 0, 0)
    ratio, lower, inverse = pl.pallas_call(
        pivot_kernel,
        out_shape=(jax.ShapeDtypeStruct((8 * levels, LANES), f32),) * 3,
        in_specs=[VMEM] * 2,
        out_specs=(VMEM,) * 3,
        scratch_shapes=[pltpu.VMEM((8 * levels, LANES), f32)],
        cost_estimate=estimate(1000000, 1000000),
        name="pivots",
    )(kappa, depth8)
    small = pl.BlockSpec((SMALL, cells), lambda *_: (ROW_DEPTH // SMALL, 0))
    small_listed = pl.BlockSpec((SMALL, listed), lambda *_: (ROW_DEPTH // SMALL, 0))

    def subcycles(values, last):
        return pl.pallas_call(
            functools.partial(surface_kernel, last=last),
            out_shape=jax.ShapeDtypeStruct((8, LANES), f32) if last else payload_shape,
            grid=(1,),
            in_specs=[SMEM, VMEM, small, small, small, small_listed, small_listed, VMEM],
            out_specs=VMEM,
            scratch_shapes=[pltpu.VMEM((8 * SMALL, LANES), f32)] * 4
            + [pltpu.VMEM((32, LANES), f32)] * 3
            + [pltpu.VMEM((32, 8, LANES), f32)],
            cost_estimate=estimate(2000000, 1000000),
            name="surface_last" if last else "surface_first",
        )(place, values, message, swap_in, swap_out, picked_below, picked_above, send4)

    picked_below, picked_above = below, above
    payload2 = subcycles(heights, False)
    heights2 = lax.all_to_all(payload2, AXES, 0, 0)
    surface = subcycles(heights2, True)
    theta_next, salt_next = pl.pallas_call(
        tracer_kernel,
        out_shape=(jax.ShapeDtypeStruct((levels, cells), f32),) * 2,
        in_specs=[SMEM] + [VMEM] * 8,
        out_specs=(VMEM,) * 2,
        scratch_shapes=[
            pltpu.VMEM((5 * levels, 3 * cells + 2 * listed), jnp.bfloat16),
            pltpu.VMEM((16, cells), f32),
            pltpu.VMEM((2, 8 * levels, LANES), f32),
        ],
        cost_estimate=estimate(4000000000, 4000000),
        compiler_params=pltpu.CompilerParams(vmem_limit_bytes=40 * 1024 * 1024),
        name="tracers",
    )(place, message, swap_in, swap_out, below, above, ratio, lower, inverse)
    return (theta_next, salt_next, surface.reshape(cells))


def solution(mesh):
    columns = P(None, AXES)
    cells = P(AXES)
    return jax.shard_map(
        functools.partial(body, mesh.shape["region"], mesh.shape["dom"]),
        mesh=mesh,
        in_specs=(columns, columns, cells, cells, columns, cells, columns, columns),
        out_specs=(columns, columns, cells),
        check_vma=False,
    )
```

time: 436 us -> 65.6 us (0.15); the launches traced: 428 us -> 65 us
  local copies, waits for them, and re-layouts: 136 us -> 10.6 us
  matrix products: 111 us -> 0 us
  loops' own time: 80 us -> 0 us
  other arithmetic: 61.9 us -> 0 us
  Pallas kernels: 0 us -> 21.4 us
  starting transfers between devices: 31.9 us -> 17.1 us
  waiting for transfers between devices: 4.9 us -> 15.2 us
    dot_general x44 -> x0, matrix products: 111 us -> none  [the longest x32 74.8 us: apply_band(): jnp.dot(window, band, precision=lax.Precision.HIGHEST, preferred_element_...]
    another operation x6 -> x0, loops' own time: 80 us -> none  [the longest x4 64.1 us: subcycle(): gathered = lax.map(apply_band, (block_starts, bands)).reshape(cell_count)]
    dynamic_update_slice x48 -> x0, local copies, waits for them, and re-layouts: 73.4 us -> none  [the longest x16 72.6 us: body(): gathered_all = lax.map(gather_block, (block_starts, neighbor_blocks))]
    dynamic_slice x96 -> x0, local copies, waits for them, and re-layouts: 40 us -> none  [the longest x56 34.3 us: body(): lax.map(surface_band, (block_starts, neighbor_blocks, weight_blocks))]
    ppermute x16 -> x4, starting transfers between devices: 31.9 us -> 4.12 us  [the longest x1 1.82 us: body(): below = lax.ppermute(picked, AXES, upward)]
    select_n x16 -> x0, other arithmetic: 21.4 us -> none  [window_positions(): jnp.where(index_rows >= cell_count + 2 * HALO, index_rows - cell_count +...]
    pallas_call x0 -> x5, Pallas kernels: none -> 21.4 us  [the longest x1 10.2 us: body(): pl.pallas_call(tracer_kernel, out_shape=(jax.ShapeDtypeStruct((levels, ce...]
    dynamic_update_slice x8 -> x0, other arithmetic: 17.2 us -> none  [body(): lax.map(surface_band, (block_starts, neighbor_blocks, weight_blocks))]
  transfers between devices with their start and end apart: 16 -> 6, of which waited for: 5 -> 2; matrix products, arithmetic and copies ran while one was open for 16% -> 1% of each run, Pallas kernels for 0% -> 19%
where the time goes in v1:
time: 65.6 us; the launch traced here: 65 us
  Pallas kernels  21.4 us (33%)
  starting transfers between devices  17.1 us (26%)
  waiting for transfers between devices  15.2 us (23%)
  local copies, waits for them, and re-layouts  10.6 us (16%)
  between operations  0.71 us (1%)
    pallas_call x1, Pallas kernels, body(): pl.pallas_call(tracer_kernel, out_shape=(jax.ShapeDtypeStruct((levels, ce...  10.2 us
    unnamed x32, local copies, waits for them, and re-layouts  10 us
    ppermute x1, waiting for transfers between devices, body(): below = lax.ppermute(picked, AXES, upward)  9.77 us
    all_to_all x1, starting transfers between devices, body(): heights = lax.all_to_all(payload, AXES, 0, 0)  8.62 us
    pallas_call x2, Pallas kernels, subcycles(): pl.pallas_call(functools.partial(surface_kernel, last=last), out_shape=ja...  5.78 us
    ppermute x1, waiting for transfers between devices, body(): above = lax.ppermute(picked, AXES, downward)  5.39 us
    all_to_all x1, starting transfers between devices, body(): heights2 = lax.all_to_all(payload2, AXES, 0, 0)  4.41 us
    pallas_call x1, Pallas kernels, body(): pl.pallas_call(prepare_kernel, out_shape=(jax.ShapeDtypeStruct((ROWS, cel...  2.94 us
  transfers between devices with their start and end apart: 6, of which 2 were waited for; matrix products, arithmetic and copies ran while one was open for 1% of the time, Pallas kernels for 19%

profile of v1, /device:TPU:0, one launch (start us, length us, event | category | flops | bytes accessed | tf_op | source)
XLA Modules:
  0.0 65.0 jit_solution(15470097995220376648)
XLA Ops:
  0.6 2.9 %prepare.1 = (f32[144,1024]{1,0:T(8,128)}, f32[144,512]{1,0:T(8,128)}, f32[32,12,128]{2,1,0:T(8,128)}) custom-call(f32[64,1024]{1,0:T(8,128)} %theta.1, f32[64,1024]{1,0:T(8,128)} %salt.1, s32[8,128]{1,0:T(8,128)} %bitcast.25, f32[8,128]{1,0:T(8,128)} %bitcast.27, s32[6,1024]{1,0:T(8,128)} %neighbors.1, f32[6,1024]{1,0:T(8,128)} %weights.1, s32[4,128]{1,0:T(4,128)} %bitcast.22), custom_call_target="tpu_custom_call" | custom-call | tf_op jit(solution)/shard_map/prepare/pallas_call | solution.py:371
  3.6 0.5 collective-permute-start
  4.0 0.7 %collective-permute-start.1 = (f32[144,1024]{1,0:T(8,128)}, f32[144,1024]{1,0:T(8,128)S(1)}, u32[]{:S(2)}, u32[]{:S(2)}) collective-permute-start(f32[144,1024]{1,0:T(8,128)} %get-tuple-element.11.own.own_small), channel_id=1, source_target_pairs={{1,2},{2,1},{3,4},{4,3},{5,6},{6,5},{9,10},{10,9},{11,12},{12,11},... | collective-permute-start | bytes 1769480 | tf_op jit(solution)/shard_map/ppermute | solution.py:397
  4.7 8.6 %all-to-all-start = ((f32[32,12,128]{2,1,0:T(8,128)}), f32[32,12,128]{2,1,0:T(8,128)S(1)}, u32[]{:S(2)}, u32[]{:S(2)}) async-start(f32[32,12,128]{2,1,0:T(8,128)} %get-tuple-element.18), calls=%async_computation | async-start | bytes 524288 | tf_op jit(solution)/shard_map/all_to_all | solution.py:398
  13.4 1.8 %collective-permute-start.2 = (f32[144,512]{1,0:T(8,128)S(1)}, f32[144,512]{1,0:T(8,128)S(1)}, u32[]{:S(2)}, u32[]{:S(2)}) collective-permute-start(f32[144,512]{1,0:T(8,128)S(1)} %copy-done.15), channel_id=1, source_target_pairs={{0,8},{1,9},{2,10},{3,11},{4,12},{5,13},{6,14},{7,15},{8,16},{9,17... | collective-permute-start | bytes 884744 | tf_op jit(solution)/shard_map/ppermute | solution.py:394
  15.2 1.2 %collective-permute-start.3 = (f32[144,512]{1,0:T(8,128)S(1)}, f32[144,512]{1,0:T(8,128)S(1)}, u32[]{:S(2)}, u32[]{:S(2)}) collective-permute-start(f32[144,512]{1,0:T(8,128)S(1)} %copy-done.15), channel_id=1, source_target_pairs={{8,0},{9,1},{10,2},{11,3},{12,4},{13,5},{14,6},{15,7},{16,8},{17,9... | collective-permute-start | bytes 884744 | tf_op jit(solution)/shard_map/ppermute | solution.py:395
  16.3 0.6 stack.91.place
  16.9 9.8 %collective-permute-done.2.below = f32[144,512]{1,0:T(8,128)S(1)} collective-permute-done((f32[144,512]{1,0:T(8,128)S(1)}, f32[144,512]{1,0:T(8,128)S(1)}, u32[]{:S(2)}, u32[]{:S(2)}) %collective-permute-start.2) | collective-permute-done | bytes 294944 | tf_op jit(solution)/shard_map/ppermute | solution.py:394
  26.7 5.4 %collective-permute-done.3.above = f32[144,512]{1,0:T(8,128)S(1)} collective-permute-done((f32[144,512]{1,0:T(8,128)S(1)}, f32[144,512]{1,0:T(8,128)S(1)}, u32[]{:S(2)}, u32[]{:S(2)}) %collective-permute-start.3) | collective-permute-done | bytes 294944 | tf_op jit(solution)/shard_map/ppermute | solution.py:395
  32.1 0.0 all-to-all-done.heights
  32.1 0.0 collective-permute-done.swap_in
  32.1 0.0 copy-start.1
  32.1 0.0 collective-permute-done.1.swap_out
  32.1 0.7 %copy-done.7 = f32[144,512]{1,0:T(8,128)} copy-done((f32[144,512]{1,0:T(8,128)}, f32[144,512]{1,0:T(8,128)S(1)}, u32[]{:S(2)}) %copy-start.7) | copy-done | bytes 294936
  32.8 0.1 copy-done.14
  32.9 0.2 copy-done.1
  33.1 0.8 %copy-done.3 = f32[144,1024]{1,0:T(8,128)} copy-done((f32[144,1024]{1,0:T(8,128)}, f32[144,1024]{1,0:T(8,128)S(1)}, u32[]{:S(2)}) %copy-start.3) | copy-done | bytes 589848
  33.9 3.1 %surface_first.1 = f32[32,12,128]{2,1,0:T(8,128)} custom-call(s32[18]{0:T(128)} %stack.91.place, f32[32,12,128]{2,1,0:T(8,128)} %copy-done.14, f32[144,1024]{1,0:T(8,128)} %get-tuple-element.11.own.own_small, f32[144,1024]{1,0:T(8,128)} %copy-done.1, f32[144,1024]{1,0:T(8,128)} %copy-done.3, f32[144,512]{1,0:T(8,128)} %copy-done.5, f32[144,512]{1,0:T(8,128)} %copy-done.7, ...), custom_call_target="tpu_custom_call" | custom-call | flops 2000000 | bytes 1000000 | tf_op jit(solution)/shard_map/surface_first/pallas_call | solution.py:412
  37.0 4.4 %all-to-all-start.1 = ((f32[32,12,128]{2,1,0:T(8,128)}), f32[32,12,128]{2,1,0:T(8,128)S(1)}, u32[]{:S(2)}, u32[]{:S(2)}) async-start(f32[32,12,128]{2,1,0:T(8,128)} %surface_first.1), calls=%async_computation.1 | async-start | bytes 524288 | tf_op jit(solution)/shard_map/all_to_all | solution.py:427
  41.4 2.5 %pivots.1 = (f32[512,128]{1,0:T(8,128)}, f32[512,128]{1,0:T(8,128)}, f32[512,128]{1,0:T(8,128)}) custom-call(f32[63,1024]{1,0:T(8,128)} %kappa.1, s32[8,128]{1,0:T(8,128)} %bitcast.26), custom_call_target="tpu_custom_call" | custom-call | flops 1000000 | bytes 1000000 | tf_op jit(solution)/shard_map/pivots/pallas_call | solution.py:399
  43.9 0.6 copy-done.9
  44.5 1.1 %copy-done.2 = f32[144,1024]{1,0:T(8,128)S(1)} copy-done((f32[144,1024]{1,0:T(8,128)S(1)}, f32[144,1024]{1,0:T(8,128)}, u32[]{:S(2)}) %copy-start.2) | copy-done | bytes 589848
  45.6 1.1 %copy-done.4 = f32[144,1024]{1,0:T(8,128)S(1)} copy-done((f32[144,1024]{1,0:T(8,128)S(1)}, f32[144,1024]{1,0:T(8,128)}, u32[]{:S(2)}) %copy-start.4) | copy-done | bytes 589848
  46.6 1.0 %copy-done.6 = f32[144,512]{1,0:T(8,128)S(1)} copy-done((f32[144,512]{1,0:T(8,128)S(1)}, f32[144,512]{1,0:T(8,128)}, u32[]{:S(2)}) %copy-start.6) | copy-done | bytes 294936
  47.6 1.0 %copy-done.8 = f32[144,512]{1,0:T(8,128)S(1)} copy-done((f32[144,512]{1,0:T(8,128)S(1)}, f32[144,512]{1,0:T(8,128)}, u32[]{:S(2)}) %copy-start.8) | copy-done | bytes 294936
  48.5 0.9 %copy-done.10 = f32[512,128]{1,0:T(8,128)S(1)} copy-done((f32[512,128]{1,0:T(8,128)S(1)}, f32[512,128]{1,0:T(8,128)}, u32[]{:S(2)}) %copy-start.10) | copy-done | bytes 262168
  49.5 0.9 %copy-done.11 = f32[512,128]{1,0:T(8,128)S(1)} copy-done((f32[512,128]{1,0:T(8,128)S(1)}, f32[512,128]{1,0:T(8,128)}, u32[]{:S(2)}) %copy-start.11) | copy-done | bytes 262168
  50.4 0.9 %copy-done.12 = f32[512,128]{1,0:T(8,128)S(1)} copy-done((f32[512,128]{1,0:T(8,128)S(1)}, f32[512,128]{1,0:T(8,128)}, u32[]{:S(2)}) %copy-start.12) | copy-done | bytes 262168
  51.4 10.2 %tracers.1 = (f32[64,1024]{1,0:T(8,128)}, f32[64,1024]{1,0:T(8,128)}) custom-call(s32[18]{0:T(128)S(1)} %copy-done.9, f32[144,1024]{1,0:T(8,128)S(1)} %copy-done, f32[144,1024]{1,0:T(8,128)S(1)} %copy-done.2, f32[144,1024]{1,0:T(8,128)S(1)} %copy-done.4, f32[144,512]{1,0:T(8,128)S(1)} %copy-done.6, f32[144,512]{1,0:T(8,128)S(1)} %copy-done.8, ...), custom_call_target="tpu_custom_call" | custom-call | flops 4000000000 | bytes 4000000 | tf_op jit(solution)/shard_map/tracers/pallas_call | solution.py:429
  61.6 0.0 all-to-all-done.1.heights
  61.6 0.7 %copy-done.13 = f32[32,12,128]{2,1,0:T(8,128)} copy-done((f32[32,12,128]{2,1,0:T(8,128)}, f32[32,12,128]{2,1,0:T(8,128)S(1)}, u32[]{:S(2)}) %copy-start.13) | copy-done | bytes 196632
  62.3 2.7 %surface_last.1 = f32[8,128]{1,0:T(8,128)} custom-call(s32[18]{0:T(128)} %stack.91.place, f32[32,12,128]{2,1,0:T(8,128)} %copy-done.13, f32[144,1024]{1,0:T(8,128)} %get-tuple-element.11.own.own_small, f32[144,1024]{1,0:T(8,128)} %copy-done.1, f32[144,1024]{1,0:T(8,128)} %copy-done.3, f32[144,512]{1,0:T(8,128)} %copy-done.5, f32[144,512]{1,0:T(8,128)} %copy-done.7, ...), custom_call_target="tpu_custom_call" | custom-call | flops 2000000 | bytes 1000000 | tf_op jit(solution)/shard_map/surface_last/pallas_call | solution.py:412
  (18 shorter events, 0.0 us)
Async XLA Ops:
  3.6 9.8 %copy-start.15 = (f32[144,512]{1,0:T(8,128)S(1)}, f32[144,512]{1,0:T(8,128)}, u32[]{:S(2)}) copy-start(f32[144,512]{1,0:T(8,128)} %get-tuple-element.12) | copy-start | bytes 884740
  3.6 28.5 %collective-permute-start = (f32[144,1024]{1,0:T(8,128)}, f32[144,1024]{1,0:T(8,128)S(1)}, u32[]{:S(2)}, u32[]{:S(2)}) collective-permute-start(f32[144,1024]{1,0:T(8,128)} %get-tuple-element.11.own.own_small), channel_id=1, source_target_pairs={{0,1},{1,0},{2,3},{3,2},{4,5},{5,4},{6,7},{7,6},{8,9},{9,8},{10,11... | collective-permute-start | bytes 1769480 | tf_op jit(solution)/shard_map/ppermute | solution.py:396
  4.0 28.1 %collective-permute-start.1 = (f32[144,1024]{1,0:T(8,128)}, f32[144,1024]{1,0:T(8,128)S(1)}, u32[]{:S(2)}, u32[]{:S(2)}) collective-permute-start(f32[144,1024]{1,0:T(8,128)} %get-tuple-element.11.own.own_small), channel_id=1, source_target_pairs={{1,2},{2,1},{3,4},{4,3},{5,6},{6,5},{9,10},{10,9},{11,12},{12,11},... | collective-permute-start | bytes 1769480 | tf_op jit(solution)/shard_map/ppermute | solution.py:397
  4.7 27.4 %all-to-all-start = ((f32[32,12,128]{2,1,0:T(8,128)}), f32[32,12,128]{2,1,0:T(8,128)S(1)}, u32[]{:S(2)}, u32[]{:S(2)}) async-start(f32[32,12,128]{2,1,0:T(8,128)} %get-tuple-element.18), calls=%async_computation | async-start | bytes 524288 | tf_op jit(solution)/shard_map/all_to_all | solution.py:398
  13.4 13.4 %collective-permute-start.2 = (f32[144,512]{1,0:T(8,128)S(1)}, f32[144,512]{1,0:T(8,128)S(1)}, u32[]{:S(2)}, u32[]{:S(2)}) collective-permute-start(f32[144,512]{1,0:T(8,128)S(1)} %copy-done.15), channel_id=1, source_target_pairs={{0,8},{1,9},{2,10},{3,11},{4,12},{5,13},{6,14},{7,15},{8,16},{9,17... | collective-permute-start | bytes 884744 | tf_op jit(solution)/shard_map/ppermute | solution.py:394
  15.2 16.9 %collective-permute-start.3 = (f32[144,512]{1,0:T(8,128)S(1)}, f32[144,512]{1,0:T(8,128)S(1)}, u32[]{:S(2)}, u32[]{:S(2)}) collective-permute-start(f32[144,512]{1,0:T(8,128)S(1)} %copy-done.15), channel_id=1, source_target_pairs={{8,0},{9,1},{10,2},{11,3},{12,4},{13,5},{14,6},{15,7},{16,8},{17,9... | collective-permute-start | bytes 884744 | tf_op jit(solution)/shard_map/ppermute | solution.py:395
  26.7 5.4 %copy-start.5 = (f32[144,512]{1,0:T(8,128)}, f32[144,512]{1,0:T(8,128)S(1)}, u32[]{:S(2)}) copy-start(f32[144,512]{1,0:T(8,128)S(1)} %collective-permute-done.2.below) | copy-start | bytes 884740
  32.1 0.7 %copy-start.7 = (f32[144,512]{1,0:T(8,128)}, f32[144,512]{1,0:T(8,128)S(1)}, u32[]{:S(2)}) copy-start(f32[144,512]{1,0:T(8,128)S(1)} %collective-permute-done.3.above) | copy-start | bytes 884740
  32.1 0.8 %copy-start.14 = (f32[32,12,128]{2,1,0:T(8,128)}, f32[32,12,128]{2,1,0:T(8,128)S(1)}, u32[]{:S(2)}) copy-start(f32[32,12,128]{2,1,0:T(8,128)S(1)} %all-to-all-done.heights) | copy-start | bytes 589828
  32.1 1.0 %copy-start.1 = (f32[144,1024]{1,0:T(8,128)}, f32[144,1024]{1,0:T(8,128)S(1)}, u32[]{:S(2)}) copy-start(f32[144,1024]{1,0:T(8,128)S(1)} %collective-permute-done.swap_in) | copy-start | bytes 1769476
  33.1 0.8 %copy-start.3 = (f32[144,1024]{1,0:T(8,128)}, f32[144,1024]{1,0:T(8,128)S(1)}, u32[]{:S(2)}) copy-start(f32[144,1024]{1,0:T(8,128)S(1)} %collective-permute-done.1.swap_out) | copy-start | bytes 1769476
  37.0 6.9 %copy-start = (f32[144,1024]{1,0:T(8,128)S(1)}, f32[144,1024]{1,0:T(8,128)}, u32[]{:S(2)}) copy-start(f32[144,1024]{1,0:T(8,128)} %get-tuple-element.11.own.own_small) | copy-start | bytes 1769476
  37.0 24.6 %all-to-all-start.1 = ((f32[32,12,128]{2,1,0:T(8,128)}), f32[32,12,128]{2,1,0:T(8,128)S(1)}, u32[]{:S(2)}, u32[]{:S(2)}) async-start(f32[32,12,128]{2,1,0:T(8,128)} %surface_first.1), calls=%async_computation.1 | async-start | bytes 524288 | tf_op jit(solution)/shard_map/all_to_all | solution.py:427
  43.9 0.6 copy-start.9
  44.5 1.1 %copy-start.2 = (f32[144,1024]{1,0:T(8,128)S(1)}, f32[144,1024]{1,0:T(8,128)}, u32[]{:S(2)}) copy-start(f32[144,1024]{1,0:T(8,128)} %copy-done.1) | copy-start | bytes 1769476
  45.5 1.1 %copy-start.4 = (f32[144,1024]{1,0:T(8,128)S(1)}, f32[144,1024]{1,0:T(8,128)}, u32[]{:S(2)}) copy-start(f32[144,1024]{1,0:T(8,128)} %copy-done.3) | copy-start | bytes 1769476
  46.6 1.0 %copy-start.6 = (f32[144,512]{1,0:T(8,128)S(1)}, f32[144,512]{1,0:T(8,128)}, u32[]{:S(2)}) copy-start(f32[144,512]{1,0:T(8,128)} %copy-done.5) | copy-start | bytes 884740
  47.6 1.0 %copy-start.8 = (f32[144,512]{1,0:T(8,128)S(1)}, f32[144,512]{1,0:T(8,128)}, u32[]{:S(2)}) copy-start(f32[144,512]{1,0:T(8,128)} %copy-done.7) | copy-start | bytes 884740
  48.5 0.9 %copy-start.10 = (f32[512,128]{1,0:T(8,128)S(1)}, f32[512,128]{1,0:T(8,128)}, u32[]{:S(2)}) copy-start(f32[512,128]{1,0:T(8,128)} %get-tuple-element.13.ratio) | copy-start | bytes 786436
  49.5 0.9 %copy-start.11 = (f32[512,128]{1,0:T(8,128)S(1)}, f32[512,128]{1,0:T(8,128)}, u32[]{:S(2)}) copy-start(f32[512,128]{1,0:T(8,128)} %get-tuple-element.14.lower) | copy-start | bytes 786436
  50.4 0.9 %copy-start.12 = (f32[512,128]{1,0:T(8,128)S(1)}, f32[512,128]{1,0:T(8,128)}, u32[]{:S(2)}) copy-start(f32[512,128]{1,0:T(8,128)} %get-tuple-element.15.inverse) | copy-start | bytes 786436
  61.6 0.7 %copy-start.13 = (f32[32,12,128]{2,1,0:T(8,128)}, f32[32,12,128]{2,1,0:T(8,128)S(1)}, u32[]{:S(2)}) copy-start(f32[32,12,128]{2,1,0:T(8,128)S(1)} %all-to-all-done.1.heights) | copy-start | bytes 589828

commit v2 on v1

v2 whole, which is shorter than its diff:
```python
import functools
import math

import jax
import jax.numpy as jnp
from jax import lax
from jax.experimental import pallas as pl
from jax.experimental.pallas import tpu as pltpu
from jax.sharding import PartitionSpec as P

AXES = ("region", "dom")
LANES = 128
TILE = 256
ROW_DEPTH = 0
ROW_INDEX = 1
ROW_WEIGHT = 7
ROW_FORCING = 13
ROW_SURFACE = 14
SMALL = 16
PART_INDEX = 192
PART_WEIGHT = 200


def lane_gather(source, lane):
    return jnp.take_along_axis(source, lane, axis=1, mode="promise_in_bounds")


def pick_block(source_rows, positions, blocks):
    lane = positions & (LANES - 1)
    block = positions >> 7
    result = lane_gather(source_rows(0), lane)
    for b in range(1, blocks):
        result = jnp.where(block == b, lane_gather(source_rows(b), lane), result)
    return result


def copies(pairs, semaphores):
    started = []
    for n, (source, target) in enumerate(pairs):
        copy = pltpu.make_async_copy(source, target, semaphores.at[n])
        copy.start()
        started.append(copy)
    return started


def prepare_kernel(
    theta_in, salt_in, depth8, ssh8, neighbors, weights, send4,
    small, picked_small, picked, payload,
    theta, salt, depths, heights, nbr, wts, sends, loaded
):
    levels, cells = theta.shape
    blocks = cells // LANES
    arrivals = copies(
        [
            (send4, sends), (ssh8, heights), (depth8, depths), (neighbors, nbr), (weights, wts),
            (theta_in, theta), (salt_in, salt),
        ],
        loaded,
    )
    for copy in arrivals[:5]:
        copy.wait()
    small[ROW_INDEX : ROW_INDEX + 6, :] = nbr[...].astype(jnp.float32)
    small[ROW_WEIGHT : ROW_WEIGHT + 6, :] = wts[...]
    small[SMALL - 1 : SMALL, :] = jnp.zeros((1, cells), jnp.float32)
    level = lax.broadcasted_iota(jnp.int32, (levels, LANES), 0)
    for b in range(blocks):
        cols = slice(b * LANES, (b + 1) * LANES)
        small[ROW_DEPTH : ROW_DEPTH + 1, cols] = depths[b : b + 1, :].astype(jnp.float32)
        small[ROW_SURFACE : ROW_SURFACE + 1, cols] = heights[b : b + 1, :]
    send_blocks = sends.shape[0]

    def pick(source, target, groups, offset):
        for t in range(send_blocks):
            positions = jnp.broadcast_to(sends[t : t + 1, :], (8, LANES))
            for r in range(groups):
                rows = slice(8 * r, 8 * r + 8)
                target[offset + 8 * r : offset + 8 * r + 8, t * LANES : (t + 1) * LANES] = pick_block(
                    lambda b: source[rows, b * LANES : (b + 1) * LANES], positions, blocks
                )

    arrivals[5].wait()
    pick(theta, picked, levels // 8, 0)
    arrivals[6].wait()
    pick(salt, picked, levels // 8, levels)
    for b in range(blocks):
        cols = slice(b * LANES, (b + 1) * LANES)
        term = 0.2 * theta[:, cols] - 0.15 * salt[:, cols]
        wet = level < depths[b : b + 1, :]
        total = jnp.sum(jnp.where(wet, term, 0.0), axis=0, keepdims=True)
        small[ROW_FORCING : ROW_FORCING + 1, cols] = total / math.sqrt(levels)
    pick(small, picked_small, SMALL // 8, 0)
    tail = jnp.concatenate(
        [
            picked_small[ROW_SURFACE : ROW_SURFACE + 1, t * LANES : (t + 1) * LANES]
            for t in range(send_blocks)
        ],
        axis=0,
    )
    head = heights[...]

    def send(i, carry):
        payload[i, 0:blocks, :] = head
        payload[i, blocks : blocks + send_blocks, :] = tail
        return carry

    lax.fori_loop(0, payload.shape[0], send, 0)


def banded_step(ext, stat, own, sub):
    total = 0.25 * stat[8 * 13 : 8 * 14, :]
    for e in range(6):
        index = stat[8 * (1 + e) : 8 * (2 + e), :].astype(jnp.int32)
        weight = stat[8 * (7 + e) : 8 * (8 + e), :]
        lane = index & (LANES - 1)
        block = index >> 7
        key = jnp.where(block >= 24, block, block - sub)
        gathered = lane_gather(ext[0:8, :], lane)
        for d in range(1, 17):
            gathered = jnp.where(key == d, lane_gather(ext[d : d + 8, :], lane), gathered)
        for b in range(24, 32):
            row = jnp.broadcast_to(ext[b : b + 1, :], (8, LANES))
            gathered = jnp.where(key == b, lane_gather(row, lane), gathered)
        total = total + weight * (gathered - own)
    return own + total


def listed_step(ext, stat, own):
    total = 0.25 * stat[8 * 13 : 8 * 14, :]
    for e in range(6):
        index = stat[8 * (1 + e) : 8 * (2 + e), :].astype(jnp.int32)
        weight = stat[8 * (7 + e) : 8 * (8 + e), :]
        gathered = pick_block(lambda b: ext[b], index, 32)
        total = total + weight * (gathered - own)
    return own + total


def surface_kernel(
    place, heights, own_in, swap_in, swap_out, below, above, sends, token, out,
    stat_own, stat_left, stat_right, stat_list, ext_own, ext_left, ext_right, ext_list, *, last
):
    blocks = own_in.shape[1] // LANES
    half = below.shape[1] // LANES
    odd = place[12]
    sub = lax.broadcasted_iota(jnp.int32, (8, LANES), 0)
    for b in range(blocks):
        cols = slice(b * LANES, (b + 1) * LANES)
        rows = pl.ds(b, SMALL, stride=8)
        first = swap_in[:, cols]
        second = swap_out[:, cols]
        stat_own[rows, :] = own_in[:, cols]
        stat_left[rows, :] = jnp.where(odd == 1, first, second)
        stat_right[rows, :] = jnp.where(odd == 1, second, first)
    for b in range(half):
        cols = slice(b * LANES, (b + 1) * LANES)
        stat_list[pl.ds(b, SMALL, stride=8), :] = below[:, cols]
        stat_list[pl.ds(half + b, SMALL, stride=8), :] = above[:, cols]

    def full(n, side):
        value = heights[place[n], 0:8, :]
        if side is None:
            return value
        return jnp.where(place[13 + side] == 1, value, 0.0)

    def listed(n):
        return heights[place[n], 8:12, :]

    own = full(0, None)
    left2, left, right, right2 = full(1, 0), full(2, 1), full(3, 2), full(4, 3)
    ext_own[0:8, :] = left
    ext_own[8:16, :] = own
    ext_own[16:24, :] = right
    ext_own[24:28, :] = listed(6)
    ext_own[28:32, :] = listed(9)
    ext_left[0:8, :] = left2
    ext_left[8:16, :] = left
    ext_left[16:24, :] = own
    ext_left[24:28, :] = listed(5)
    ext_left[28:32, :] = listed(8)
    ext_right[0:8, :] = own
    ext_right[8:16, :] = right
    ext_right[16:24, :] = right2
    ext_right[24:28, :] = listed(7)
    ext_right[28:32, :] = listed(10)
    low = sub < 4
    below_ext = [full(5, 1), full(6, None), full(7, 2)]
    above_ext = [full(8, 1), full(9, None), full(10, 2)]
    for part in range(3):
        for b in range(8):
            ext_list[8 * part + b] = jnp.where(
                low,
                jnp.broadcast_to(below_ext[part][b : b + 1, :], (8, LANES)),
                jnp.broadcast_to(above_ext[part][b : b + 1, :], (8, LANES)),
            )
    own_listed = listed(0)
    tails = [(listed(11), own_listed), (own_listed, listed(17))]
    for part in range(2):
        for b in range(4):
            ext_list[24 + 4 * part + b] = jnp.where(
                low,
                jnp.broadcast_to(tails[part][0][b : b + 1, :], (8, LANES)),
                jnp.broadcast_to(tails[part][1][b : b + 1, :], (8, LANES)),
            )
    own_list = jnp.concatenate([listed(6), listed(9)], axis=0)
    new_own = banded_step(ext_own, stat_own, own, sub)
    new_left = banded_step(ext_left, stat_left, left, sub)
    new_right = banded_step(ext_right, stat_right, right, sub)
    new_list = listed_step(ext_list, stat_list, own_list)
    ext_own[0:8, :] = jnp.where(place[14] == 1, new_left, 0.0)
    ext_own[8:16, :] = new_own
    ext_own[16:24, :] = jnp.where(place[15] == 1, new_right, 0.0)
    ext_own[24:32, :] = new_list
    final = banded_step(ext_own, stat_own, new_own, sub)
    if last:
        out[...] = final
        return
    ext_left[0:8, :] = final
    positions = jnp.concatenate([sends[...], sends[...]], axis=0)
    tail = pick_block(
        lambda b: jnp.broadcast_to(ext_left[b : b + 1, :], (8, LANES)), positions, blocks
    )

    def send(i, carry):
        out[i, 0:8, :] = final
        out[i, 8:12, :] = tail[0:4, :]
        return carry

    lax.fori_loop(0, out.shape[0], send, 0)


def stage(sources, depth, target, width, offset, level):
    levels = level.shape[0]
    for b in range(width // LANES):
        cols = slice(b * LANES, (b + 1) * LANES)
        where = pl.ds(offset + b * LANES, LANES)
        wet = (level < depth[ROW_DEPTH : ROW_DEPTH + 1, cols]).astype(jnp.float32)
        for c in range(2):
            value = sources[c][:, cols] * wet
            high = value.astype(jnp.bfloat16)
            low = (value - high.astype(jnp.float32)).astype(jnp.bfloat16)
            target[c * levels : (c + 1) * levels, where] = low
            target[(2 + c) * levels : (3 + c) * levels, where] = high
        target[4 * levels : 5 * levels, where] = wet.astype(jnp.bfloat16)


def weight_tile(line, index, highs, lows, base):
    high = jnp.zeros((TILE, TILE), jnp.bfloat16)
    low = jnp.zeros((TILE, TILE), jnp.bfloat16)
    for e in range(6):
        local = index[e] - base
        local = jnp.where(jnp.logical_and(local >= 0, local < TILE), local, -1)
        local = local.astype(jnp.float32).astype(jnp.bfloat16)
        hit = line == local
        high = jnp.where(hit, highs[e], high)
        low = jnp.where(hit, lows[e], low)
    return high, low


def tile_line():
    line = lax.broadcasted_iota(jnp.int32, (TILE, TILE), 0)
    return line.astype(jnp.float32).astype(jnp.bfloat16)


def split_weights(rows, columns):
    weights = [rows[e : e + 1, columns] for e in range(6)]
    highs = [w.astype(jnp.bfloat16) for w in weights]
    lows = [(w - h.astype(jnp.float32)).astype(jnp.bfloat16) for w, h in zip(weights, highs)]
    return highs, lows


def product(rows, columns, high, low, levels):
    first = jnp.dot(rows[:, columns], high, preferred_element_type=jnp.float32)
    second = jnp.dot(rows[2 * levels :, columns], low, preferred_element_type=jnp.float32)
    return jnp.concatenate(
        [
            first[0 : 2 * levels] + first[2 * levels : 4 * levels] + second[0 : 2 * levels],
            first[4 * levels :] + second[2 * levels :],
        ],
        axis=0,
    )


def local_kernel(
    theta_in, salt_in, small, kappa_in, depth_in, pivots, part, token,
    theta, salt, kappa, depth8, kap, rows_own, loaded
):
    cells = small.shape[1]
    levels = pivots.shape[1] // 8
    arrivals = copies(
        [(depth_in, depth8), (kappa_in, kappa), (theta_in, theta), (salt_in, salt)], loaded
    )
    for copy in arrivals[:2]:
        copy.wait()
    for b in range(cells // LANES):
        cols = slice(b * LANES, (b + 1) * LANES)
        kap[pl.ds(b, levels - 1, stride=8), :] = kappa[:, cols]
    depth = depth8[...]
    before = jnp.zeros((8, LANES), jnp.float32)
    last_ratio = before
    for k in range(levels):
        rows = slice(8 * k, 8 * k + 8)
        if k < levels - 1:
            after = jnp.where(depth > k + 1, kap[rows, :], 0.0)
        else:
            after = jnp.zeros((8, LANES), jnp.float32)
        pivot = 1.0 + before + after - before * last_ratio
        inverse = 1.0 / pivot
        last_ratio = after * inverse
        pivots[0, rows, :] = last_ratio
        pivots[1, rows, :] = before * inverse
        pivots[2, rows, :] = inverse
        before = after
    index = [small[ROW_INDEX + e : ROW_INDEX + e + 1, :].astype(jnp.int32) for e in range(6)]
    weight = [small[ROW_WEIGHT + e : ROW_WEIGHT + e + 1, :] for e in range(6)]
    for e in range(5, 0, -1):
        taken = index[e] < 0
        for f in range(e):
            same = jnp.logical_and(index[e] == index[f], jnp.logical_not(taken))
            weight[f] = weight[f] + jnp.where(same, weight[e], 0.0)
            taken = jnp.logical_or(taken, same)
        index[e] = jnp.where(taken, -1, index[e])
    for e in range(6):
        part[PART_INDEX + e : PART_INDEX + e + 1, :] = index[e].astype(jnp.float32)
        part[PART_WEIGHT + e : PART_WEIGHT + e + 1, :] = weight[e]
    token[...] = depth
    level = lax.broadcasted_iota(jnp.int32, (levels, LANES), 0).astype(jnp.float32)
    for copy in arrivals[2:]:
        copy.wait()
    stage((theta, salt), small, rows_own, cells, 0, level)
    line = tile_line()

    def block(t, carry):
        here = pl.ds(pl.multiple_of(t * TILE, TILE), TILE)
        idx = [part[PART_INDEX + e : PART_INDEX + e + 1, here].astype(jnp.int32) for e in range(6)]
        highs, lows = split_weights(part.at[pl.ds(PART_WEIGHT, 8), :], here)
        total = jnp.zeros((3 * levels, TILE), jnp.float32)
        for j in range(cells // TILE):
            high, low = weight_tile(line, idx, highs, lows, cells + j * TILE)
            columns = slice(j * TILE, (j + 1) * TILE)
            total = total + product(rows_own, columns, high, low, levels)
        part[0 : 3 * levels, here] = total
        return carry

    lax.fori_loop(0, cells // TILE, block, 0)


def tracer_kernel(
    place, theta_in, salt_in, small, theta_inner, salt_inner, small_inner, theta_outer, salt_outer,
    small_outer, below, small_below, above, small_above, pivots, part, theta_out, salt_out,
    own, rows_ext, star, result, loaded, stored
):
    levels, cells = theta_out.shape
    listed = below.shape[1]
    arrivals = copies([(theta_in, own.at[0]), (salt_in, own.at[1])], loaded)
    level = lax.broadcasted_iota(jnp.int32, (levels, LANES), 0).astype(jnp.float32)
    odd = place[12] == 1
    inner = pl.multiple_of(jnp.where(odd, 0, cells), LANES)
    outer = pl.multiple_of(jnp.where(odd, cells, 0), LANES)
    stage((theta_inner, salt_inner), small_inner, rows_ext, cells, inner, level)
    stage((theta_outer, salt_outer), small_outer, rows_ext, cells, outer, level)

    def halves(picked):
        return picked.at[pl.ds(0, levels), :], picked.at[pl.ds(levels, levels), :]

    stage(halves(below), small_below, rows_ext, listed, 2 * cells, level)
    stage(halves(above), small_above, rows_ext, listed, 2 * cells + listed, level)
    for copy in arrivals:
        copy.wait()
    line = tile_line()
    band = (TILE + cells) // TILE
    region = 2 * listed // TILE

    def block(t, carry):
        start = pl.multiple_of(t * TILE, TILE)
        here = pl.ds(start, TILE)
        idx = []
        for e in range(6):
            value = part[PART_INDEX + e : PART_INDEX + e + 1, here].astype(jnp.int32)
            outside = jnp.where(value >= 2 * cells, value - cells, -1)
            idx.append(jnp.where(value < cells, value, outside))
        highs, lows = split_weights(part.at[pl.ds(PART_WEIGHT, 8), :], here)
        total = part[0 : 3 * levels, here]
        for j in range(band + region):
            base = start + j * TILE if j < band else 2 * cells + (j - band) * TILE
            base = pl.multiple_of(base, TILE)
            high, low = weight_tile(line, idx, highs, lows, base)
            total = total + product(rows_ext, pl.ds(base, TILE), high, low, levels)
        for b in range(TILE // LANES):
            cols = slice(b * LANES, (b + 1) * LANES)
            sub = pl.ds(start + b * LANES, LANES)
            wet = level < small[ROW_DEPTH : ROW_DEPTH + 1, sub]
            for c in range(2):
                value = own[c, :, sub]
                change = total[c * levels : (c + 1) * levels, cols] - value * total[2 * levels :, cols]
                stepped = value + jnp.where(wet, change, 0.0)
                star[c, pl.ds(t * (TILE // LANES) + b, levels, stride=8), :] = stepped
        return carry

    lax.fori_loop(0, cells // TILE, block, 0)
    for c in range(2):
        star[c] = star[c] * pivots[2]
    before = [star[0, 0:8, :], star[1, 0:8, :]]
    for k in range(1, levels):
        rows = slice(8 * k, 8 * k + 8)
        factor = pivots[1, rows, :]
        for c in range(2):
            before[c] = star[c, rows, :] + factor * before[c]
            star[c, rows, :] = before[c]
    for k in range(levels - 2, -1, -1):
        rows = slice(8 * k, 8 * k + 8)
        factor = pivots[0, rows, :]
        for c in range(2):
            before[c] = star[c, rows, :] + factor * before[c]
            star[c, rows, :] = before[c]
    departures = []
    for c, out in enumerate((theta_out, salt_out)):
        for b in range(cells // LANES):
            cols = slice(b * LANES, (b + 1) * LANES)
            result[c, :, cols] = star[c, pl.ds(b, levels, stride=8), :]
            if b % 4 == 3:
                done = pl.ds((b - 3) * LANES, 4 * LANES)
                departures += copies(
                    [(result.at[c, :, done], out.at[:, done])],
                    stored.at[pl.ds(2 * c + b // 4, 1)],
                )
    for copy in departures:
        copy.wait()


HBM = pl.BlockSpec(memory_space=pltpu.HBM)
VMEM = pl.BlockSpec(memory_space=pltpu.VMEM)
SMEM = pl.BlockSpec(memory_space=pltpu.SMEM)


def grant(mebibytes):
    return pltpu.CompilerParams(vmem_limit_bytes=mebibytes * 1024 * 1024)


def estimate(flops, size):
    return pl.CostEstimate(flops=flops, bytes_accessed=size, transcendentals=0)


def body(regions, doms, theta, salt, ssh, depth, neighbors, send_list, weights, kappa):
    levels, cells = theta.shape
    listed = send_list.shape[0]
    devices = regions * doms
    f32 = jnp.float32
    depth8 = depth.reshape(cells // LANES, LANES)
    ssh8 = ssh.reshape(cells // LANES, LANES)
    send4 = send_list.reshape(listed // LANES, LANES)
    r = lax.axis_index("region")
    q = lax.axis_index("dom")

    def at(dr, dq):
        return ((r + dr) % regions) * doms + jnp.clip(q + dq, 0, doms - 1)

    place = jnp.stack(
        [
            at(0, 0), at(0, -2), at(0, -1), at(0, 1), at(0, 2),
            at(-1, -1), at(-1, 0), at(-1, 1), at(1, -1), at(1, 0), at(1, 1), at(-2, 0),
            q % 2, (q >= 2), (q >= 1), (q < doms - 1), (q < doms - 2), at(2, 0),
        ]
    ).astype(jnp.int32)
    def vmem(*shape, dtype=f32):
        return pltpu.VMEM(shape, dtype)

    def semaphores(count):
        return pltpu.SemaphoreType.DMA((count,))

    payload_shape = jax.ShapeDtypeStruct((devices, 12, LANES), f32)

    def hbm(*arrays):
        return [pltpu.with_memory_space_constraint(array, pltpu.HBM) for array in arrays]

    small, picked_small, picked, payload = pl.pallas_call(
        prepare_kernel,
        out_shape=(
            jax.ShapeDtypeStruct((SMALL, cells), f32),
            jax.ShapeDtypeStruct((SMALL, listed), f32),
            jax.ShapeDtypeStruct((2 * levels, listed), f32),
            payload_shape,
        ),
        in_specs=[HBM] * 7,
        out_specs=(VMEM,) * 4,
        scratch_shapes=[
            vmem(levels, cells), vmem(levels, cells),
            vmem(8, LANES, dtype=jnp.int32), vmem(8, LANES), vmem(6, cells, dtype=jnp.int32),
            vmem(6, cells), vmem(listed // LANES, LANES, dtype=jnp.int32), semaphores(7),
        ],
        compiler_params=grant(8),
        name="prepare",
    )(*hbm(theta, salt, depth8, ssh8, neighbors, weights, send4))

    def device(i, j):
        return (i % regions) * doms + j

    inner = [(device(i, j), device(i, j ^ 1)) for i in range(regions) for j in range(doms)]
    outer = [
        (device(i, j), device(i, j + 1 if j % 2 else j - 1))
        for i in range(regions)
        for j in range(1, doms - 1)
    ]
    upward = [(device(i, j), device(i + 1, j)) for i in range(regions) for j in range(doms)]
    downward = [(target, source) for source, target in upward]
    below = lax.ppermute(picked, AXES, upward)
    above = lax.ppermute(picked, AXES, downward)
    small_below = lax.ppermute(picked_small, AXES, upward)
    small_above = lax.ppermute(picked_small, AXES, downward)
    small_inner = lax.ppermute(small, AXES, inner)
    small_outer = lax.ppermute(small, AXES, outer)
    theta_inner = lax.ppermute(theta, AXES, inner)
    salt_inner = lax.ppermute(salt, AXES, inner)
    theta_outer = lax.ppermute(theta, AXES, outer)
    salt_outer = lax.ppermute(salt, AXES, outer)
    heights = lax.all_to_all(payload, AXES, 0, 0)
    pivots, part, token = pl.pallas_call(
        local_kernel,
        out_shape=(
            jax.ShapeDtypeStruct((3, 8 * levels, LANES), f32),
            jax.ShapeDtypeStruct((PART_WEIGHT + 8, cells), f32),
            jax.ShapeDtypeStruct((8, LANES), jnp.int32),
        ),
        in_specs=[HBM, HBM, VMEM, HBM, HBM],
        out_specs=(VMEM,) * 3,
        scratch_shapes=[
            vmem(levels, cells), vmem(levels, cells),
            vmem(levels - 1, cells), vmem(8, LANES, dtype=jnp.int32), vmem(8 * levels, LANES),
            vmem(5 * levels, cells, dtype=jnp.bfloat16), semaphores(4),
        ],
        compiler_params=grant(8),
        cost_estimate=estimate(2000000000, 4000000),
        name="local",
    )(*hbm(theta, salt), small, *hbm(kappa, depth8))
    small_below, small_above, small_inner, small_outer, heights, token, place = (
        lax.optimization_barrier(
            (small_below, small_above, small_inner, small_outer, heights, token, place)
        )
    )

    def subcycles(values, last):
        shape = jax.ShapeDtypeStruct((8, LANES), f32) if last else payload_shape
        return pl.pallas_call(
            functools.partial(surface_kernel, last=last),
            out_shape=shape,
            in_specs=[SMEM] + [VMEM] * 8,
            out_specs=VMEM,
            scratch_shapes=[vmem(8 * SMALL, LANES)] * 4
            + [vmem(32, LANES)] * 3
            + [vmem(32, 8, LANES)],
            compiler_params=grant(8),
            cost_estimate=estimate(2000000, 1000000),
            name="surface_last" if last else "surface_first",
        )(
            place, values, small, small_inner, small_outer, small_below, small_above, send4, token
        )

    heights2 = lax.all_to_all(subcycles(heights, False), AXES, 0, 0)
    surface = subcycles(heights2, True)
    theta_next, salt_next = pl.pallas_call(
        tracer_kernel,
        out_shape=(jax.ShapeDtypeStruct((levels, cells), f32),) * 2,
        in_specs=[SMEM] + [HBM] * 2 + [VMEM] * 13,
        out_specs=(HBM,) * 2,
        scratch_shapes=[
            vmem(2, levels, cells),
            vmem(5 * levels, 2 * cells + 2 * listed, dtype=jnp.bfloat16),
            vmem(2, 8 * levels, LANES), vmem(2, levels, cells), semaphores(2), semaphores(4),
        ],
        cost_estimate=estimate(4000000000, 8000000),
        compiler_params=grant(12),
        name="tracers",
    )(
        place, *hbm(theta, salt), small, theta_inner, salt_inner, small_inner, theta_outer,
        salt_outer, small_outer, below, small_below, above, small_above, pivots, part
    )
    return (theta_next, salt_next, surface.reshape(cells))


def solution(mesh):
    columns = P(None, AXES)
    cells = P(AXES)
    return jax.shard_map(
        functools.partial(body, mesh.shape["region"], mesh.shape["dom"]),
        mesh=mesh,
        in_specs=(columns, columns, cells, cells, columns, cells, columns, columns),
        out_specs=(columns, columns, cells),
        check_vma=False,
    )
```

time: 65.6 us -> 52.7 us (0.80)
  waiting for transfers between devices: 15.2 us -> 3.17 us
  starting transfers between devices: 17.1 us -> 25.8 us
  local copies, waits for them, and re-layouts: 10.6 us -> 2.11 us
  Pallas kernels: 21.4 us -> 20.3 us
    ppermute x1, waiting for transfers between devices: 9.77 us -> 0.01 us  [body(): below = lax.ppermute(picked, AXES, upward)]
    unnamed x32 -> x8, local copies, waits for them, and re-layouts: 10 us -> 2.01 us
    ppermute x2 -> x8, starting transfers between devices: 1.14 us -> 7.14 us  [the longest x1 1.77 us: body(): theta_inner = lax.ppermute(theta, AXES, inner)]
    ppermute x1, waiting for transfers between devices: 5.39 us -> 0.01 us  [body(): above = lax.ppermute(picked, AXES, downward)]
    all_to_all x1, starting transfers between devices: 4.41 us -> 9.45 us  [body(): heights2 = lax.all_to_all(subcycles(heights, False), AXES, 0, 0)]
    all_to_all x1, starting transfers between devices: 8.62 us -> 4.92 us  [body(): heights = lax.all_to_all(payload, AXES, 0, 0)]
    ppermute x2 -> x8, waiting for transfers between devices: 0.01 us -> 2.25 us  [the longest x1 2.23 us: body(): small_below = lax.ppermute(picked_small, AXES, upward)]
    pallas_call x1, Pallas kernels: 10.2 us -> 8.27 us  [body(): pl.pallas_call(tracer_kernel, out_shape=(jax.ShapeDtypeStruct((levels, ce...]
  transfers between devices with their start and end apart: 6 -> 12, of which waited for: 2 -> 2; matrix products, arithmetic and copies ran while one was open for 1% -> 0% of each run, Pallas kernels for 19% -> 29%
where the time goes in v2:
time: 52.7 us; the launch traced here: 52.3 us
  starting transfers between devices  25.8 us (49%)
  Pallas kernels  20.3 us (39%)
  waiting for transfers between devices  3.17 us (6%)
  local copies, waits for them, and re-layouts  2.11 us (4%)
  between operations  0.87 us (2%)
    all_to_all x1, starting transfers between devices, body(): heights2 = lax.all_to_all(subcycles(heights, False), AXES, 0, 0)  9.45 us
    pallas_call x1, Pallas kernels, body(): pl.pallas_call(tracer_kernel, out_shape=(jax.ShapeDtypeStruct((levels, ce...  8.27 us
    all_to_all x1, starting transfers between devices, body(): heights = lax.all_to_all(payload, AXES, 0, 0)  4.92 us
    pallas_call x2, Pallas kernels, subcycles(): pl.pallas_call(functools.partial(surface_kernel, last=last), out_shape=sh...  4.73 us
    pallas_call x1, Pallas kernels, body(): pl.pallas_call(local_kernel, out_shape=(jax.ShapeDtypeStruct((3, 8 * leve...  4.54 us
    ppermute x1, starting transfers between devices, body(): below = lax.ppermute(picked, AXES, upward)  2.99 us
    pallas_call x1, Pallas kernels, body(): pl.pallas_call(prepare_kernel, out_shape=(jax.ShapeDtypeStruct((SMALL, ce...  2.77 us
    ppermute x1, waiting for transfers between devices, body(): small_below = lax.ppermute(picked_small, AXES, upward)  2.23 us
  transfers between devices with their start and end apart: 12, of which 2 were waited for; matrix products, arithmetic and copies ran while one was open for 0% of the time, Pallas kernels for 29%

profile of v2, /device:TPU:0, one launch (start us, length us, event | category | flops | bytes accessed | tf_op | source)
XLA Modules:
  0.0 52.3 jit_solution(4369059155726055327)
XLA Ops:
  0.6 2.8 %prepare.1 = (f32[16,1024]{1,0:T(8,128)S(1)}, f32[16,512]{1,0:T(8,128)S(1)}, f32[128,512]{1,0:T(8,128)S(1)}, f32[32,12,128]{2,1,0:T(8,128)}) custom-call(f32[64,1024]{1,0:T(8,128)} %theta_in.5, f32[64,1024]{1,0:T(8,128)} %salt_in.5, s32[8,128]{1,0:T(8,128)} %bitcast.26, f32[8,128]{1,0:T(8,128)} %bitcast.25, s32[6,1024]{1,0:T(8,128)} %neighbors.1, ...), custom_call_target="tpu_custom_call" | custom-call | tf_op jit(solution)/shard_map/prepare/pallas_call | solution.py:474
  3.4 3.0 %collective-permute-start.8 = (f32[128,512]{1,0:T(8,128)S(1)}, f32[128,512]{1,0:T(8,128)S(1)}, u32[]{:S(2)}, u32[]{:S(2)}) collective-permute-start(f32[128,512]{1,0:T(8,128)S(1)} %get-tuple-element.26), channel_id=1, source_target_pairs={{0,8},{1,9},{2,10},{3,11},{4,12},{5,13},{6,14},{7,15},{8,16},{9,17... | collective-permute-start | bytes 786440 | tf_op jit(solution)/shard_map/ppermute | solution.py:504
  6.4 4.9 %all-to-all-start = ((f32[32,12,128]{2,1,0:T(8,128)}), f32[32,12,128]{2,1,0:T(8,128)S(1)}, u32[]{:S(2)}, u32[]{:S(2)}) async-start(f32[32,12,128]{2,1,0:T(8,128)} %get-tuple-element.21), calls=%async_computation | async-start | bytes 524288 | tf_op jit(solution)/shard_map/all_to_all | solution.py:514
  11.3 0.3 collective-permute-start.2
  11.7 0.7 %collective-permute-start.3 = (f32[16,1024]{1,0:T(8,128)S(1)}, f32[16,1024]{1,0:T(8,128)S(1)}, u32[]{:S(2)}, u32[]{:S(2)}) collective-permute-start(f32[16,1024]{1,0:T(8,128)S(1)} %get-tuple-element.20.small.own_in), channel_id=1, source_target_pairs={{1,2},{2,1},{3,4},{4,3},{5,6},{6,5},{9,10},{10,9},{11,12},{12,11},... | collective-permute-start | bytes 196616 | tf_op jit(solution)/shard_map/ppermute | solution.py:509
  12.3 1.7 %collective-permute-start = (f32[16,512]{1,0:T(8,128)S(1)}, f32[16,512]{1,0:T(8,128)S(1)}, u32[]{:S(2)}, u32[]{:S(2)}) collective-permute-start(f32[16,512]{1,0:T(8,128)S(1)} %get-tuple-element.19), channel_id=1, source_target_pairs={{0,8},{1,9},{2,10},{3,11},{4,12},{5,13},{6,14},{7,15},{8,16},{9,17... | collective-permute-start | bytes 98312 | tf_op jit(solution)/shard_map/ppermute | solution.py:506
  14.0 1.3 %collective-permute-start.1 = (f32[16,512]{1,0:T(8,128)S(1)}, f32[16,512]{1,0:T(8,128)S(1)}, u32[]{:S(2)}, u32[]{:S(2)}) collective-permute-start(f32[16,512]{1,0:T(8,128)S(1)} %get-tuple-element.19), channel_id=1, source_target_pairs={{8,0},{9,1},{10,2},{11,3},{12,4},{13,5},{14,6},{15,7},{16,8},{17,9... | collective-permute-start | bytes 98312 | tf_op jit(solution)/shard_map/ppermute | solution.py:507
  15.3 2.2 %collective-permute-done.small_below.below = f32[16,512]{1,0:T(8,128)S(1)} collective-permute-done((f32[16,512]{1,0:T(8,128)S(1)}, f32[16,512]{1,0:T(8,128)S(1)}, u32[]{:S(2)}, u32[]{:S(2)}) %collective-permute-start) | collective-permute-done | bytes 32800 | tf_op jit(solution)/shard_map/ppermute | solution.py:506
  17.5 1.3 %collective-permute-start.9 = (f32[128,512]{1,0:T(8,128)S(1)}, f32[128,512]{1,0:T(8,128)S(1)}, u32[]{:S(2)}, u32[]{:S(2)}) collective-permute-start(f32[128,512]{1,0:T(8,128)S(1)} %get-tuple-element.26), channel_id=1, source_target_pairs={{8,0},{9,1},{10,2},{11,3},{12,4},{13,5},{14,6},{15,7},{16,8},{17,9... | collective-permute-start | bytes 786440 | tf_op jit(solution)/shard_map/ppermute | solution.py:505
  18.9 0.0 collective-permute-done.1.small_above.above
  18.9 1.8 %collective-permute-start.4 = (f32[64,1024]{1,0:T(8,128)S(1)}, f32[64,1024]{1,0:T(8,128)S(1)}, u32[]{:S(2)}, u32[]{:S(2)}) collective-permute-start(f32[64,1024]{1,0:T(8,128)S(1)} %copy-done.3), channel_id=1, source_target_pairs={{0,1},{1,0},{2,3},{3,2},{4,5},{5,4},{6,7},{7,6},{8,9},{9,8},{10,11... | collective-permute-start | bytes 786440 | tf_op jit(solution)/shard_map/ppermute | solution.py:510
  20.6 0.0 collective-permute-done.2.small_inner.swap_in
  20.6 0.1 collective-permute-start.5
  20.7 0.0 collective-permute-done.3.small_outer.swap_out
  20.7 0.7 %collective-permute-start.6 = (f32[64,1024]{1,0:T(8,128)S(1)}, f32[64,1024]{1,0:T(8,128)S(1)}, u32[]{:S(2)}, u32[]{:S(2)}) collective-permute-start(f32[64,1024]{1,0:T(8,128)S(1)} %copy-done.3), channel_id=1, source_target_pairs={{1,2},{2,1},{3,4},{4,3},{5,6},{6,5},{9,10},{10,9},{11,12},{12,11},... | collective-permute-start | bytes 786440 | tf_op jit(solution)/shard_map/ppermute | solution.py:512
  21.4 0.0 collective-permute-done.8.below
  21.4 0.7 %collective-permute-start.7 = (f32[64,1024]{1,0:T(8,128)}, f32[64,1024]{1,0:T(8,128)S(1)}, u32[]{:S(2)}, u32[]{:S(2)}) collective-permute-start(f32[64,1024]{1,0:T(8,128)} %salt_in.5), channel_id=1, source_target_pairs={{1,2},{2,1},{3,4},{4,3},{5,6},{6,5},{9,10},{10,9},{11,12},{12,11},... | collective-permute-start | bytes 786440 | tf_op jit(solution)/shard_map/ppermute | solution.py:513
  22.2 0.1 stack.91.place
  22.3 0.0 copy-start
  22.3 4.5 %local.1 = (f32[3,512,128]{2,1,0:T(8,128)S(1)}, f32[208,1024]{1,0:T(8,128)S(1)}, s32[8,128]{1,0:T(8,128)S(1)}) custom-call(f32[64,1024]{1,0:T(8,128)} %theta_in.5, f32[64,1024]{1,0:T(8,128)} %salt_in.5, f32[16,1024]{1,0:T(8,128)S(1)} %get-tuple-element.20.small.own_in, f32[63,1024]{1,0:T(8,128)} %kappa_in.1, s32[8,128]{1,0:T(8,128)} %bitcast.27), custom_call_target="tpu_custom_call" | custom-call | flops 2000000000 | bytes 4000000 | tf_op jit(solution)/shard_map/local/pallas_call | solution.py:515
  26.8 0.9 %copy-done.1 = f32[3,512,128]{2,1,0:T(8,128)} copy-done((f32[3,512,128]{2,1,0:T(8,128)}, f32[3,512,128]{2,1,0:T(8,128)S(1)}, u32[]{:S(2)}) %copy-start.1) | copy-done | bytes 786456
  27.7 0.0 all-to-all-done.heights
  27.7 2.5 %surface_first.1 = f32[32,12,128]{2,1,0:T(8,128)} custom-call(s32[18]{0:T(128)S(1)} %stack.91.place, f32[32,12,128]{2,1,0:T(8,128)S(1)} %all-to-all-done.heights, f32[16,1024]{1,0:T(8,128)S(1)} %get-tuple-element.20.small.own_in, f32[16,1024]{1,0:T(8,128)S(1)} %collective-permute-done.2.small_inner.swap_in, ...), custom_call_target="tpu_custom_call" | custom-call | flops 2000000 | bytes 1000000 | tf_op jit(solution)/shard_map/surface_first/pallas_call | solution.py:541
  30.3 9.4 %all-to-all-start.1 = ((f32[32,12,128]{2,1,0:T(8,128)}), f32[32,12,128]{2,1,0:T(8,128)S(1)}, u32[]{:S(2)}, u32[]{:S(2)}) async-start(f32[32,12,128]{2,1,0:T(8,128)} %surface_first.1), calls=%async_computation.1 | async-start | bytes 524288 | tf_op jit(solution)/shard_map/all_to_all | solution.py:556
  39.7 0.0 collective-permute-done.9.above
  39.7 0.0 collective-permute-done.4.theta_inner
  39.7 0.0 collective-permute-done.5.salt_inner
  39.7 0.0 collective-permute-done.6.theta_outer
  39.8 1.1 %copy-done.2 = f32[3,512,128]{2,1,0:T(8,128)S(1)} copy-done((f32[3,512,128]{2,1,0:T(8,128)S(1)}, f32[3,512,128]{2,1,0:T(8,128)}, u32[]{:S(2)}) %copy-start.2) | copy-done | bytes 786456
  40.9 8.3 %tracers.1 = (f32[64,1024]{1,0:T(8,128)}, f32[64,1024]{1,0:T(8,128)}) custom-call(s32[18]{0:T(128)S(1)} %stack.91.place, f32[64,1024]{1,0:T(8,128)} %theta_in.5, f32[64,1024]{1,0:T(8,128)} %salt_in.5, f32[16,1024]{1,0:T(8,128)S(1)} %get-tuple-element.20.small.own_in, f32[64,1024]{1,0:T(8,128)S(1)} %collective-permute-done.4.theta_inner, ...), custom_call_target="tpu_custom_call" | custom-call | flops 4000000000 | bytes 8000000 | tf_op jit(solution)/shard_map/tracers/pallas_call | solution.py:558
  49.2 0.9 %all-to-all-done.1.heights = f32[32,12,128]{2,1,0:T(8,128)S(1)} async-done(((f32[32,12,128]{2,1,0:T(8,128)}), f32[32,12,128]{2,1,0:T(8,128)S(1)}, u32[]{:S(2)}, u32[]{:S(2)}) %all-to-all-start.1) | async-done | bytes 196640 | tf_op jit(solution)/shard_map/all_to_all | solution.py:556
  50.1 2.2 %surface_last.1 = f32[8,128]{1,0:T(8,128)} custom-call(s32[18]{0:T(128)S(1)} %stack.91.place, f32[32,12,128]{2,1,0:T(8,128)S(1)} %all-to-all-done.1.heights, f32[16,1024]{1,0:T(8,128)S(1)} %get-tuple-element.20.small.own_in, f32[16,1024]{1,0:T(8,128)S(1)} %collective-permute-done.2.small_inner.swap_in, ...), custom_call_target="tpu_custom_call" | custom-call | flops 2000000 | bytes 1000000 | tf_op jit(solution)/shard_map/surface_last/pallas_call | solution.py:541
  (6 shorter events, 0.0 us)
Async XLA Ops:
  3.4 18.0 %collective-permute-start.8 = (f32[128,512]{1,0:T(8,128)S(1)}, f32[128,512]{1,0:T(8,128)S(1)}, u32[]{:S(2)}, u32[]{:S(2)}) collective-permute-start(f32[128,512]{1,0:T(8,128)S(1)} %get-tuple-element.26), channel_id=1, source_target_pairs={{0,8},{1,9},{2,10},{3,11},{4,12},{5,13},{6,14},{7,15},{8,16},{9,17... | collective-permute-start | bytes 786440 | tf_op jit(solution)/shard_map/ppermute | solution.py:504
  6.4 12.5 %copy-start.3 = (f32[64,1024]{1,0:T(8,128)S(1)}, f32[64,1024]{1,0:T(8,128)}, u32[]{:S(2)}) copy-start(f32[64,1024]{1,0:T(8,128)} %theta_in.5) | copy-start | bytes 786436
  6.4 21.3 %all-to-all-start = ((f32[32,12,128]{2,1,0:T(8,128)}), f32[32,12,128]{2,1,0:T(8,128)S(1)}, u32[]{:S(2)}, u32[]{:S(2)}) async-start(f32[32,12,128]{2,1,0:T(8,128)} %get-tuple-element.21), calls=%async_computation | async-start | bytes 524288 | tf_op jit(solution)/shard_map/all_to_all | solution.py:514
  11.3 9.3 %collective-permute-start.2 = (f32[16,1024]{1,0:T(8,128)S(1)}, f32[16,1024]{1,0:T(8,128)S(1)}, u32[]{:S(2)}, u32[]{:S(2)}) collective-permute-start(f32[16,1024]{1,0:T(8,128)S(1)} %get-tuple-element.20.small.own_in), channel_id=1, source_target_pairs={{0,1},{1,0},{2,3},{3,2},{4,5},{5,4},{6,7},{7,6},{8,9},{9,8},{10,11... | collective-permute-start | bytes 196616 | tf_op jit(solution)/shard_map/ppermute | solution.py:508
  11.7 9.1 %collective-permute-start.3 = (f32[16,1024]{1,0:T(8,128)S(1)}, f32[16,1024]{1,0:T(8,128)S(1)}, u32[]{:S(2)}, u32[]{:S(2)}) collective-permute-start(f32[16,1024]{1,0:T(8,128)S(1)} %get-tuple-element.20.small.own_in), channel_id=1, source_target_pairs={{1,2},{2,1},{3,4},{4,3},{5,6},{6,5},{9,10},{10,9},{11,12},{12,11},... | collective-permute-start | bytes 196616 | tf_op jit(solution)/shard_map/ppermute | solution.py:509
  12.3 5.2 %collective-permute-start = (f32[16,512]{1,0:T(8,128)S(1)}, f32[16,512]{1,0:T(8,128)S(1)}, u32[]{:S(2)}, u32[]{:S(2)}) collective-permute-start(f32[16,512]{1,0:T(8,128)S(1)} %get-tuple-element.19), channel_id=1, source_target_pairs={{0,8},{1,9},{2,10},{3,11},{4,12},{5,13},{6,14},{7,15},{8,16},{9,17... | collective-permute-start | bytes 98312 | tf_op jit(solution)/shard_map/ppermute | solution.py:506
  14.0 4.8 %collective-permute-start.1 = (f32[16,512]{1,0:T(8,128)S(1)}, f32[16,512]{1,0:T(8,128)S(1)}, u32[]{:S(2)}, u32[]{:S(2)}) collective-permute-start(f32[16,512]{1,0:T(8,128)S(1)} %get-tuple-element.19), channel_id=1, source_target_pairs={{8,0},{9,1},{10,2},{11,3},{12,4},{13,5},{14,6},{15,7},{16,8},{17,9... | collective-permute-start | bytes 98312 | tf_op jit(solution)/shard_map/ppermute | solution.py:507
  17.5 22.2 %collective-permute-start.9 = (f32[128,512]{1,0:T(8,128)S(1)}, f32[128,512]{1,0:T(8,128)S(1)}, u32[]{:S(2)}, u32[]{:S(2)}) collective-permute-start(f32[128,512]{1,0:T(8,128)S(1)} %get-tuple-element.26), channel_id=1, source_target_pairs={{8,0},{9,1},{10,2},{11,3},{12,4},{13,5},{14,6},{15,7},{16,8},{17,9... | collective-permute-start | bytes 786440 | tf_op jit(solution)/shard_map/ppermute | solution.py:505
  18.9 20.9 %collective-permute-start.4 = (f32[64,1024]{1,0:T(8,128)S(1)}, f32[64,1024]{1,0:T(8,128)S(1)}, u32[]{:S(2)}, u32[]{:S(2)}) collective-permute-start(f32[64,1024]{1,0:T(8,128)S(1)} %copy-done.3), channel_id=1, source_target_pairs={{0,1},{1,0},{2,3},{3,2},{4,5},{5,4},{6,7},{7,6},{8,9},{9,8},{10,11... | collective-permute-start | bytes 786440 | tf_op jit(solution)/shard_map/ppermute | solution.py:510
  20.6 19.1 %collective-permute-start.5 = (f32[64,1024]{1,0:T(8,128)}, f32[64,1024]{1,0:T(8,128)S(1)}, u32[]{:S(2)}, u32[]{:S(2)}) collective-permute-start(f32[64,1024]{1,0:T(8,128)} %salt_in.5), channel_id=1, source_target_pairs={{0,1},{1,0},{2,3},{3,2},{4,5},{5,4},{6,7},{7,6},{8,9},{9,8},{10,11... | collective-permute-start | bytes 786440 | tf_op jit(solution)/shard_map/ppermute | solution.py:511
  20.7 19.0 %collective-permute-start.6 = (f32[64,1024]{1,0:T(8,128)S(1)}, f32[64,1024]{1,0:T(8,128)S(1)}, u32[]{:S(2)}, u32[]{:S(2)}) collective-permute-start(f32[64,1024]{1,0:T(8,128)S(1)} %copy-done.3), channel_id=1, source_target_pairs={{1,2},{2,1},{3,4},{4,3},{5,6},{6,5},{9,10},{10,9},{11,12},{12,11},... | collective-permute-start | bytes 786440 | tf_op jit(solution)/shard_map/ppermute | solution.py:512
  21.4 18.4 %collective-permute-start.7 = (f32[64,1024]{1,0:T(8,128)}, f32[64,1024]{1,0:T(8,128)S(1)}, u32[]{:S(2)}, u32[]{:S(2)}) collective-permute-start(f32[64,1024]{1,0:T(8,128)} %salt_in.5), channel_id=1, source_target_pairs={{1,2},{2,1},{3,4},{4,3},{5,6},{6,5},{9,10},{10,9},{11,12},{12,11},... | collective-permute-start | bytes 786440 | tf_op jit(solution)/shard_map/ppermute | solution.py:513
  22.3 5.4 %copy-start = (s32[512]{0:T(512)S(1)}, s32[512]{0:T(512)}, u32[]{:S(2)}) copy-start(s32[512]{0:T(512)} %param.13) | copy-start | bytes 6148
  26.8 0.9 %copy-start.1 = (f32[3,512,128]{2,1,0:T(8,128)}, f32[3,512,128]{2,1,0:T(8,128)S(1)}, u32[]{:S(2)}) copy-start(f32[3,512,128]{2,1,0:T(8,128)S(1)} %get-tuple-element.29.pivots) | copy-start | bytes 2359300
  30.3 19.8 %all-to-all-start.1 = ((f32[32,12,128]{2,1,0:T(8,128)}), f32[32,12,128]{2,1,0:T(8,128)S(1)}, u32[]{:S(2)}, u32[]{:S(2)}) async-start(f32[32,12,128]{2,1,0:T(8,128)} %surface_first.1), calls=%async_computation.1 | async-start | bytes 524288 | tf_op jit(solution)/shard_map/all_to_all | solution.py:556
  39.8 1.1 %copy-start.2 = (f32[3,512,128]{2,1,0:T(8,128)S(1)}, f32[3,512,128]{2,1,0:T(8,128)}, u32[]{:S(2)}) copy-start(f32[3,512,128]{2,1,0:T(8,128)} %copy-done.1) | copy-start | bytes 2359300

commit v3 on v2

--- a/solution.py
+++ b/solution.py
@@ -21,6 +21,20 @@
 PART_WEIGHT = 200
 
 
+def places(regions, doms):
+    r = lax.axis_index("region")
+    q = lax.axis_index("dom")
+
+    def at(dr, dq):
+        return lax.rem(r + dr + 2 * regions, regions) * doms + jnp.clip(q + dq, 0, doms - 1)
+
+    return [
+        at(0, 0), at(0, -2), at(0, -1), at(0, 1), at(0, 2),
+        at(-1, -1), at(-1, 0), at(-1, 1), at(1, -1), at(1, 0), at(1, 1), at(-2, 0),
+        q % 2 == 1, q >= 2, q >= 1, q < doms - 1, q < doms - 2, at(2, 0),
+    ]
+
+
 def lane_gather(source, lane):
     return jnp.take_along_axis(source, lane, axis=1, mode="promise_in_bounds")
 
@@ -43,10 +57,9 @@
     return started
 
 
-def prepare_kernel(
+def pick_kernel(
     theta_in, salt_in, depth8, ssh8, neighbors, weights, send4,
-    small, picked_small, picked, payload,
-    theta, salt, depths, heights, nbr, wts, sends, loaded
+    small, picked, picked_small, theta, salt, depths, heights, nbr, wts, sends, loaded
 ):
     levels, cells = theta.shape
     blocks = cells // LANES
@@ -89,18 +102,40 @@
         total = jnp.sum(jnp.where(wet, term, 0.0), axis=0, keepdims=True)
         small[ROW_FORCING : ROW_FORCING + 1, cols] = total / math.sqrt(levels)
     pick(small, picked_small, SMALL // 8, 0)
+
+
+def pack_kernel(theta, salt, ssh8, small, picked_small, message, payload, heights, loaded):
+    levels = theta.shape[0]
+    arrivals = copies(
+        [
+            (ssh8, heights),
+            (theta, message.at[pl.ds(0, levels), :]),
+            (salt, message.at[pl.ds(levels, levels), :]),
+        ],
+        loaded,
+    )
+    message[2 * levels :, :] = small[...]
+    arrivals[0].wait()
+    blocks = heights.shape[0]
+    row = slice(ROW_SURFACE, ROW_SURFACE + 1)
     tail = jnp.concatenate(
         [
-            picked_small[ROW_SURFACE : ROW_SURFACE + 1, t * LANES : (t + 1) * LANES]
-            for t in range(send_blocks)
+            picked_small[row, t * LANES : (t + 1) * LANES]
+            for t in range(picked_small.shape[1] // LANES)
         ],
         axis=0,
     )
-    head = heights[...]
+    send_all(payload, heights[...], tail)
+    for copy in arrivals[1:]:
+        copy.wait()
+
+
+def send_all(payload, head, tail):
+    blocks = head.shape[0]
 
     def send(i, carry):
         payload[i, 0:blocks, :] = head
-        payload[i, blocks : blocks + send_blocks, :] = tail
+        payload[i, blocks:, :] = tail
         return carry
 
     lax.fori_loop(0, payload.shape[0], send, 0)
@@ -135,21 +170,23 @@
 
 
 def surface_kernel(
-    place, heights, own_in, swap_in, swap_out, below, above, sends, token, out,
-    stat_own, stat_left, stat_right, stat_list, ext_own, ext_left, ext_right, ext_list, *, last
+    below, above, heights, own_in, swap_in, swap_out, sends, pivots, part, out,
+    stat_own, stat_left, stat_right, stat_list, ext_own, ext_left, ext_right, ext_list, *, last, shape
 ):
     blocks = own_in.shape[1] // LANES
+    rest = slice(swap_in.shape[0] - SMALL, swap_in.shape[0])
     half = below.shape[1] // LANES
+    place = places(*shape)
     odd = place[12]
     sub = lax.broadcasted_iota(jnp.int32, (8, LANES), 0)
     for b in range(blocks):
         cols = slice(b * LANES, (b + 1) * LANES)
         rows = pl.ds(b, SMALL, stride=8)
-        first = swap_in[:, cols]
-        second = swap_out[:, cols]
+        first = swap_in[rest, cols]
+        second = swap_out[rest, cols]
         stat_own[rows, :] = own_in[:, cols]
-        stat_left[rows, :] = jnp.where(odd == 1, first, second)
-        stat_right[rows, :] = jnp.where(odd == 1, second, first)
+        stat_left[rows, :] = jnp.where(odd, first, second)
+        stat_right[rows, :] = jnp.where(odd, second, first)
     for b in range(half):
         cols = slice(b * LANES, (b + 1) * LANES)
         stat_list[pl.ds(b, SMALL, stride=8), :] = below[:, cols]
@@ -159,7 +196,7 @@
         value = heights[place[n], 0:8, :]
         if side is None:
             return value
-        return jnp.where(place[13 + side] == 1, value, 0.0)
+        return jnp.where(place[13 + side], value, 0.0)
 
     def listed(n):
         return heights[place[n], 8:12, :]
@@ -205,9 +242,9 @@
     new_left = banded_step(ext_left, stat_left, left, sub)
     new_right = banded_step(ext_right, stat_right, right, sub)
     new_list = listed_step(ext_list, stat_list, own_list)
-    ext_own[0:8, :] = jnp.where(place[14] == 1, new_left, 0.0)
+    ext_own[0:8, :] = jnp.where(place[14], new_left, 0.0)
     ext_own[8:16, :] = new_own
-    ext_own[16:24, :] = jnp.where(place[15] == 1, new_right, 0.0)
+    ext_own[16:24, :] = jnp.where(place[15], new_right, 0.0)
     ext_own[24:32, :] = new_list
     final = banded_step(ext_own, stat_own, new_own, sub)
     if last:
@@ -219,12 +256,7 @@
         lambda b: jnp.broadcast_to(ext_left[b : b + 1, :], (8, LANES)), positions, blocks
     )
 
-    def send(i, carry):
-        out[i, 0:8, :] = final
-        out[i, 8:12, :] = tail[0:4, :]
-        return carry
-
-    lax.fori_loop(0, out.shape[0], send, 0)
+    send_all(out, final, tail[0:4, :])
 
 
 def stage(sources, depth, target, width, offset, level):
@@ -280,7 +312,7 @@
 
 
 def local_kernel(
-    theta_in, salt_in, small, kappa_in, depth_in, pivots, part, token,
+    theta_in, salt_in, small, kappa_in, depth_in, pivots, part,
     theta, salt, kappa, depth8, kap, rows_own, loaded
 ):
     cells = small.shape[1]
@@ -321,7 +353,6 @@
     for e in range(6):
         part[PART_INDEX + e : PART_INDEX + e + 1, :] = index[e].astype(jnp.float32)
         part[PART_WEIGHT + e : PART_WEIGHT + e + 1, :] = weight[e]
-    token[...] = depth
     level = lax.broadcasted_iota(jnp.int32, (levels, LANES), 0).astype(jnp.float32)
     for copy in arrivals[2:]:
         copy.wait()
@@ -344,25 +375,22 @@
 
 
 def tracer_kernel(
-    place, theta_in, salt_in, small, theta_inner, salt_inner, small_inner, theta_outer, salt_outer,
-    small_outer, below, small_below, above, small_above, pivots, part, theta_out, salt_out,
-    own, rows_ext, star, result, loaded, stored
+    theta_in, salt_in, small, small_below, small_above, below, above, swap_in, swap_out, pivots, part,
+    theta_out, salt_out, own, rows_ext, star, result, loaded, stored
 ):
     levels, cells = theta_out.shape
     listed = below.shape[1]
     arrivals = copies([(theta_in, own.at[0]), (salt_in, own.at[1])], loaded)
     level = lax.broadcasted_iota(jnp.int32, (levels, LANES), 0).astype(jnp.float32)
-    odd = place[12] == 1
+    odd = lax.axis_index("dom") % 2 == 1
     inner = pl.multiple_of(jnp.where(odd, 0, cells), LANES)
     outer = pl.multiple_of(jnp.where(odd, cells, 0), LANES)
-    stage((theta_inner, salt_inner), small_inner, rows_ext, cells, inner, level)
-    stage((theta_outer, salt_outer), small_outer, rows_ext, cells, outer, level)
-
-    def halves(picked):
-        return picked.at[pl.ds(0, levels), :], picked.at[pl.ds(levels, levels), :]
-
-    stage(halves(below), small_below, rows_ext, listed, 2 * cells, level)
-    stage(halves(above), small_above, rows_ext, listed, 2 * cells + listed, level)
+    starts = (inner, outer, 2 * cells, 2 * cells + listed)
+    depths = [source.at[pl.ds(2 * levels, SMALL), :] for source in (swap_in, swap_out)]
+    depths += [small_below, small_above]
+    for source, depth, start in zip((swap_in, swap_out, below, above), depths, starts):
+        tracers = [source.at[pl.ds(c * levels, levels), :] for c in range(2)]
+        stage(tracers, depth, rows_ext, source.shape[1], start, level)
     for copy in arrivals:
         copy.wait()
     line = tile_line()
@@ -428,7 +456,6 @@
 
 HBM = pl.BlockSpec(memory_space=pltpu.HBM)
 VMEM = pl.BlockSpec(memory_space=pltpu.VMEM)
-SMEM = pl.BlockSpec(memory_space=pltpu.SMEM)
 
 
 def grant(mebibytes):
@@ -447,19 +474,6 @@
     depth8 = depth.reshape(cells // LANES, LANES)
     ssh8 = ssh.reshape(cells // LANES, LANES)
     send4 = send_list.reshape(listed // LANES, LANES)
-    r = lax.axis_index("region")
-    q = lax.axis_index("dom")
-
-    def at(dr, dq):
-        return ((r + dr) % regions) * doms + jnp.clip(q + dq, 0, doms - 1)
-
-    place = jnp.stack(
-        [
-            at(0, 0), at(0, -2), at(0, -1), at(0, 1), at(0, 2),
-            at(-1, -1), at(-1, 0), at(-1, 1), at(1, -1), at(1, 0), at(1, 1), at(-2, 0),
-            q % 2, (q >= 2), (q >= 1), (q < doms - 1), (q < doms - 2), at(2, 0),
-        ]
-    ).astype(jnp.int32)
     def vmem(*shape, dtype=f32):
         return pltpu.VMEM(shape, dtype)
 
@@ -471,24 +485,34 @@
     def hbm(*arrays):
         return [pltpu.with_memory_space_constraint(array, pltpu.HBM) for array in arrays]
 
-    small, picked_small, picked, payload = pl.pallas_call(
-        prepare_kernel,
+    small, picked, picked_small = pl.pallas_call(
+        pick_kernel,
         out_shape=(
             jax.ShapeDtypeStruct((SMALL, cells), f32),
+            jax.ShapeDtypeStruct((2 * levels, listed), f32),
             jax.ShapeDtypeStruct((SMALL, listed), f32),
-            jax.ShapeDtypeStruct((2 * levels, listed), f32),
-            payload_shape,
         ),
         in_specs=[HBM] * 7,
-        out_specs=(VMEM,) * 4,
+        out_specs=(VMEM,) * 3,
         scratch_shapes=[
             vmem(levels, cells), vmem(levels, cells),
             vmem(8, LANES, dtype=jnp.int32), vmem(8, LANES), vmem(6, cells, dtype=jnp.int32),
             vmem(6, cells), vmem(listed // LANES, LANES, dtype=jnp.int32), semaphores(7),
         ],
         compiler_params=grant(8),
-        name="prepare",
+        cost_estimate=estimate(2000000, 2000000),
+        name="pick",
     )(*hbm(theta, salt, depth8, ssh8, neighbors, weights, send4))
+    message, payload = pl.pallas_call(
+        pack_kernel,
+        out_shape=(jax.ShapeDtypeStruct((2 * levels + SMALL, cells), f32), payload_shape),
+        in_specs=[HBM] * 3 + [VMEM] * 2,
+        out_specs=(VMEM,) * 2,
+        scratch_shapes=[vmem(8, LANES), semaphores(3)],
+        compiler_params=grant(8),
+        cost_estimate=estimate(1000000, 2000000),
+        name="pack",
+    )(*hbm(theta, salt, ssh8), small, picked_small)
 
     def device(i, j):
         return (i % regions) * doms + j
@@ -505,52 +529,45 @@
     above = lax.ppermute(picked, AXES, downward)
     small_below = lax.ppermute(picked_small, AXES, upward)
     small_above = lax.ppermute(picked_small, AXES, downward)
-    small_inner = lax.ppermute(small, AXES, inner)
-    small_outer = lax.ppermute(small, AXES, outer)
-    theta_inner = lax.ppermute(theta, AXES, inner)
-    salt_inner = lax.ppermute(salt, AXES, inner)
-    theta_outer = lax.ppermute(theta, AXES, outer)
-    salt_outer = lax.ppermute(salt, AXES, outer)
+    swap_in = lax.ppermute(message, AXES, inner)
+    swap_out = lax.ppermute(message, AXES, outer)
     heights = lax.all_to_all(payload, AXES, 0, 0)
-    pivots, part, token = pl.pallas_call(
+    pivots, part = pl.pallas_call(
         local_kernel,
         out_shape=(
             jax.ShapeDtypeStruct((3, 8 * levels, LANES), f32),
             jax.ShapeDtypeStruct((PART_WEIGHT + 8, cells), f32),
-            jax.ShapeDtypeStruct((8, LANES), jnp.int32),
         ),
         in_specs=[HBM, HBM, VMEM, HBM, HBM],
-        out_specs=(VMEM,) * 3,
+        out_specs=(VMEM,) * 2,
         scratch_shapes=[
             vmem(levels, cells), vmem(levels, cells),
             vmem(levels - 1, cells), vmem(8, LANES, dtype=jnp.int32), vmem(8 * levels, LANES),
             vmem(5 * levels, cells, dtype=jnp.bfloat16), semaphores(4),
         ],
         compiler_params=grant(8),
-        cost_estimate=estimate(2000000000, 4000000),
+        cost_estimate=estimate(40000000000, 4000000),
         name="local",
     )(*hbm(theta, salt), small, *hbm(kappa, depth8))
-    small_below, small_above, small_inner, small_outer, heights, token, place = (
-        lax.optimization_barrier(
-            (small_below, small_above, small_inner, small_outer, heights, token, place)
-        )
+    small_below, small_above, swap_in, swap_out, heights, pivots, part = lax.optimization_barrier(
+        (small_below, small_above, swap_in, swap_out, heights, pivots, part)
     )
 
     def subcycles(values, last):
         shape = jax.ShapeDtypeStruct((8, LANES), f32) if last else payload_shape
         return pl.pallas_call(
-            functools.partial(surface_kernel, last=last),
+            functools.partial(surface_kernel, last=last, shape=(regions, doms)),
             out_shape=shape,
-            in_specs=[SMEM] + [VMEM] * 8,
+            in_specs=[VMEM] * 9,
             out_specs=VMEM,
             scratch_shapes=[vmem(8 * SMALL, LANES)] * 4
             + [vmem(32, LANES)] * 3
             + [vmem(32, 8, LANES)],
             compiler_params=grant(8),
-            cost_estimate=estimate(2000000, 1000000),
+            cost_estimate=estimate(1000, 1000),
             name="surface_last" if last else "surface_first",
         )(
-            place, values, small, small_inner, small_outer, small_below, small_above, send4, token
+            small_below, small_above, values, small, swap_in, swap_out, send4, pivots, part
         )
 
     heights2 = lax.all_to_all(subcycles(heights, False), AXES, 0, 0)
@@ -558,7 +575,7 @@
     theta_next, salt_next = pl.pallas_call(
         tracer_kernel,
         out_shape=(jax.ShapeDtypeStruct((levels, cells), f32),) * 2,
-        in_specs=[SMEM] + [HBM] * 2 + [VMEM] * 13,
+        in_specs=[HBM] * 2 + [VMEM] * 9,
         out_specs=(HBM,) * 2,
         scratch_shapes=[
             vmem(2, levels, cells),
@@ -569,8 +586,8 @@
         compiler_params=grant(12),
         name="tracers",
     )(
-        place, *hbm(theta, salt), small, theta_inner, salt_inner, small_inner, theta_outer,
-        salt_outer, small_outer, below, small_below, above, small_above, pivots, part
+        *hbm(theta, salt), small, small_below, small_above, below, above, swap_in, swap_out,
+        pivots, part
     )
     return (theta_next, salt_next, surface.reshape(cells))
 

time: 52.7 us -> 44.9 us (0.85)
  starting transfers between devices: 25.8 us -> 17.7 us
  local copies, waits for them, and re-layouts: 2.11 us -> 0.01 us
  waiting for transfers between devices: 3.17 us -> 5.24 us
    all_to_all x1, starting transfers between devices: 9.45 us -> 2.73 us  [body(): heights2 = lax.all_to_all(subcycles(heights, False), AXES, 0, 0)]
    ppermute x6 -> x2, starting transfers between devices: 4.16 us -> 0.77 us  [the longest x1 0.7 us: body(): swap_out = lax.ppermute(message, AXES, outer)]
    all_to_all x1, waiting for transfers between devices: 0.01 us -> 2.85 us  [body(): heights = lax.all_to_all(payload, AXES, 0, 0)]
    ppermute x1, waiting for transfers between devices: 0.01 us -> 2.38 us  [body(): above = lax.ppermute(picked, AXES, downward)]
    all_to_all x1, starting transfers between devices: 4.92 us -> 7.16 us  [body(): heights = lax.all_to_all(payload, AXES, 0, 0)]
    ppermute x1, waiting for transfers between devices: 2.23 us -> 0.01 us  [body(): small_below = lax.ppermute(picked_small, AXES, upward)]
    unnamed x8 -> x2, local copies, waits for them, and re-layouts: 2.01 us -> 0.01 us
    ppermute x1, starting transfers between devices: 1.72 us -> 2.99 us  [body(): small_below = lax.ppermute(picked_small, AXES, upward)]
  transfers between devices with their start and end apart: 12 -> 8, of which waited for: 2 -> 2; matrix products, arithmetic and copies ran while one was open for 0% -> 0% of each run, Pallas kernels for 29% -> 39%
where the time goes in v3:
time: 44.9 us; the launch traced here: 44.5 us
  Pallas kernels  20.8 us (46%)
  starting transfers between devices  17.7 us (39%)
  waiting for transfers between devices  5.24 us (12%)
  between operations  0.73 us (2%)
    pallas_call x1, Pallas kernels, body(): pl.pallas_call(tracer_kernel, out_shape=(jax.ShapeDtypeStruct((levels, ce...  8.77 us
    all_to_all x1, starting transfers between devices, body(): heights = lax.all_to_all(payload, AXES, 0, 0)  7.16 us
    pallas_call x1, Pallas kernels, body(): pl.pallas_call(local_kernel, out_shape=(jax.ShapeDtypeStruct((3, 8 * leve...  4.53 us
    pallas_call x2, Pallas kernels, subcycles(): pl.pallas_call(functools.partial(surface_kernel, last=last, shape=(region...  3.69 us
    ppermute x1, starting transfers between devices, body(): small_below = lax.ppermute(picked_small, AXES, upward)  2.99 us
    all_to_all x1, waiting for transfers between devices, body(): heights = lax.all_to_all(payload, AXES, 0, 0)  2.85 us
    all_to_all x1, starting transfers between devices, body(): heights2 = lax.all_to_all(subcycles(heights, False), AXES, 0, 0)  2.73 us
    ppermute x1, waiting for transfers between devices, body(): above = lax.ppermute(picked, AXES, downward)  2.38 us
  transfers between devices with their start and end apart: 8, of which 2 were waited for; matrix products, arithmetic and copies ran while one was open for 0% of the time, Pallas kernels for 39%

profile of v3, /device:TPU:0, one launch (start us, length us, event | category | flops | bytes accessed | tf_op | source)
XLA Modules:
  0.0 44.5 jit_solution(6407144070243125531)
XLA Ops:
  0.6 1.9 %pick.1 = (f32[16,1024]{1,0:T(8,128)S(1)}, f32[128,512]{1,0:T(8,128)S(1)}, f32[16,512]{1,0:T(8,128)S(1)}) custom-call(f32[64,1024]{1,0:T(8,128)} %theta_in.5, f32[64,1024]{1,0:T(8,128)} %salt_in.5, s32[8,128]{1,0:T(8,128)} %bitcast.9, f32[8,128]{1,0:T(8,128)} %bitcast.7, s32[6,1024]{1,0:T(8,128)} %neighbors.1, f32[6,1024]{1,0:T(8,128)} %weights.1, ...), custom_call_target="tpu_custom_call" | custom-call | flops 2000000 | bytes 2000000 | tf_op jit(solution)/shard_map/pick/pallas_call | solution.py:488
  2.5 3.0 %collective-permute-start = (f32[16,512]{1,0:T(8,128)S(1)}, f32[16,512]{1,0:T(8,128)S(1)}, u32[]{:S(2)}, u32[]{:S(2)}) collective-permute-start(f32[16,512]{1,0:T(8,128)S(1)} %get-tuple-element.20.picked_small), channel_id=1, source_target_pairs={{0,8},{1,9},{2,10},{3,11},{4,12},{5,13},{6,14},{7,15},{8,16},{9,17... | collective-permute-start | bytes 98312 | tf_op jit(solution)/shard_map/ppermute | solution.py:530
  5.5 2.0 %pack.1 = (f32[144,1024]{1,0:T(8,128)}, f32[32,12,128]{2,1,0:T(8,128)}) custom-call(f32[64,1024]{1,0:T(8,128)} %theta_in.5, f32[64,1024]{1,0:T(8,128)} %salt_in.5, f32[8,128]{1,0:T(8,128)} %bitcast.8, f32[16,1024]{1,0:T(8,128)S(1)} %get-tuple-element.19.small.own_in, f32[16,512]{1,0:T(8,128)S(1)} %get-tuple-element.20.picked_small), custom_call_target="tpu_custom_call" | custom-call | flops 1000000 | bytes 2000000 | tf_op jit(solution)/shard_map/pack/pallas_call | solution.py:506
  7.5 0.1 collective-permute-start.2
  7.6 0.7 %collective-permute-start.3 = (f32[144,1024]{1,0:T(8,128)}, f32[144,1024]{1,0:T(8,128)S(1)}, u32[]{:S(2)}, u32[]{:S(2)}) collective-permute-start(f32[144,1024]{1,0:T(8,128)} %get-tuple-element.21), channel_id=1, source_target_pairs={{1,2},{2,1},{3,4},{4,3},{5,6},{6,5},{9,10},{10,9},{11,12},{12,11},... | collective-permute-start | bytes 1769480 | tf_op jit(solution)/shard_map/ppermute | solution.py:533
  8.3 1.0 %collective-permute-start.1 = (f32[16,512]{1,0:T(8,128)S(1)}, f32[16,512]{1,0:T(8,128)S(1)}, u32[]{:S(2)}, u32[]{:S(2)}) collective-permute-start(f32[16,512]{1,0:T(8,128)S(1)} %get-tuple-element.20.picked_small), channel_id=1, source_target_pairs={{8,0},{9,1},{10,2},{11,3},{12,4},{13,5},{14,6},{15,7},{16,8},{17,9... | collective-permute-start | bytes 98312 | tf_op jit(solution)/shard_map/ppermute | solution.py:531
  9.3 7.2 %all-to-all-start = ((f32[32,12,128]{2,1,0:T(8,128)}), f32[32,12,128]{2,1,0:T(8,128)S(1)}, u32[]{:S(2)}, u32[]{:S(2)}) async-start(f32[32,12,128]{2,1,0:T(8,128)} %get-tuple-element.22), calls=%async_computation | async-start | bytes 524288 | tf_op jit(solution)/shard_map/all_to_all | solution.py:534
  16.5 1.8 %collective-permute-start.4 = (f32[128,512]{1,0:T(8,128)S(1)}, f32[128,512]{1,0:T(8,128)}, u32[]{:S(2)}, u32[]{:S(2)}) collective-permute-start(f32[128,512]{1,0:T(8,128)S(1)} %get-tuple-element.27), channel_id=1, source_target_pairs={{0,8},{1,9},{2,10},{3,11},{4,12},{5,13},{6,14},{7,15},{8,16},{9,17... | collective-permute-start | bytes 786440 | tf_op jit(solution)/shard_map/ppermute | solution.py:528
  18.3 0.0 collective-permute-done.small_below.below
  18.3 1.2 %collective-permute-start.5 = (f32[128,512]{1,0:T(8,128)S(1)}, f32[128,512]{1,0:T(8,128)}, u32[]{:S(2)}, u32[]{:S(2)}) collective-permute-start(f32[128,512]{1,0:T(8,128)S(1)} %get-tuple-element.27), channel_id=1, source_target_pairs={{8,0},{9,1},{10,2},{11,3},{12,4},{13,5},{14,6},{15,7},{16,8},{17,9... | collective-permute-start | bytes 786440 | tf_op jit(solution)/shard_map/ppermute | solution.py:529
  19.5 4.5 %local.1 = (f32[3,512,128]{2,1,0:T(8,128)S(1)}, f32[208,1024]{1,0:T(8,128)S(1)}) custom-call(f32[64,1024]{1,0:T(8,128)} %theta_in.5, f32[64,1024]{1,0:T(8,128)} %salt_in.5, f32[16,1024]{1,0:T(8,128)S(1)} %get-tuple-element.19.small.own_in, f32[63,1024]{1,0:T(8,128)} %kappa_in.1, s32[8,128]{1,0:T(8,128)} %bitcast.10), custom_call_target="tpu_custom_call" | custom-call | flops 40000000000 | bytes 4000000 | tf_op jit(solution)/shard_map/local/pallas_call | solution.py:535
  24.0 0.0 copy-start
  24.0 0.0 collective-permute-done.1.small_above.above
  24.0 2.8 %all-to-all-done.heights = f32[32,12,128]{2,1,0:T(8,128)S(1)} async-done(((f32[32,12,128]{2,1,0:T(8,128)}), f32[32,12,128]{2,1,0:T(8,128)S(1)}, u32[]{:S(2)}, u32[]{:S(2)}) %all-to-all-start) | async-done | bytes 196640 | tf_op jit(solution)/shard_map/all_to_all | solution.py:534
  26.9 0.0 collective-permute-done.2.swap_in
  26.9 0.0 collective-permute-done.3.swap_out
  26.9 0.0 copy-done
  26.9 2.0 %surface_first.1 = f32[32,12,128]{2,1,0:T(8,128)} custom-call(f32[16,512]{1,0:T(8,128)S(1)} %collective-permute-done.small_below.below, f32[16,512]{1,0:T(8,128)S(1)} %collective-permute-done.1.small_above.above, f32[32,12,128]{2,1,0:T(8,128)S(1)} %all-to-all-done.heights, f32[16,1024]{1,0:T(8,128)S(1)} %get-tuple-element.19.small.own_in, ...), custom_call_target="tpu_custom_call" | custom-call | flops 1000 | bytes 1000 | tf_op jit(solution)/shard_map/surface_first/pallas_call | solution.py:558
  28.9 2.7 %all-to-all-start.1 = ((f32[32,12,128]{2,1,0:T(8,128)}), f32[32,12,128]{2,1,0:T(8,128)S(1)}, u32[]{:S(2)}, u32[]{:S(2)}) async-start(f32[32,12,128]{2,1,0:T(8,128)} %surface_first.1), calls=%async_computation.1 | async-start | bytes 524288 | tf_op jit(solution)/shard_map/all_to_all | solution.py:573
  31.6 0.0 collective-permute-done.4.below
  31.6 2.4 %collective-permute-done.5.above = f32[128,512]{1,0:T(8,128)} collective-permute-done((f32[128,512]{1,0:T(8,128)S(1)}, f32[128,512]{1,0:T(8,128)}, u32[]{:S(2)}, u32[]{:S(2)}) %collective-permute-start.5) | collective-permute-done | bytes 262176 | tf_op jit(solution)/shard_map/ppermute | solution.py:529
  34.0 8.8 %tracers.1 = (f32[64,1024]{1,0:T(8,128)}, f32[64,1024]{1,0:T(8,128)}) custom-call(f32[64,1024]{1,0:T(8,128)} %theta_in.5, f32[64,1024]{1,0:T(8,128)} %salt_in.5, f32[16,1024]{1,0:T(8,128)S(1)} %get-tuple-element.19.small.own_in, f32[16,512]{1,0:T(8,128)S(1)} %collective-permute-done.small_below.below, ...), custom_call_target="tpu_custom_call" | custom-call | flops 4000000000 | bytes 8000000 | tf_op jit(solution)/shard_map/tracers/pallas_call | solution.py:575
  42.8 0.0 all-to-all-done.1.heights
  42.8 1.7 %surface_last.1 = f32[8,128]{1,0:T(8,128)} custom-call(f32[16,512]{1,0:T(8,128)S(1)} %collective-permute-done.small_below.below, f32[16,512]{1,0:T(8,128)S(1)} %collective-permute-done.1.small_above.above, f32[32,12,128]{2,1,0:T(8,128)S(1)} %all-to-all-done.1.heights, f32[16,1024]{1,0:T(8,128)S(1)} %get-tuple-element.19.small.own_in, ...), custom_call_target="tpu_custom_call" | custom-call | flops 1000 | bytes 1000 | tf_op jit(solution)/shard_map/surface_last/pallas_call | solution.py:558
Async XLA Ops:
  2.5 15.8 %collective-permute-start = (f32[16,512]{1,0:T(8,128)S(1)}, f32[16,512]{1,0:T(8,128)S(1)}, u32[]{:S(2)}, u32[]{:S(2)}) collective-permute-start(f32[16,512]{1,0:T(8,128)S(1)} %get-tuple-element.20.picked_small), channel_id=1, source_target_pairs={{0,8},{1,9},{2,10},{3,11},{4,12},{5,13},{6,14},{7,15},{8,16},{9,17... | collective-permute-start | bytes 98312 | tf_op jit(solution)/shard_map/ppermute | solution.py:530
  7.5 19.4 %collective-permute-start.2 = (f32[144,1024]{1,0:T(8,128)}, f32[144,1024]{1,0:T(8,128)S(1)}, u32[]{:S(2)}, u32[]{:S(2)}) collective-permute-start(f32[144,1024]{1,0:T(8,128)} %get-tuple-element.21), channel_id=1, source_target_pairs={{0,1},{1,0},{2,3},{3,2},{4,5},{5,4},{6,7},{7,6},{8,9},{9,8},{10,11... | collective-permute-start | bytes 1769480 | tf_op jit(solution)/shard_map/ppermute | solution.py:532
  7.6 19.3 %collective-permute-start.3 = (f32[144,1024]{1,0:T(8,128)}, f32[144,1024]{1,0:T(8,128)S(1)}, u32[]{:S(2)}, u32[]{:S(2)}) collective-permute-start(f32[144,1024]{1,0:T(8,128)} %get-tuple-element.21), channel_id=1, source_target_pairs={{1,2},{2,1},{3,4},{4,3},{5,6},{6,5},{9,10},{10,9},{11,12},{12,11},... | collective-permute-start | bytes 1769480 | tf_op jit(solution)/shard_map/ppermute | solution.py:533
  8.3 15.7 %collective-permute-start.1 = (f32[16,512]{1,0:T(8,128)S(1)}, f32[16,512]{1,0:T(8,128)S(1)}, u32[]{:S(2)}, u32[]{:S(2)}) collective-permute-start(f32[16,512]{1,0:T(8,128)S(1)} %get-tuple-element.20.picked_small), channel_id=1, source_target_pairs={{8,0},{9,1},{10,2},{11,3},{12,4},{13,5},{14,6},{15,7},{16,8},{17,9... | collective-permute-start | bytes 98312 | tf_op jit(solution)/shard_map/ppermute | solution.py:531
  9.3 17.6 %all-to-all-start = ((f32[32,12,128]{2,1,0:T(8,128)}), f32[32,12,128]{2,1,0:T(8,128)S(1)}, u32[]{:S(2)}, u32[]{:S(2)}) async-start(f32[32,12,128]{2,1,0:T(8,128)} %get-tuple-element.22), calls=%async_computation | async-start | bytes 524288 | tf_op jit(solution)/shard_map/all_to_all | solution.py:534
  16.5 15.2 %collective-permute-start.4 = (f32[128,512]{1,0:T(8,128)S(1)}, f32[128,512]{1,0:T(8,128)}, u32[]{:S(2)}, u32[]{:S(2)}) collective-permute-start(f32[128,512]{1,0:T(8,128)S(1)} %get-tuple-element.27), channel_id=1, source_target_pairs={{0,8},{1,9},{2,10},{3,11},{4,12},{5,13},{6,14},{7,15},{8,16},{9,17... | collective-permute-start | bytes 786440 | tf_op jit(solution)/shard_map/ppermute | solution.py:528
  18.3 15.7 %collective-permute-start.5 = (f32[128,512]{1,0:T(8,128)S(1)}, f32[128,512]{1,0:T(8,128)}, u32[]{:S(2)}, u32[]{:S(2)}) collective-permute-start(f32[128,512]{1,0:T(8,128)S(1)} %get-tuple-element.27), channel_id=1, source_target_pairs={{8,0},{9,1},{10,2},{11,3},{12,4},{13,5},{14,6},{15,7},{16,8},{17,9... | collective-permute-start | bytes 786440 | tf_op jit(solution)/shard_map/ppermute | solution.py:529
  24.0 2.9 %copy-start = (s32[512]{0:T(512)S(1)}, s32[512]{0:T(512)}, u32[]{:S(2)}) copy-start(s32[512]{0:T(512)} %param.13) | copy-start | bytes 6148
  28.9 13.9 %all-to-all-start.1 = ((f32[32,12,128]{2,1,0:T(8,128)}), f32[32,12,128]{2,1,0:T(8,128)S(1)}, u32[]{:S(2)}, u32[]{:S(2)}) async-start(f32[32,12,128]{2,1,0:T(8,128)} %surface_first.1), calls=%async_computation.1 | async-start | bytes 524288 | tf_op jit(solution)/shard_map/all_to_all | solution.py:573

commit v4 on v3

--- a/solution.py
+++ b/solution.py
@@ -17,8 +17,8 @@
 ROW_FORCING = 13
 ROW_SURFACE = 14
 SMALL = 16
-PART_INDEX = 192
-PART_WEIGHT = 200
+PART_INDEX = 0
+PART_WEIGHT = 8
 
 
 def places(regions, doms):
@@ -59,7 +59,8 @@
 
 def pick_kernel(
     theta_in, salt_in, depth8, ssh8, neighbors, weights, send4,
-    small, picked, picked_small, theta, salt, depths, heights, nbr, wts, sends, loaded
+    small, picked, picked_small, message,
+    theta, salt, depths, heights, nbr, wts, sends, loaded, stored
 ):
     levels, cells = theta.shape
     blocks = cells // LANES
@@ -91,9 +92,12 @@
                     lambda b: source[rows, b * LANES : (b + 1) * LANES], positions, blocks
                 )
 
-    arrivals[5].wait()
+    departures = []
+    for c, tracer in enumerate((theta, salt)):
+        arrivals[5 + c].wait()
+        target = message.at[pl.ds(c * levels, levels), :]
+        departures += copies([(tracer, target)], stored.at[pl.ds(c, 1)])
     pick(theta, picked, levels // 8, 0)
-    arrivals[6].wait()
     pick(salt, picked, levels // 8, levels)
     for b in range(blocks):
         cols = slice(b * LANES, (b + 1) * LANES)
@@ -101,41 +105,35 @@
         wet = level < depths[b : b + 1, :]
         total = jnp.sum(jnp.where(wet, term, 0.0), axis=0, keepdims=True)
         small[ROW_FORCING : ROW_FORCING + 1, cols] = total / math.sqrt(levels)
+    rest = message.at[pl.ds(2 * levels, SMALL), :]
+    departures += copies([(small, rest)], stored.at[pl.ds(2, 1)])
     pick(small, picked_small, SMALL // 8, 0)
-
-
-def pack_kernel(theta, salt, ssh8, small, picked_small, message, payload, heights, loaded):
-    levels = theta.shape[0]
-    arrivals = copies(
-        [
-            (ssh8, heights),
-            (theta, message.at[pl.ds(0, levels), :]),
-            (salt, message.at[pl.ds(levels, levels), :]),
-        ],
-        loaded,
+    for copy in departures:
+        copy.wait()
+
+
+def heights_kernel(ssh8, send4, payload_out, sends, heights, payload, loaded):
+    for copy in copies([(ssh8, heights), (send4, sends)], loaded):
+        copy.wait()
+    broadcast_heights(heights[...], heights, sends, payload)
+    for copy in copies([(payload, payload_out)], loaded.at[pl.ds(2, 1)]):
+        copy.wait()
+
+
+def broadcast_heights(own, rows, sends, payload):
+    positions = jnp.concatenate([sends[...], sends[...]], axis=0)
+    blocks = own.shape[0]
+    tail = pick_block(
+        lambda b: jnp.broadcast_to(rows[b : b + 1, :], (8, LANES)), positions, blocks
     )
-    message[2 * levels :, :] = small[...]
-    arrivals[0].wait()
-    blocks = heights.shape[0]
-    row = slice(ROW_SURFACE, ROW_SURFACE + 1)
-    tail = jnp.concatenate(
-        [
-            picked_small[row, t * LANES : (t + 1) * LANES]
-            for t in range(picked_small.shape[1] // LANES)
-        ],
-        axis=0,
-    )
-    send_all(payload, heights[...], tail)
-    for copy in arrivals[1:]:
-        copy.wait()
+    send_all(payload, own, tail[0 : sends.shape[0], :])
 
 
 def send_all(payload, head, tail):
-    blocks = head.shape[0]
-
     def send(i, carry):
-        payload[i, 0:blocks, :] = head
-        payload[i, blocks:, :] = tail
+        payload[i, 0] = head[0:4, :]
+        payload[i, 1] = head[4:8, :]
+        payload[i, 2] = tail
         return carry
 
     lax.fori_loop(0, payload.shape[0], send, 0)
@@ -170,8 +168,9 @@
 
 
 def surface_kernel(
-    below, above, heights, own_in, swap_in, swap_out, sends, pivots, part, out,
-    stat_own, stat_left, stat_right, stat_list, ext_own, ext_left, ext_right, ext_list, *, last, shape
+    below, above, heights, own_in, swap_in, swap_out, sends, pivots, part, out_ref,
+    stat_own, stat_left, stat_right, stat_list, ext_own, ext_left, ext_right, ext_list, out, stored,
+    *, last, shape
 ):
     blocks = own_in.shape[1] // LANES
     rest = slice(swap_in.shape[0] - SMALL, swap_in.shape[0])
@@ -193,13 +192,13 @@
         stat_list[pl.ds(half + b, SMALL, stride=8), :] = above[:, cols]
 
     def full(n, side):
-        value = heights[place[n], 0:8, :]
+        value = jnp.concatenate([heights[place[n], 0], heights[place[n], 1]], axis=0)
         if side is None:
             return value
         return jnp.where(place[13 + side], value, 0.0)
 
     def listed(n):
-        return heights[place[n], 8:12, :]
+        return heights[place[n], 2]
 
     own = full(0, None)
     left2, left, right, right2 = full(1, 0), full(2, 1), full(3, 2), full(4, 3)
@@ -248,15 +247,12 @@
     ext_own[24:32, :] = new_list
     final = banded_step(ext_own, stat_own, new_own, sub)
     if last:
-        out[...] = final
+        out_ref[...] = final
         return
     ext_left[0:8, :] = final
-    positions = jnp.concatenate([sends[...], sends[...]], axis=0)
-    tail = pick_block(
-        lambda b: jnp.broadcast_to(ext_left[b : b + 1, :], (8, LANES)), positions, blocks
-    )
-
-    send_all(out, final, tail[0:4, :])
+    broadcast_heights(final, ext_left, sends, out)
+    for copy in copies([(out, out_ref)], stored):
+        copy.wait()
 
 
 def stage(sources, depth, target, width, offset, level):
@@ -274,17 +270,20 @@
         target[4 * levels : 5 * levels, where] = wet.astype(jnp.bfloat16)
 
 
-def weight_tile(line, index, highs, lows, base):
-    high = jnp.zeros((TILE, TILE), jnp.bfloat16)
-    low = jnp.zeros((TILE, TILE), jnp.bfloat16)
+def weight_tile(line, index, highs, lows, base, high, low, where):
+    locals_ = []
     for e in range(6):
         local = index[e] - base
         local = jnp.where(jnp.logical_and(local >= 0, local < TILE), local, -1)
-        local = local.astype(jnp.float32).astype(jnp.bfloat16)
-        hit = line == local
-        high = jnp.where(hit, highs[e], high)
-        low = jnp.where(hit, lows[e], low)
-    return high, low
+        locals_.append(local.astype(jnp.float32).astype(jnp.bfloat16))
+    first = jnp.zeros((TILE, TILE), jnp.bfloat16)
+    second = first
+    for e in range(6):
+        hit = line == locals_[e]
+        first = jnp.where(hit, highs[e], first)
+        second = jnp.where(hit, lows[e], second)
+    high[where, :] = first
+    low[where, :] = second
 
 
 def tile_line():
@@ -299,28 +298,12 @@
     return highs, lows
 
 
-def product(rows, columns, high, low, levels):
-    first = jnp.dot(rows[:, columns], high, preferred_element_type=jnp.float32)
-    second = jnp.dot(rows[2 * levels :, columns], low, preferred_element_type=jnp.float32)
-    return jnp.concatenate(
-        [
-            first[0 : 2 * levels] + first[2 * levels : 4 * levels] + second[0 : 2 * levels],
-            first[4 * levels :] + second[2 * levels :],
-        ],
-        axis=0,
-    )
-
-
 def local_kernel(
-    theta_in, salt_in, small, kappa_in, depth_in, pivots, part,
-    theta, salt, kappa, depth8, kap, rows_own, loaded
+    small, kappa_in, depth_in, pivots, part, kappa, depth8, kap, loaded
 ):
     cells = small.shape[1]
     levels = pivots.shape[1] // 8
-    arrivals = copies(
-        [(depth_in, depth8), (kappa_in, kappa), (theta_in, theta), (salt_in, salt)], loaded
-    )
-    for copy in arrivals[:2]:
+    for copy in copies([(depth_in, depth8), (kappa_in, kappa)], loaded):
         copy.wait()
     for b in range(cells // LANES):
         cols = slice(b * LANES, (b + 1) * LANES)
@@ -353,39 +336,65 @@
     for e in range(6):
         part[PART_INDEX + e : PART_INDEX + e + 1, :] = index[e].astype(jnp.float32)
         part[PART_WEIGHT + e : PART_WEIGHT + e + 1, :] = weight[e]
-    level = lax.broadcasted_iota(jnp.int32, (levels, LANES), 0).astype(jnp.float32)
-    for copy in arrivals[2:]:
-        copy.wait()
-    stage((theta, salt), small, rows_own, cells, 0, level)
-    line = tile_line()
-
-    def block(t, carry):
-        here = pl.ds(pl.multiple_of(t * TILE, TILE), TILE)
-        idx = [part[PART_INDEX + e : PART_INDEX + e + 1, here].astype(jnp.int32) for e in range(6)]
-        highs, lows = split_weights(part.at[pl.ds(PART_WEIGHT, 8), :], here)
-        total = jnp.zeros((3 * levels, TILE), jnp.float32)
-        for j in range(cells // TILE):
-            high, low = weight_tile(line, idx, highs, lows, cells + j * TILE)
-            columns = slice(j * TILE, (j + 1) * TILE)
-            total = total + product(rows_own, columns, high, low, levels)
-        part[0 : 3 * levels, here] = total
-        return carry
-
-    lax.fori_loop(0, cells // TILE, block, 0)
 
 
 def tracer_kernel(
-    theta_in, salt_in, small, small_below, small_above, below, above, swap_in, swap_out, pivots, part,
-    theta_out, salt_out, own, rows_ext, star, result, loaded, stored
+    theta_in, salt_in, small, small_below, small_above, below, above, swap_in, swap_out, pivots,
+    part, theta_out, salt_out, own, rows_ext, high, low, star, result, loaded, stored
 ):
     levels, cells = theta_out.shape
     listed = below.shape[1]
     arrivals = copies([(theta_in, own.at[0]), (salt_in, own.at[1])], loaded)
     level = lax.broadcasted_iota(jnp.int32, (levels, LANES), 0).astype(jnp.float32)
     odd = lax.axis_index("dom") % 2 == 1
-    inner = pl.multiple_of(jnp.where(odd, 0, cells), LANES)
-    outer = pl.multiple_of(jnp.where(odd, cells, 0), LANES)
-    starts = (inner, outer, 2 * cells, 2 * cells + listed)
+    inner = pl.multiple_of(jnp.where(odd, 0, 2 * cells), LANES)
+    outer = pl.multiple_of(jnp.where(odd, 2 * cells, 0), LANES)
+    line = tile_line()
+    band = (TILE + 2 * cells) // TILE
+    region = 2 * listed // TILE
+
+    def build(t, first, last):
+        here = slice(t * TILE, (t + 1) * TILE)
+        idx = [part[PART_INDEX + e : PART_INDEX + e + 1, here].astype(jnp.int32) for e in range(6)]
+        highs, lows = split_weights(part.at[pl.ds(PART_WEIGHT, 8), :], here)
+        for j in range(first, last):
+            base = (t + j) * TILE if j < band else 3 * cells + (j - band) * TILE
+            where = slice(j * TILE, (j + 1) * TILE)
+            weight_tile(line, idx, highs, lows, base, high.at[t % 2], low.at[t % 2], where)
+
+    middle = band // 2
+    spans = ((0, middle), (middle, band), (band, band + region))
+
+    def product(t):
+        total = None
+        for first, last in spans:
+            if t + 1 < cells // TILE:
+                build(t + 1, first, last)
+            start = (t + first) * TILE if first < band else 3 * cells
+            columns = slice(start, start + (last - first) * TILE)
+            where = slice(first * TILE, last * TILE)
+            upper = jnp.dot(
+                rows_ext[:, columns], high[t % 2, where, :], preferred_element_type=jnp.float32
+            )
+            lower = jnp.dot(
+                rows_ext[2 * levels :, columns], low[t % 2, where, :],
+                preferred_element_type=jnp.float32,
+            )
+            values = upper[0 : 2 * levels] + upper[2 * levels : 4 * levels] + lower[0 : 2 * levels]
+            wets = upper[4 * levels :] + lower[2 * levels :]
+            total = (values, wets) if total is None else (total[0] + values, total[1] + wets)
+        for b in range(TILE // LANES):
+            cols = slice(b * LANES, (b + 1) * LANES)
+            here = slice(t * TILE + b * LANES, t * TILE + (b + 1) * LANES)
+            wet = level < small[ROW_DEPTH : ROW_DEPTH + 1, here]
+            for c in range(2):
+                value = own[c, :, here]
+                change = total[0][c * levels : (c + 1) * levels, cols] - value * total[1][:, cols]
+                stepped = value + jnp.where(wet, change, 0.0)
+                star[c, pl.ds(t * (TILE // LANES) + b, levels, stride=8), :] = stepped
+
+    build(0, 0, band + region)
+    starts = (inner, outer, 3 * cells, 3 * cells + listed)
     depths = [source.at[pl.ds(2 * levels, SMALL), :] for source in (swap_in, swap_out)]
     depths += [small_below, small_above]
     for source, depth, start in zip((swap_in, swap_out, below, above), depths, starts):
@@ -393,37 +402,9 @@
         stage(tracers, depth, rows_ext, source.shape[1], start, level)
     for copy in arrivals:
         copy.wait()
-    line = tile_line()
-    band = (TILE + cells) // TILE
-    region = 2 * listed // TILE
-
-    def block(t, carry):
-        start = pl.multiple_of(t * TILE, TILE)
-        here = pl.ds(start, TILE)
-        idx = []
-        for e in range(6):
-            value = part[PART_INDEX + e : PART_INDEX + e + 1, here].astype(jnp.int32)
-            outside = jnp.where(value >= 2 * cells, value - cells, -1)
-            idx.append(jnp.where(value < cells, value, outside))
-        highs, lows = split_weights(part.at[pl.ds(PART_WEIGHT, 8), :], here)
-        total = part[0 : 3 * levels, here]
-        for j in range(band + region):
-            base = start + j * TILE if j < band else 2 * cells + (j - band) * TILE
-            base = pl.multiple_of(base, TILE)
-            high, low = weight_tile(line, idx, highs, lows, base)
-            total = total + product(rows_ext, pl.ds(base, TILE), high, low, levels)
-        for b in range(TILE // LANES):
-            cols = slice(b * LANES, (b + 1) * LANES)
-            sub = pl.ds(start + b * LANES, LANES)
-            wet = level < small[ROW_DEPTH : ROW_DEPTH + 1, sub]
-            for c in range(2):
-                value = own[c, :, sub]
-                change = total[c * levels : (c + 1) * levels, cols] - value * total[2 * levels :, cols]
-                stepped = value + jnp.where(wet, change, 0.0)
-                star[c, pl.ds(t * (TILE // LANES) + b, levels, stride=8), :] = stepped
-        return carry
-
-    lax.fori_loop(0, cells // TILE, block, 0)
+    stage((own.at[0], own.at[1]), small, rows_ext, cells, cells, level)
+    for t in range(cells // TILE):
+        product(t)
     for c in range(2):
         star[c] = star[c] * pivots[2]
     before = [star[0, 0:8, :], star[1, 0:8, :]]
@@ -480,40 +461,40 @@
     def semaphores(count):
         return pltpu.SemaphoreType.DMA((count,))
 
-    payload_shape = jax.ShapeDtypeStruct((devices, 12, LANES), f32)
+    payload_shape = jax.ShapeDtypeStruct((devices, 3, 4, LANES), f32)
 
     def hbm(*arrays):
         return [pltpu.with_memory_space_constraint(array, pltpu.HBM) for array in arrays]
 
-    small, picked, picked_small = pl.pallas_call(
+    payload, sends = pl.pallas_call(
+        heights_kernel,
+        out_shape=(payload_shape, jax.ShapeDtypeStruct((listed // LANES, LANES), jnp.int32)),
+        in_specs=[HBM] * 2,
+        out_specs=(HBM, VMEM),
+        scratch_shapes=[vmem(8, LANES), vmem(*payload_shape.shape), semaphores(3)],
+        compiler_params=grant(8),
+        cost_estimate=estimate(1000, 1000),
+        name="heights",
+    )(*hbm(ssh8, send4))
+    small, picked, picked_small, message = pl.pallas_call(
         pick_kernel,
         out_shape=(
             jax.ShapeDtypeStruct((SMALL, cells), f32),
             jax.ShapeDtypeStruct((2 * levels, listed), f32),
             jax.ShapeDtypeStruct((SMALL, listed), f32),
+            jax.ShapeDtypeStruct((2 * levels + SMALL, cells), f32),
         ),
         in_specs=[HBM] * 7,
-        out_specs=(VMEM,) * 3,
+        out_specs=(VMEM,) * 3 + (HBM,),
         scratch_shapes=[
             vmem(levels, cells), vmem(levels, cells),
             vmem(8, LANES, dtype=jnp.int32), vmem(8, LANES), vmem(6, cells, dtype=jnp.int32),
-            vmem(6, cells), vmem(listed // LANES, LANES, dtype=jnp.int32), semaphores(7),
+            vmem(6, cells), vmem(listed // LANES, LANES, dtype=jnp.int32), semaphores(7), semaphores(3),
         ],
         compiler_params=grant(8),
         cost_estimate=estimate(2000000, 2000000),
         name="pick",
     )(*hbm(theta, salt, depth8, ssh8, neighbors, weights, send4))
-    message, payload = pl.pallas_call(
-        pack_kernel,
-        out_shape=(jax.ShapeDtypeStruct((2 * levels + SMALL, cells), f32), payload_shape),
-        in_specs=[HBM] * 3 + [VMEM] * 2,
-        out_specs=(VMEM,) * 2,
-        scratch_shapes=[vmem(8, LANES), semaphores(3)],
-        compiler_params=grant(8),
-        cost_estimate=estimate(1000000, 2000000),
-        name="pack",
-    )(*hbm(theta, salt, ssh8), small, picked_small)
-
     def device(i, j):
         return (i % regions) * doms + j
 
@@ -532,23 +513,23 @@
     swap_in = lax.ppermute(message, AXES, inner)
     swap_out = lax.ppermute(message, AXES, outer)
     heights = lax.all_to_all(payload, AXES, 0, 0)
+    heights, small_later = lax.optimization_barrier((heights, small))
     pivots, part = pl.pallas_call(
         local_kernel,
         out_shape=(
             jax.ShapeDtypeStruct((3, 8 * levels, LANES), f32),
             jax.ShapeDtypeStruct((PART_WEIGHT + 8, cells), f32),
         ),
-        in_specs=[HBM, HBM, VMEM, HBM, HBM],
+        in_specs=[VMEM, HBM, HBM],
         out_specs=(VMEM,) * 2,
         scratch_shapes=[
-            vmem(levels, cells), vmem(levels, cells),
             vmem(levels - 1, cells), vmem(8, LANES, dtype=jnp.int32), vmem(8 * levels, LANES),
-            vmem(5 * levels, cells, dtype=jnp.bfloat16), semaphores(4),
+            semaphores(2),
         ],
         compiler_params=grant(8),
         cost_estimate=estimate(40000000000, 4000000),
         name="local",
-    )(*hbm(theta, salt), small, *hbm(kappa, depth8))
+    )(small_later, *hbm(kappa, depth8))
     small_below, small_above, swap_in, swap_out, heights, pivots, part = lax.optimization_barrier(
         (small_below, small_above, swap_in, swap_out, heights, pivots, part)
     )
@@ -559,15 +540,15 @@
             functools.partial(surface_kernel, last=last, shape=(regions, doms)),
             out_shape=shape,
             in_specs=[VMEM] * 9,
-            out_specs=VMEM,
+            out_specs=VMEM if last else HBM,
             scratch_shapes=[vmem(8 * SMALL, LANES)] * 4
             + [vmem(32, LANES)] * 3
-            + [vmem(32, 8, LANES)],
+            + [vmem(32, 8, LANES), vmem(*shape.shape), semaphores(1)],
             compiler_params=grant(8),
             cost_estimate=estimate(1000, 1000),
             name="surface_last" if last else "surface_first",
         )(
-            small_below, small_above, values, small, swap_in, swap_out, send4, pivots, part
+            small_below, small_above, values, small, swap_in, swap_out, sends, pivots, part
         )
 
     heights2 = lax.all_to_all(subcycles(heights, False), AXES, 0, 0)
@@ -579,11 +560,13 @@
         out_specs=(HBM,) * 2,
         scratch_shapes=[
             vmem(2, levels, cells),
-            vmem(5 * levels, 2 * cells + 2 * listed, dtype=jnp.bfloat16),
+            vmem(5 * levels, 3 * cells + 2 * listed, dtype=jnp.bfloat16),
+            vmem(2, TILE + 2 * cells + 2 * listed, TILE, dtype=jnp.bfloat16),
+            vmem(2, TILE + 2 * cells + 2 * listed, TILE, dtype=jnp.bfloat16),
             vmem(2, 8 * levels, LANES), vmem(2, levels, cells), semaphores(2), semaphores(4),
         ],
         cost_estimate=estimate(4000000000, 8000000),
-        compiler_params=grant(12),
+        compiler_params=grant(20),
         name="tracers",
     )(
         *hbm(theta, salt), small, small_below, small_above, below, above, swap_in, swap_out,

time: 44.9 us -> 43.6 us (0.971)
  starting transfers between devices: 17.7 us -> 21.2 us
  waiting for transfers between devices: 5.24 us -> 2.07 us
  Pallas kernels: 20.8 us -> 19 us
    all_to_all x1, starting transfers between devices: 2.73 us -> 7.93 us  [body(): heights2 = lax.all_to_all(subcycles(heights, False), AXES, 0, 0)]
    pallas_call x1, Pallas kernels: 4.53 us -> 1.62 us  [body(): pl.pallas_call(local_kernel, out_shape=(jax.ShapeDtypeStruct((3, 8 * leve...]
    ppermute x1, waiting for transfers between devices: 2.38 us -> 0.01 us  [body(): above = lax.ppermute(picked, AXES, downward)]
    pallas_call x1, Pallas kernels: 8.77 us -> 9.96 us  [body(): pl.pallas_call(tracer_kernel, out_shape=(jax.ShapeDtypeStruct((levels, ce...]
    ppermute x1, starting transfers between devices: 2.99 us -> 1.82 us  [body(): small_below = lax.ppermute(picked_small, AXES, upward)]
    ppermute x1, starting transfers between devices: 1.82 us -> 0.87 us  [body(): below = lax.ppermute(picked, AXES, upward)]
    all_to_all x1, waiting for transfers between devices: 2.85 us -> 2.05 us  [body(): heights = lax.all_to_all(payload, AXES, 0, 0)]
  transfers between devices with their start and end apart: 8 -> 8, of which waited for: 2 -> 1; matrix products, arithmetic and copies ran while one was open for 0% -> 0% of each run, Pallas kernels for 39% -> 36%
where the time goes in v4:
time: 43.6 us; the launch traced here: 43 us
  starting transfers between devices  21.2 us (49%)
  Pallas kernels  19 us (44%)
  waiting for transfers between devices  2.07 us (5%)
  between operations  0.74 us (2%)
    pallas_call x1, Pallas kernels, body(): pl.pallas_call(tracer_kernel, out_shape=(jax.ShapeDtypeStruct((levels, ce...  9.96 us
    all_to_all x1, starting transfers between devices, body(): heights2 = lax.all_to_all(subcycles(heights, False), AXES, 0, 0)  7.93 us
    all_to_all x1, starting transfers between devices, body(): heights = lax.all_to_all(payload, AXES, 0, 0)  7.3 us
    pallas_call x2, Pallas kernels, subcycles(): pl.pallas_call(functools.partial(surface_kernel, last=last, shape=(region...  3.67 us
    pallas_call x1, Pallas kernels, body(): pl.pallas_call(pick_kernel, out_shape=(jax.ShapeDtypeStruct((SMALL, cells...  2.09 us
    all_to_all x1, waiting for transfers between devices, body(): heights = lax.all_to_all(payload, AXES, 0, 0)  2.05 us
    ppermute x1, starting transfers between devices, body(): small_below = lax.ppermute(picked_small, AXES, upward)  1.82 us
    pallas_call x1, Pallas kernels, body(): pl.pallas_call(heights_kernel, out_shape=(payload_shape, jax.ShapeDtypeSt...  1.64 us
  transfers between devices with their start and end apart: 8, of which 1 were waited for; matrix products, arithmetic and copies ran while one was open for 0% of the time, Pallas kernels for 36%

profile of v4, /device:TPU:0, one launch (start us, length us, event | category | flops | bytes accessed | tf_op | source)
XLA Modules:
  0.0 43.0 jit_solution(3897813935123770735)
XLA Ops:
  0.6 1.6 %heights.1 = (f32[32,3,4,128]{3,2,1,0:T(4,128)}, s32[4,128]{1,0:T(4,128)S(1)}) custom-call(f32[8,128]{1,0:T(8,128)} %bitcast.4, s32[4,128]{1,0:T(4,128)} %bitcast.6), custom_call_target="tpu_custom_call" | custom-call | flops 1000 | bytes 1000 | tf_op jit(solution)/shard_map/heights/pallas_call | solution.py:469
  2.3 7.3 %all-to-all-start = ((f32[32,3,4,128]{3,2,1,0:T(4,128)}), f32[32,3,4,128]{3,2,1,0:T(4,128)S(1)}, u32[]{:S(2)}, u32[]{:S(2)}) async-start(f32[32,3,4,128]{3,2,1,0:T(4,128)} %get-tuple-element.25), calls=%async_computation | async-start | bytes 393216 | tf_op jit(solution)/shard_map/all_to_all | solution.py:515
  9.6 2.1 %pick.1 = (f32[16,1024]{1,0:T(8,128)S(1)}, f32[128,512]{1,0:T(8,128)S(1)}, f32[16,512]{1,0:T(8,128)S(1)}, f32[144,1024]{1,0:T(8,128)S(1)}) custom-call(f32[64,1024]{1,0:T(8,128)} %theta_in.3, f32[64,1024]{1,0:T(8,128)} %salt_in.3, s32[8,128]{1,0:T(8,128)} %bitcast.8, f32[8,128]{1,0:T(8,128)} %bitcast.5, s32[6,1024]{1,0:T(8,128)} %neighbors.1, ...), custom_call_target="tpu_custom_call" | custom-call | flops 2000000 | bytes 2000000 | tf_op jit(solution)/shard_map/pick/pallas_call | solution.py:479
  11.7 1.8 %collective-permute-start = (f32[16,512]{1,0:T(8,128)S(1)}, f32[16,512]{1,0:T(8,128)S(1)}, u32[]{:S(2)}, u32[]{:S(2)}) collective-permute-start(f32[16,512]{1,0:T(8,128)S(1)} %get-tuple-element.23), channel_id=1, source_target_pairs={{0,8},{1,9},{2,10},{3,11},{4,12},{5,13},{6,14},{7,15},{8,16},{9,17... | collective-permute-start | bytes 98312 | tf_op jit(solution)/shard_map/ppermute | solution.py:511
  13.5 0.0 collective-permute-start.2
  13.5 0.7 %collective-permute-start.3 = (f32[144,1024]{1,0:T(8,128)S(1)}, f32[144,1024]{1,0:T(8,128)S(1)}, u32[]{:S(2)}, u32[]{:S(2)}) collective-permute-start(f32[144,1024]{1,0:T(8,128)S(1)} %get-tuple-element.24), channel_id=1, source_target_pairs={{1,2},{2,1},{3,4},{4,3},{5,6},{6,5},{9,10},{10,9},{11,12},{12,11},... | collective-permute-start | bytes 1769480 | tf_op jit(solution)/shard_map/ppermute | solution.py:514
  14.2 1.2 %collective-permute-start.1 = (f32[16,512]{1,0:T(8,128)S(1)}, f32[16,512]{1,0:T(8,128)S(1)}, u32[]{:S(2)}, u32[]{:S(2)}) collective-permute-start(f32[16,512]{1,0:T(8,128)S(1)} %get-tuple-element.23), channel_id=1, source_target_pairs={{8,0},{9,1},{10,2},{11,3},{12,4},{13,5},{14,6},{15,7},{16,8},{17,9... | collective-permute-start | bytes 98312 | tf_op jit(solution)/shard_map/ppermute | solution.py:512
  15.4 0.9 %collective-permute-start.4 = (f32[128,512]{1,0:T(8,128)S(1)}, f32[128,512]{1,0:T(8,128)S(1)}, u32[]{:S(2)}, u32[]{:S(2)}) collective-permute-start(f32[128,512]{1,0:T(8,128)S(1)} %get-tuple-element.32), channel_id=1, source_target_pairs={{0,8},{1,9},{2,10},{3,11},{4,12},{5,13},{6,14},{7,15},{8,16},{9,17... | collective-permute-start | bytes 786440 | tf_op jit(solution)/shard_map/ppermute | solution.py:509
  16.3 2.1 %all-to-all-done.heights = f32[32,3,4,128]{3,2,1,0:T(4,128)S(1)} async-done(((f32[32,3,4,128]{3,2,1,0:T(4,128)}), f32[32,3,4,128]{3,2,1,0:T(4,128)S(1)}, u32[]{:S(2)}, u32[]{:S(2)}) %all-to-all-start) | async-done | bytes 196640 | tf_op jit(solution)/shard_map/all_to_all | solution.py:515
  18.3 0.0 collective-permute-done.small_below.below
  18.3 1.4 %collective-permute-start.5 = (f32[128,512]{1,0:T(8,128)S(1)}, f32[128,512]{1,0:T(8,128)}, u32[]{:S(2)}, u32[]{:S(2)}) collective-permute-start(f32[128,512]{1,0:T(8,128)S(1)} %get-tuple-element.32), channel_id=1, source_target_pairs={{8,0},{9,1},{10,2},{11,3},{12,4},{13,5},{14,6},{15,7},{16,8},{17,9... | collective-permute-start | bytes 786440 | tf_op jit(solution)/shard_map/ppermute | solution.py:510
  19.8 1.6 %local.1 = (f32[3,512,128]{2,1,0:T(8,128)S(1)}, f32[16,1024]{1,0:T(8,128)S(1)}) custom-call(f32[16,1024]{1,0:T(8,128)S(1)} %get-tuple-element.27.small.own_in, f32[63,1024]{1,0:T(8,128)} %kappa_in.1, s32[8,128]{1,0:T(8,128)} %bitcast.9), custom_call_target="tpu_custom_call" | custom-call | flops 40000000000 | bytes 4000000 | tf_op jit(solution)/shard_map/local/pallas_call | solution.py:517
  21.4 0.0 collective-permute-done.1.small_above.above
  21.4 0.0 collective-permute-done.2.swap_in
  21.4 0.0 collective-permute-done.3.swap_out
  21.4 2.0 %surface_first.1 = f32[32,3,4,128]{3,2,1,0:T(4,128)} custom-call(f32[16,512]{1,0:T(8,128)S(1)} %collective-permute-done.small_below.below, f32[16,512]{1,0:T(8,128)S(1)} %collective-permute-done.1.small_above.above, f32[32,3,4,128]{3,2,1,0:T(4,128)S(1)} %all-to-all-done.heights, f32[16,1024]{1,0:T(8,128)S(1)} %get-tuple-element.27.small.own_in, ...), custom_call_target="tpu_custom_call" | custom-call | flops 1000 | bytes 1000 | tf_op jit(solution)/shard_map/surface_first/pallas_call | solution.py:539
  23.4 7.9 %all-to-all-start.1 = ((f32[32,3,4,128]{3,2,1,0:T(4,128)}), f32[32,3,4,128]{3,2,1,0:T(4,128)S(1)}, u32[]{:S(2)}, u32[]{:S(2)}) async-start(f32[32,3,4,128]{3,2,1,0:T(4,128)} %surface_first.1), calls=%async_computation.1 | async-start | bytes 393216 | tf_op jit(solution)/shard_map/all_to_all | solution.py:554
  31.3 0.0 collective-permute-done.4.below
  31.4 0.0 collective-permute-done.5.above
  31.4 10.0 %tracers.1 = (f32[64,1024]{1,0:T(8,128)}, f32[64,1024]{1,0:T(8,128)}) custom-call(f32[64,1024]{1,0:T(8,128)} %theta_in.3, f32[64,1024]{1,0:T(8,128)} %salt_in.3, f32[16,1024]{1,0:T(8,128)S(1)} %get-tuple-element.27.small.own_in, f32[16,512]{1,0:T(8,128)S(1)} %collective-permute-done.small_below.below, ...), custom_call_target="tpu_custom_call" | custom-call | flops 4000000000 | bytes 8000000 | tf_op jit(solution)/shard_map/tracers/pallas_call | solution.py:556
  41.3 0.0 all-to-all-done.1.heights
  41.3 1.7 %surface_last.1 = f32[8,128]{1,0:T(8,128)} custom-call(f32[16,512]{1,0:T(8,128)S(1)} %collective-permute-done.small_below.below, f32[16,512]{1,0:T(8,128)S(1)} %collective-permute-done.1.small_above.above, f32[32,3,4,128]{3,2,1,0:T(4,128)S(1)} %all-to-all-done.1.heights, f32[16,1024]{1,0:T(8,128)S(1)} %get-tuple-element.27.small.own_in, ...), custom_call_target="tpu_custom_call" | custom-call | flops 1000 | bytes 1000 | tf_op jit(solution)/shard_map/surface_last/pallas_call | solution.py:539
Async XLA Ops:
  2.3 16.1 %all-to-all-start = ((f32[32,3,4,128]{3,2,1,0:T(4,128)}), f32[32,3,4,128]{3,2,1,0:T(4,128)S(1)}, u32[]{:S(2)}, u32[]{:S(2)}) async-start(f32[32,3,4,128]{3,2,1,0:T(4,128)} %get-tuple-element.25), calls=%async_computation | async-start | bytes 393216 | tf_op jit(solution)/shard_map/all_to_all | solution.py:515
  11.7 6.7 %collective-permute-start = (f32[16,512]{1,0:T(8,128)S(1)}, f32[16,512]{1,0:T(8,128)S(1)}, u32[]{:S(2)}, u32[]{:S(2)}) collective-permute-start(f32[16,512]{1,0:T(8,128)S(1)} %get-tuple-element.23), channel_id=1, source_target_pairs={{0,8},{1,9},{2,10},{3,11},{4,12},{5,13},{6,14},{7,15},{8,16},{9,17... | collective-permute-start | bytes 98312 | tf_op jit(solution)/shard_map/ppermute | solution.py:511
  13.5 7.9 %collective-permute-start.2 = (f32[144,1024]{1,0:T(8,128)S(1)}, f32[144,1024]{1,0:T(8,128)S(1)}, u32[]{:S(2)}, u32[]{:S(2)}) collective-permute-start(f32[144,1024]{1,0:T(8,128)S(1)} %get-tuple-element.24), channel_id=1, source_target_pairs={{0,1},{1,0},{2,3},{3,2},{4,5},{5,4},{6,7},{7,6},{8,9},{9,8},{10,11... | collective-permute-start | bytes 1769480 | tf_op jit(solution)/shard_map/ppermute | solution.py:513
  13.5 7.9 %collective-permute-start.3 = (f32[144,1024]{1,0:T(8,128)S(1)}, f32[144,1024]{1,0:T(8,128)S(1)}, u32[]{:S(2)}, u32[]{:S(2)}) collective-permute-start(f32[144,1024]{1,0:T(8,128)S(1)} %get-tuple-element.24), channel_id=1, source_target_pairs={{1,2},{2,1},{3,4},{4,3},{5,6},{6,5},{9,10},{10,9},{11,12},{12,11},... | collective-permute-start | bytes 1769480 | tf_op jit(solution)/shard_map/ppermute | solution.py:514
  14.2 7.2 %collective-permute-start.1 = (f32[16,512]{1,0:T(8,128)S(1)}, f32[16,512]{1,0:T(8,128)S(1)}, u32[]{:S(2)}, u32[]{:S(2)}) collective-permute-start(f32[16,512]{1,0:T(8,128)S(1)} %get-tuple-element.23), channel_id=1, source_target_pairs={{8,0},{9,1},{10,2},{11,3},{12,4},{13,5},{14,6},{15,7},{16,8},{17,9... | collective-permute-start | bytes 98312 | tf_op jit(solution)/shard_map/ppermute | solution.py:512
  15.4 15.9 %collective-permute-start.4 = (f32[128,512]{1,0:T(8,128)S(1)}, f32[128,512]{1,0:T(8,128)S(1)}, u32[]{:S(2)}, u32[]{:S(2)}) collective-permute-start(f32[128,512]{1,0:T(8,128)S(1)} %get-tuple-element.32), channel_id=1, source_target_pairs={{0,8},{1,9},{2,10},{3,11},{4,12},{5,13},{6,14},{7,15},{8,16},{9,17... | collective-permute-start | bytes 786440 | tf_op jit(solution)/shard_map/ppermute | solution.py:509
  18.3 13.0 %collective-permute-start.5 = (f32[128,512]{1,0:T(8,128)S(1)}, f32[128,512]{1,0:T(8,128)}, u32[]{:S(2)}, u32[]{:S(2)}) collective-permute-start(f32[128,512]{1,0:T(8,128)S(1)} %get-tuple-element.32), channel_id=1, source_target_pairs={{8,0},{9,1},{10,2},{11,3},{12,4},{13,5},{14,6},{15,7},{16,8},{17,9... | collective-permute-start | bytes 786440 | tf_op jit(solution)/shard_map/ppermute | solution.py:510
  23.4 17.9 %all-to-all-start.1 = ((f32[32,3,4,128]{3,2,1,0:T(4,128)}), f32[32,3,4,128]{3,2,1,0:T(4,128)S(1)}, u32[]{:S(2)}, u32[]{:S(2)}) async-start(f32[32,3,4,128]{3,2,1,0:T(4,128)} %surface_first.1), calls=%async_computation.1 | async-start | bytes 393216 | tf_op jit(solution)/shard_map/all_to_all | solution.py:554

commit v5 on v3

--- a/solution.py
+++ b/solution.py
@@ -59,7 +59,8 @@
 
 def pick_kernel(
     theta_in, salt_in, depth8, ssh8, neighbors, weights, send4,
-    small, picked, picked_small, theta, salt, depths, heights, nbr, wts, sends, loaded
+    small, picked, picked_small, message,
+    theta, salt, depths, heights, nbr, wts, sends, loaded, stored
 ):
     levels, cells = theta.shape
     blocks = cells // LANES
@@ -91,9 +92,12 @@
                     lambda b: source[rows, b * LANES : (b + 1) * LANES], positions, blocks
                 )
 
-    arrivals[5].wait()
+    departures = []
+    for c, tracer in enumerate((theta, salt)):
+        arrivals[5 + c].wait()
+        target = message.at[pl.ds(c * levels, levels), :]
+        departures += copies([(tracer, target)], stored.at[pl.ds(c, 1)])
     pick(theta, picked, levels // 8, 0)
-    arrivals[6].wait()
     pick(salt, picked, levels // 8, levels)
     for b in range(blocks):
         cols = slice(b * LANES, (b + 1) * LANES)
@@ -101,41 +105,35 @@
         wet = level < depths[b : b + 1, :]
         total = jnp.sum(jnp.where(wet, term, 0.0), axis=0, keepdims=True)
         small[ROW_FORCING : ROW_FORCING + 1, cols] = total / math.sqrt(levels)
+    rest = message.at[pl.ds(2 * levels, SMALL), :]
+    departures += copies([(small, rest)], stored.at[pl.ds(2, 1)])
     pick(small, picked_small, SMALL // 8, 0)
-
-
-def pack_kernel(theta, salt, ssh8, small, picked_small, message, payload, heights, loaded):
-    levels = theta.shape[0]
-    arrivals = copies(
-        [
-            (ssh8, heights),
-            (theta, message.at[pl.ds(0, levels), :]),
-            (salt, message.at[pl.ds(levels, levels), :]),
-        ],
-        loaded,
+    for copy in departures:
+        copy.wait()
+
+
+def heights_kernel(ssh8, send4, payload_out, sends, heights, payload, loaded):
+    for copy in copies([(ssh8, heights), (send4, sends)], loaded):
+        copy.wait()
+    broadcast_heights(heights[...], heights, sends, payload)
+    for copy in copies([(payload, payload_out)], loaded.at[pl.ds(2, 1)]):
+        copy.wait()
+
+
+def broadcast_heights(own, rows, sends, payload):
+    positions = jnp.concatenate([sends[...], sends[...]], axis=0)
+    blocks = own.shape[0]
+    tail = pick_block(
+        lambda b: jnp.broadcast_to(rows[b : b + 1, :], (8, LANES)), positions, blocks
     )
-    message[2 * levels :, :] = small[...]
-    arrivals[0].wait()
-    blocks = heights.shape[0]
-    row = slice(ROW_SURFACE, ROW_SURFACE + 1)
-    tail = jnp.concatenate(
-        [
-            picked_small[row, t * LANES : (t + 1) * LANES]
-            for t in range(picked_small.shape[1] // LANES)
-        ],
-        axis=0,
-    )
-    send_all(payload, heights[...], tail)
-    for copy in arrivals[1:]:
-        copy.wait()
+    send_all(payload, own, tail[0 : sends.shape[0], :])
 
 
 def send_all(payload, head, tail):
-    blocks = head.shape[0]
-
     def send(i, carry):
-        payload[i, 0:blocks, :] = head
-        payload[i, blocks:, :] = tail
+        payload[i, 0] = head[0:4, :]
+        payload[i, 1] = head[4:8, :]
+        payload[i, 2] = tail
         return carry
 
     lax.fori_loop(0, payload.shape[0], send, 0)
@@ -170,8 +168,9 @@
 
 
 def surface_kernel(
-    below, above, heights, own_in, swap_in, swap_out, sends, pivots, part, out,
-    stat_own, stat_left, stat_right, stat_list, ext_own, ext_left, ext_right, ext_list, *, last, shape
+    below, above, heights, own_in, swap_in, swap_out, sends, pivots, part, out_ref,
+    stat_own, stat_left, stat_right, stat_list, ext_own, ext_left, ext_right, ext_list, out, stored,
+    *, last, shape
 ):
     blocks = own_in.shape[1] // LANES
     rest = slice(swap_in.shape[0] - SMALL, swap_in.shape[0])
@@ -193,13 +192,13 @@
         stat_list[pl.ds(half + b, SMALL, stride=8), :] = above[:, cols]
 
     def full(n, side):
-        value = heights[place[n], 0:8, :]
+        value = jnp.concatenate([heights[place[n], 0], heights[place[n], 1]], axis=0)
         if side is None:
             return value
         return jnp.where(place[13 + side], value, 0.0)
 
     def listed(n):
-        return heights[place[n], 8:12, :]
+        return heights[place[n], 2]
 
     own = full(0, None)
     left2, left, right, right2 = full(1, 0), full(2, 1), full(3, 2), full(4, 3)
@@ -248,15 +247,12 @@
     ext_own[24:32, :] = new_list
     final = banded_step(ext_own, stat_own, new_own, sub)
     if last:
-        out[...] = final
+        out_ref[...] = final
         return
     ext_left[0:8, :] = final
-    positions = jnp.concatenate([sends[...], sends[...]], axis=0)
-    tail = pick_block(
-        lambda b: jnp.broadcast_to(ext_left[b : b + 1, :], (8, LANES)), positions, blocks
-    )
-
-    send_all(out, final, tail[0:4, :])
+    broadcast_heights(final, ext_left, sends, out)
+    for copy in copies([(out, out_ref)], stored):
+        copy.wait()
 
 
 def stage(sources, depth, target, width, offset, level):
@@ -480,40 +476,40 @@
     def semaphores(count):
         return pltpu.SemaphoreType.DMA((count,))
 
-    payload_shape = jax.ShapeDtypeStruct((devices, 12, LANES), f32)
+    payload_shape = jax.ShapeDtypeStruct((devices, 3, 4, LANES), f32)
 
     def hbm(*arrays):
         return [pltpu.with_memory_space_constraint(array, pltpu.HBM) for array in arrays]
 
-    small, picked, picked_small = pl.pallas_call(
+    payload, sends = pl.pallas_call(
+        heights_kernel,
+        out_shape=(payload_shape, jax.ShapeDtypeStruct((listed // LANES, LANES), jnp.int32)),
+        in_specs=[HBM] * 2,
+        out_specs=(HBM, VMEM),
+        scratch_shapes=[vmem(8, LANES), vmem(*payload_shape.shape), semaphores(3)],
+        compiler_params=grant(8),
+        cost_estimate=estimate(1000, 1000),
+        name="heights",
+    )(*hbm(ssh8, send4))
+    small, picked, picked_small, message = pl.pallas_call(
         pick_kernel,
         out_shape=(
             jax.ShapeDtypeStruct((SMALL, cells), f32),
             jax.ShapeDtypeStruct((2 * levels, listed), f32),
             jax.ShapeDtypeStruct((SMALL, listed), f32),
+            jax.ShapeDtypeStruct((2 * levels + SMALL, cells), f32),
         ),
         in_specs=[HBM] * 7,
-        out_specs=(VMEM,) * 3,
+        out_specs=(VMEM,) * 3 + (HBM,),
         scratch_shapes=[
             vmem(levels, cells), vmem(levels, cells),
             vmem(8, LANES, dtype=jnp.int32), vmem(8, LANES), vmem(6, cells, dtype=jnp.int32),
-            vmem(6, cells), vmem(listed // LANES, LANES, dtype=jnp.int32), semaphores(7),
+            vmem(6, cells), vmem(listed // LANES, LANES, dtype=jnp.int32), semaphores(7), semaphores(3),
         ],
         compiler_params=grant(8),
         cost_estimate=estimate(2000000, 2000000),
         name="pick",
     )(*hbm(theta, salt, depth8, ssh8, neighbors, weights, send4))
-    message, payload = pl.pallas_call(
-        pack_kernel,
-        out_shape=(jax.ShapeDtypeStruct((2 * levels + SMALL, cells), f32), payload_shape),
-        in_specs=[HBM] * 3 + [VMEM] * 2,
-        out_specs=(VMEM,) * 2,
-        scratch_shapes=[vmem(8, LANES), semaphores(3)],
-        compiler_params=grant(8),
-        cost_estimate=estimate(1000000, 2000000),
-        name="pack",
-    )(*hbm(theta, salt, ssh8), small, picked_small)
-
     def device(i, j):
         return (i % regions) * doms + j
 
@@ -532,6 +528,7 @@
     swap_in = lax.ppermute(message, AXES, inner)
     swap_out = lax.ppermute(message, AXES, outer)
     heights = lax.all_to_all(payload, AXES, 0, 0)
+    heights, small_later = lax.optimization_barrier((heights, small))
     pivots, part = pl.pallas_call(
         local_kernel,
         out_shape=(
@@ -548,7 +545,7 @@
         compiler_params=grant(8),
         cost_estimate=estimate(40000000000, 4000000),
         name="local",
-    )(*hbm(theta, salt), small, *hbm(kappa, depth8))
+    )(*hbm(theta, salt), small_later, *hbm(kappa, depth8))
     small_below, small_above, swap_in, swap_out, heights, pivots, part = lax.optimization_barrier(
         (small_below, small_above, swap_in, swap_out, heights, pivots, part)
     )
@@ -559,15 +556,15 @@
             functools.partial(surface_kernel, last=last, shape=(regions, doms)),
             out_shape=shape,
             in_specs=[VMEM] * 9,
-            out_specs=VMEM,
+            out_specs=VMEM if last else HBM,
             scratch_shapes=[vmem(8 * SMALL, LANES)] * 4
             + [vmem(32, LANES)] * 3
-            + [vmem(32, 8, LANES)],
+            + [vmem(32, 8, LANES), vmem(*shape.shape), semaphores(1)],
             compiler_params=grant(8),
             cost_estimate=estimate(1000, 1000),
             name="surface_last" if last else "surface_first",
         )(
-            small_below, small_above, values, small, swap_in, swap_out, send4, pivots, part
+            small_below, small_above, values, small, swap_in, swap_out, sends, pivots, part
         )
 
     heights2 = lax.all_to_all(subcycles(heights, False), AXES, 0, 0)

time: 44.9 us -> 43.1 us (0.960)
  waiting for transfers between devices: 5.24 us -> 1.79 us
  starting transfers between devices: 17.7 us -> 18.9 us
    all_to_all x1, starting transfers between devices: 2.73 us -> 5.62 us  [body(): heights2 = lax.all_to_all(subcycles(heights, False), AXES, 0, 0)]
    ppermute x1, waiting for transfers between devices: 2.38 us -> 0.01 us  [body(): above = lax.ppermute(picked, AXES, downward)]
    ppermute x1, starting transfers between devices: 2.99 us -> 1.82 us  [body(): small_below = lax.ppermute(picked_small, AXES, upward)]
    all_to_all x1, waiting for transfers between devices: 2.85 us -> 1.77 us  [body(): heights = lax.all_to_all(payload, AXES, 0, 0)]
    ppermute x1, starting transfers between devices: 1.82 us -> 0.87 us  [body(): below = lax.ppermute(picked, AXES, upward)]
    pallas_call x1, Pallas kernels: 1.89 us -> 2.37 us  [body(): pl.pallas_call(pick_kernel, out_shape=(jax.ShapeDtypeStruct((SMALL, cells...]
  transfers between devices with their start and end apart: 8 -> 8, of which waited for: 2 -> 1; matrix products, arithmetic and copies ran while one was open for 0% -> 0% of each run, Pallas kernels for 39% -> 42%
where the time goes in v5:
time: 43.1 us; the launch traced here: 42.4 us
  Pallas kernels  21 us (49%)
  starting transfers between devices  18.9 us (44%)
  waiting for transfers between devices  1.79 us (4%)
  between operations  0.74 us (2%)
    pallas_call x1, Pallas kernels, body(): pl.pallas_call(tracer_kernel, out_shape=(jax.ShapeDtypeStruct((levels, ce...  8.77 us
    all_to_all x1, starting transfers between devices, body(): heights = lax.all_to_all(payload, AXES, 0, 0)  7.3 us
    all_to_all x1, starting transfers between devices, body(): heights2 = lax.all_to_all(subcycles(heights, False), AXES, 0, 0)  5.62 us
    pallas_call x1, Pallas kernels, body(): pl.pallas_call(local_kernel, out_shape=(jax.ShapeDtypeStruct((3, 8 * leve...  4.53 us
    pallas_call x2, Pallas kernels, subcycles(): pl.pallas_call(functools.partial(surface_kernel, last=last, shape=(region...  3.67 us
    pallas_call x1, Pallas kernels, body(): pl.pallas_call(pick_kernel, out_shape=(jax.ShapeDtypeStruct((SMALL, cells...  2.37 us
    ppermute x1, starting transfers between devices, body(): small_below = lax.ppermute(picked_small, AXES, upward)  1.82 us
    all_to_all x1, waiting for transfers between devices, body(): heights = lax.all_to_all(payload, AXES, 0, 0)  1.77 us
  transfers between devices with their start and end apart: 8, of which 1 were waited for; matrix products, arithmetic and copies ran while one was open for 0% of the time, Pallas kernels for 42%

profile of v5, /device:TPU:0, one launch (start us, length us, event | category | flops | bytes accessed | tf_op | source)
XLA Modules:
  0.0 42.4 jit_solution(17959565050133031285)
XLA Ops:
  0.6 1.6 %heights.1 = (f32[32,3,4,128]{3,2,1,0:T(4,128)}, s32[4,128]{1,0:T(4,128)S(1)}) custom-call(f32[8,128]{1,0:T(8,128)} %bitcast.4, s32[4,128]{1,0:T(4,128)} %bitcast.6), custom_call_target="tpu_custom_call" | custom-call | flops 1000 | bytes 1000 | tf_op jit(solution)/shard_map/heights/pallas_call | solution.py:484
  2.3 7.3 %all-to-all-start = ((f32[32,3,4,128]{3,2,1,0:T(4,128)}), f32[32,3,4,128]{3,2,1,0:T(4,128)S(1)}, u32[]{:S(2)}, u32[]{:S(2)}) async-start(f32[32,3,4,128]{3,2,1,0:T(4,128)} %get-tuple-element.25), calls=%async_computation | async-start | bytes 393216 | tf_op jit(solution)/shard_map/all_to_all | solution.py:530
  9.6 2.4 %pick.1 = (f32[16,1024]{1,0:T(8,128)S(1)}, f32[128,512]{1,0:T(8,128)S(1)}, f32[16,512]{1,0:T(8,128)S(1)}, f32[144,1024]{1,0:T(8,128)}) custom-call(f32[64,1024]{1,0:T(8,128)} %theta_in.5, f32[64,1024]{1,0:T(8,128)} %salt_in.5, s32[8,128]{1,0:T(8,128)} %bitcast.8, f32[8,128]{1,0:T(8,128)} %bitcast.5, s32[6,1024]{1,0:T(8,128)} %neighbors.1, ...), custom_call_target="tpu_custom_call" | custom-call | flops 2000000 | bytes 2000000 | tf_op jit(solution)/shard_map/pick/pallas_call | solution.py:494
  12.0 1.8 %collective-permute-start = (f32[16,512]{1,0:T(8,128)S(1)}, f32[16,512]{1,0:T(8,128)S(1)}, u32[]{:S(2)}, u32[]{:S(2)}) collective-permute-start(f32[16,512]{1,0:T(8,128)S(1)} %get-tuple-element.23), channel_id=1, source_target_pairs={{0,8},{1,9},{2,10},{3,11},{4,12},{5,13},{6,14},{7,15},{8,16},{9,17... | collective-permute-start | bytes 98312 | tf_op jit(solution)/shard_map/ppermute | solution.py:526
  13.8 0.0 collective-permute-start.2
  13.8 0.7 %collective-permute-start.3 = (f32[144,1024]{1,0:T(8,128)}, f32[144,1024]{1,0:T(8,128)S(1)}, u32[]{:S(2)}, u32[]{:S(2)}) collective-permute-start(f32[144,1024]{1,0:T(8,128)} %get-tuple-element.24), channel_id=1, source_target_pairs={{1,2},{2,1},{3,4},{4,3},{5,6},{6,5},{9,10},{10,9},{11,12},{12,11},... | collective-permute-start | bytes 1769480 | tf_op jit(solution)/shard_map/ppermute | solution.py:529
  14.5 1.2 %collective-permute-start.1 = (f32[16,512]{1,0:T(8,128)S(1)}, f32[16,512]{1,0:T(8,128)S(1)}, u32[]{:S(2)}, u32[]{:S(2)}) collective-permute-start(f32[16,512]{1,0:T(8,128)S(1)} %get-tuple-element.23), channel_id=1, source_target_pairs={{8,0},{9,1},{10,2},{11,3},{12,4},{13,5},{14,6},{15,7},{16,8},{17,9... | collective-permute-start | bytes 98312 | tf_op jit(solution)/shard_map/ppermute | solution.py:527
  15.7 0.9 %collective-permute-start.4 = (f32[128,512]{1,0:T(8,128)S(1)}, f32[128,512]{1,0:T(8,128)}, u32[]{:S(2)}, u32[]{:S(2)}) collective-permute-start(f32[128,512]{1,0:T(8,128)S(1)} %get-tuple-element.32), channel_id=1, source_target_pairs={{0,8},{1,9},{2,10},{3,11},{4,12},{5,13},{6,14},{7,15},{8,16},{9,17... | collective-permute-start | bytes 786440 | tf_op jit(solution)/shard_map/ppermute | solution.py:524
  16.6 1.8 %all-to-all-done.heights = f32[32,3,4,128]{3,2,1,0:T(4,128)S(1)} async-done(((f32[32,3,4,128]{3,2,1,0:T(4,128)}), f32[32,3,4,128]{3,2,1,0:T(4,128)S(1)}, u32[]{:S(2)}, u32[]{:S(2)}) %all-to-all-start) | async-done | bytes 196640 | tf_op jit(solution)/shard_map/all_to_all | solution.py:530
  18.3 0.0 collective-permute-done.small_below.below
  18.3 1.4 %collective-permute-start.5 = (f32[128,512]{1,0:T(8,128)S(1)}, f32[128,512]{1,0:T(8,128)}, u32[]{:S(2)}, u32[]{:S(2)}) collective-permute-start(f32[128,512]{1,0:T(8,128)S(1)} %get-tuple-element.32), channel_id=1, source_target_pairs={{8,0},{9,1},{10,2},{11,3},{12,4},{13,5},{14,6},{15,7},{16,8},{17,9... | collective-permute-start | bytes 786440 | tf_op jit(solution)/shard_map/ppermute | solution.py:525
  19.8 4.5 %local.1 = (f32[3,512,128]{2,1,0:T(8,128)S(1)}, f32[208,1024]{1,0:T(8,128)S(1)}) custom-call(f32[64,1024]{1,0:T(8,128)} %theta_in.5, f32[64,1024]{1,0:T(8,128)} %salt_in.5, f32[16,1024]{1,0:T(8,128)S(1)} %get-tuple-element.27.small.own_in, f32[63,1024]{1,0:T(8,128)} %kappa_in.1, s32[8,128]{1,0:T(8,128)} %bitcast.9), custom_call_target="tpu_custom_call" | custom-call | flops 40000000000 | bytes 4000000 | tf_op jit(solution)/shard_map/local/pallas_call | solution.py:532
  24.3 0.0 collective-permute-done.1.small_above.above
  24.3 0.0 collective-permute-done.2.swap_in
  24.3 0.0 collective-permute-done.3.swap_out
  24.3 2.0 %surface_first.1 = f32[32,3,4,128]{3,2,1,0:T(4,128)} custom-call(f32[16,512]{1,0:T(8,128)S(1)} %collective-permute-done.small_below.below, f32[16,512]{1,0:T(8,128)S(1)} %collective-permute-done.1.small_above.above, f32[32,3,4,128]{3,2,1,0:T(4,128)S(1)} %all-to-all-done.heights, f32[16,1024]{1,0:T(8,128)S(1)} %get-tuple-element.27.small.own_in, ...), custom_call_target="tpu_custom_call" | custom-call | flops 1000 | bytes 1000 | tf_op jit(solution)/shard_map/surface_first/pallas_call | solution.py:555
  26.3 5.6 %all-to-all-start.1 = ((f32[32,3,4,128]{3,2,1,0:T(4,128)}), f32[32,3,4,128]{3,2,1,0:T(4,128)S(1)}, u32[]{:S(2)}, u32[]{:S(2)}) async-start(f32[32,3,4,128]{3,2,1,0:T(4,128)} %surface_first.1), calls=%async_computation.1 | async-start | bytes 393216 | tf_op jit(solution)/shard_map/all_to_all | solution.py:570
  31.9 0.0 collective-permute-done.4.below
  32.0 0.0 collective-permute-done.5.above
  32.0 8.8 %tracers.1 = (f32[64,1024]{1,0:T(8,128)}, f32[64,1024]{1,0:T(8,128)}) custom-call(f32[64,1024]{1,0:T(8,128)} %theta_in.5, f32[64,1024]{1,0:T(8,128)} %salt_in.5, f32[16,1024]{1,0:T(8,128)S(1)} %get-tuple-element.27.small.own_in, f32[16,512]{1,0:T(8,128)S(1)} %collective-permute-done.small_below.below, ...), custom_call_target="tpu_custom_call" | custom-call | flops 4000000000 | bytes 8000000 | tf_op jit(solution)/shard_map/tracers/pallas_call | solution.py:572
  40.7 0.0 all-to-all-done.1.heights
  40.8 1.7 %surface_last.1 = f32[8,128]{1,0:T(8,128)} custom-call(f32[16,512]{1,0:T(8,128)S(1)} %collective-permute-done.small_below.below, f32[16,512]{1,0:T(8,128)S(1)} %collective-permute-done.1.small_above.above, f32[32,3,4,128]{3,2,1,0:T(4,128)S(1)} %all-to-all-done.1.heights, f32[16,1024]{1,0:T(8,128)S(1)} %get-tuple-element.27.small.own_in, ...), custom_call_target="tpu_custom_call" | custom-call | flops 1000 | bytes 1000 | tf_op jit(solution)/shard_map/surface_last/pallas_call | solution.py:555
Async XLA Ops:
  2.3 16.1 %all-to-all-start = ((f32[32,3,4,128]{3,2,1,0:T(4,128)}), f32[32,3,4,128]{3,2,1,0:T(4,128)S(1)}, u32[]{:S(2)}, u32[]{:S(2)}) async-start(f32[32,3,4,128]{3,2,1,0:T(4,128)} %get-tuple-element.25), calls=%async_computation | async-start | bytes 393216 | tf_op jit(solution)/shard_map/all_to_all | solution.py:530
  12.0 6.4 %collective-permute-start = (f32[16,512]{1,0:T(8,128)S(1)}, f32[16,512]{1,0:T(8,128)S(1)}, u32[]{:S(2)}, u32[]{:S(2)}) collective-permute-start(f32[16,512]{1,0:T(8,128)S(1)} %get-tuple-element.23), channel_id=1, source_target_pairs={{0,8},{1,9},{2,10},{3,11},{4,12},{5,13},{6,14},{7,15},{8,16},{9,17... | collective-permute-start | bytes 98312 | tf_op jit(solution)/shard_map/ppermute | solution.py:526
  13.8 10.5 %collective-permute-start.2 = (f32[144,1024]{1,0:T(8,128)}, f32[144,1024]{1,0:T(8,128)S(1)}, u32[]{:S(2)}, u32[]{:S(2)}) collective-permute-start(f32[144,1024]{1,0:T(8,128)} %get-tuple-element.24), channel_id=1, source_target_pairs={{0,1},{1,0},{2,3},{3,2},{4,5},{5,4},{6,7},{7,6},{8,9},{9,8},{10,11... | collective-permute-start | bytes 1769480 | tf_op jit(solution)/shard_map/ppermute | solution.py:528
  13.8 10.5 %collective-permute-start.3 = (f32[144,1024]{1,0:T(8,128)}, f32[144,1024]{1,0:T(8,128)S(1)}, u32[]{:S(2)}, u32[]{:S(2)}) collective-permute-start(f32[144,1024]{1,0:T(8,128)} %get-tuple-element.24), channel_id=1, source_target_pairs={{1,2},{2,1},{3,4},{4,3},{5,6},{6,5},{9,10},{10,9},{11,12},{12,11},... | collective-permute-start | bytes 1769480 | tf_op jit(solution)/shard_map/ppermute | solution.py:529
  14.5 9.8 %collective-permute-start.1 = (f32[16,512]{1,0:T(8,128)S(1)}, f32[16,512]{1,0:T(8,128)S(1)}, u32[]{:S(2)}, u32[]{:S(2)}) collective-permute-start(f32[16,512]{1,0:T(8,128)S(1)} %get-tuple-element.23), channel_id=1, source_target_pairs={{8,0},{9,1},{10,2},{11,3},{12,4},{13,5},{14,6},{15,7},{16,8},{17,9... | collective-permute-start | bytes 98312 | tf_op jit(solution)/shard_map/ppermute | solution.py:527
  15.7 16.2 %collective-permute-start.4 = (f32[128,512]{1,0:T(8,128)S(1)}, f32[128,512]{1,0:T(8,128)}, u32[]{:S(2)}, u32[]{:S(2)}) collective-permute-start(f32[128,512]{1,0:T(8,128)S(1)} %get-tuple-element.32), channel_id=1, source_target_pairs={{0,8},{1,9},{2,10},{3,11},{4,12},{5,13},{6,14},{7,15},{8,16},{9,17... | collective-permute-start | bytes 786440 | tf_op jit(solution)/shard_map/ppermute | solution.py:524
  18.3 13.6 %collective-permute-start.5 = (f32[128,512]{1,0:T(8,128)S(1)}, f32[128,512]{1,0:T(8,128)}, u32[]{:S(2)}, u32[]{:S(2)}) collective-permute-start(f32[128,512]{1,0:T(8,128)S(1)} %get-tuple-element.32), channel_id=1, source_target_pairs={{8,0},{9,1},{10,2},{11,3},{12,4},{13,5},{14,6},{15,7},{16,8},{17,9... | collective-permute-start | bytes 786440 | tf_op jit(solution)/shard_map/ppermute | solution.py:525
  26.3 14.4 %all-to-all-start.1 = ((f32[32,3,4,128]{3,2,1,0:T(4,128)}), f32[32,3,4,128]{3,2,1,0:T(4,128)S(1)}, u32[]{:S(2)}, u32[]{:S(2)}) async-start(f32[32,3,4,128]{3,2,1,0:T(4,128)} %surface_first.1), calls=%async_computation.1 | async-start | bytes 393216 | tf_op jit(solution)/shard_map/all_to_all | solution.py:570

commit v6 on v5

--- a/solution.py
+++ b/solution.py
@@ -17,6 +17,7 @@
 ROW_FORCING = 13
 ROW_SURFACE = 14
 SMALL = 16
+PARALLEL = 4
 PART_INDEX = 192
 PART_WEIGHT = 200
 
@@ -116,7 +117,13 @@
     for copy in copies([(ssh8, heights), (send4, sends)], loaded):
         copy.wait()
     broadcast_heights(heights[...], heights, sends, payload)
-    for copy in copies([(payload, payload_out)], loaded.at[pl.ds(2, 1)]):
+    send_payload(payload, payload_out, loaded.at[pl.ds(2, PARALLEL)])
+
+
+def send_payload(source, target, semaphores):
+    count = source.shape[0] // PARALLEL
+    rows = [pl.ds(n * count, count) for n in range(PARALLEL)]
+    for copy in copies([(source.at[part], target.at[part]) for part in rows], semaphores):
         copy.wait()
 
 
@@ -251,8 +258,7 @@
         return
     ext_left[0:8, :] = final
     broadcast_heights(final, ext_left, sends, out)
-    for copy in copies([(out, out_ref)], stored):
-        copy.wait()
+    send_payload(out, out_ref, stored)
 
 
 def stage(sources, depth, target, width, offset, level):
@@ -281,6 +287,11 @@
         high = jnp.where(hit, highs[e], high)
         low = jnp.where(hit, lows[e], low)
     return high, low
+
+
+def weight_tiles(line, index, highs, lows, base, count):
+    tiles = [weight_tile(line, index, highs, lows, base + n * TILE) for n in range(count)]
+    return tuple(jnp.concatenate([tile[part] for tile in tiles], axis=0) for part in range(2))
 
 
 def tile_line():
@@ -360,9 +371,9 @@
         idx = [part[PART_INDEX + e : PART_INDEX + e + 1, here].astype(jnp.int32) for e in range(6)]
         highs, lows = split_weights(part.at[pl.ds(PART_WEIGHT, 8), :], here)
         total = jnp.zeros((3 * levels, TILE), jnp.float32)
-        for j in range(cells // TILE):
-            high, low = weight_tile(line, idx, highs, lows, cells + j * TILE)
-            columns = slice(j * TILE, (j + 1) * TILE)
+        for j in range(0, cells // TILE, 2):
+            high, low = weight_tiles(line, idx, highs, lows, cells + j * TILE, 2)
+            columns = slice(j * TILE, (j + 2) * TILE)
             total = total + product(rows_own, columns, high, low, levels)
         part[0 : 3 * levels, here] = total
         return carry
@@ -403,11 +414,12 @@
             idx.append(jnp.where(value < cells, value, outside))
         highs, lows = split_weights(part.at[pl.ds(PART_WEIGHT, 8), :], here)
         total = part[0 : 3 * levels, here]
-        for j in range(band + region):
-            base = start + j * TILE if j < band else 2 * cells + (j - band) * TILE
+        spans = [(start + j * TILE, min(3, band - j)) for j in range(0, band, 3)]
+        spans += [(2 * cells + j * TILE, min(2, region - j)) for j in range(0, region, 2)]
+        for base, count in spans:
             base = pl.multiple_of(base, TILE)
-            high, low = weight_tile(line, idx, highs, lows, base)
-            total = total + product(rows_ext, pl.ds(base, TILE), high, low, levels)
+            high, low = weight_tiles(line, idx, highs, lows, base, count)
+            total = total + product(rows_ext, pl.ds(base, count * TILE), high, low, levels)
         for b in range(TILE // LANES):
             cols = slice(b * LANES, (b + 1) * LANES)
             sub = pl.ds(start + b * LANES, LANES)
@@ -486,7 +498,7 @@
         out_shape=(payload_shape, jax.ShapeDtypeStruct((listed // LANES, LANES), jnp.int32)),
         in_specs=[HBM] * 2,
         out_specs=(HBM, VMEM),
-        scratch_shapes=[vmem(8, LANES), vmem(*payload_shape.shape), semaphores(3)],
+        scratch_shapes=[vmem(8, LANES), vmem(*payload_shape.shape), semaphores(2 + PARALLEL)],
         compiler_params=grant(8),
         cost_estimate=estimate(1000, 1000),
         name="heights",
@@ -559,7 +571,7 @@
             out_specs=VMEM if last else HBM,
             scratch_shapes=[vmem(8 * SMALL, LANES)] * 4
             + [vmem(32, LANES)] * 3
-            + [vmem(32, 8, LANES), vmem(*shape.shape), semaphores(1)],
+            + [vmem(32, 8, LANES), vmem(*shape.shape), semaphores(PARALLEL)],
             compiler_params=grant(8),
             cost_estimate=estimate(1000, 1000),
             name="surface_last" if last else "surface_first",

time: 43.1 us -> 43.1 us (level)
  transfers between devices with their start and end apart: 8 -> 8, of which waited for: 1 -> 2; matrix products, arithmetic and copies ran while one was open for 0% -> 0% of each run, Pallas kernels for 42% -> 41%
where the time goes in v6:
time: 43.1 us; the launch traced here: 42.3 us
  Pallas kernels  20.8 us (48%)
  starting transfers between devices  18.9 us (44%)
  waiting for transfers between devices  1.89 us (4%)
  between operations  0.74 us (2%)
    pallas_call x1, Pallas kernels, body(): pl.pallas_call(tracer_kernel, out_shape=(jax.ShapeDtypeStruct((levels, ce...  8.61 us
    all_to_all x1, starting transfers between devices, body(): heights = lax.all_to_all(payload, AXES, 0, 0)  7.3 us
    all_to_all x1, starting transfers between devices, body(): heights2 = lax.all_to_all(subcycles(heights, False), AXES, 0, 0)  5.64 us
    pallas_call x1, Pallas kernels, body(): pl.pallas_call(local_kernel, out_shape=(jax.ShapeDtypeStruct((3, 8 * leve...  4.4 us
    pallas_call x2, Pallas kernels, subcycles(): pl.pallas_call(functools.partial(surface_kernel, last=last, shape=(region...  3.72 us
    pallas_call x1, Pallas kernels, body(): pl.pallas_call(pick_kernel, out_shape=(jax.ShapeDtypeStruct((SMALL, cells...  2.37 us
    ppermute x1, starting transfers between devices, body(): small_below = lax.ppermute(picked_small, AXES, upward)  1.82 us
    all_to_all x1, waiting for transfers between devices, body(): heights = lax.all_to_all(payload, AXES, 0, 0)  1.77 us
  transfers between devices with their start and end apart: 8, of which 2 were waited for; matrix products, arithmetic and copies ran while one was open for 0% of the time, Pallas kernels for 41%

profile of v6, /device:TPU:0, one launch (start us, length us, event | category | flops | bytes accessed | tf_op | source)
XLA Modules:
  0.0 42.3 jit_solution(4654980774097378958)
XLA Ops:
  0.6 1.7 %heights.1 = (f32[32,3,4,128]{3,2,1,0:T(4,128)}, s32[4,128]{1,0:T(4,128)S(1)}) custom-call(f32[8,128]{1,0:T(8,128)} %bitcast.4, s32[4,128]{1,0:T(4,128)} %bitcast.6), custom_call_target="tpu_custom_call" | custom-call | flops 1000 | bytes 1000 | tf_op jit(solution)/shard_map/heights/pallas_call | solution.py:496
  2.3 7.3 %all-to-all-start = ((f32[32,3,4,128]{3,2,1,0:T(4,128)}), f32[32,3,4,128]{3,2,1,0:T(4,128)S(1)}, u32[]{:S(2)}, u32[]{:S(2)}) async-start(f32[32,3,4,128]{3,2,1,0:T(4,128)} %get-tuple-element.25), calls=%async_computation | async-start | bytes 393216 | tf_op jit(solution)/shard_map/all_to_all | solution.py:542
  9.6 2.4 %pick.1 = (f32[16,1024]{1,0:T(8,128)S(1)}, f32[128,512]{1,0:T(8,128)S(1)}, f32[16,512]{1,0:T(8,128)S(1)}, f32[144,1024]{1,0:T(8,128)}) custom-call(f32[64,1024]{1,0:T(8,128)} %theta_in.5, f32[64,1024]{1,0:T(8,128)} %salt_in.5, s32[8,128]{1,0:T(8,128)} %bitcast.8, f32[8,128]{1,0:T(8,128)} %bitcast.5, s32[6,1024]{1,0:T(8,128)} %neighbors.1, ...), custom_call_target="tpu_custom_call" | custom-call | flops 2000000 | bytes 2000000 | tf_op jit(solution)/shard_map/pick/pallas_call | solution.py:506
  12.0 1.8 %collective-permute-start = (f32[16,512]{1,0:T(8,128)S(1)}, f32[16,512]{1,0:T(8,128)S(1)}, u32[]{:S(2)}, u32[]{:S(2)}) collective-permute-start(f32[16,512]{1,0:T(8,128)S(1)} %get-tuple-element.23), channel_id=1, source_target_pairs={{0,8},{1,9},{2,10},{3,11},{4,12},{5,13},{6,14},{7,15},{8,16},{9,17... | collective-permute-start | bytes 98312 | tf_op jit(solution)/shard_map/ppermute | solution.py:538
  13.8 0.0 collective-permute-start.2
  13.8 0.7 %collective-permute-start.3 = (f32[144,1024]{1,0:T(8,128)}, f32[144,1024]{1,0:T(8,128)S(1)}, u32[]{:S(2)}, u32[]{:S(2)}) collective-permute-start(f32[144,1024]{1,0:T(8,128)} %get-tuple-element.24), channel_id=1, source_target_pairs={{1,2},{2,1},{3,4},{4,3},{5,6},{6,5},{9,10},{10,9},{11,12},{12,11},... | collective-permute-start | bytes 1769480 | tf_op jit(solution)/shard_map/ppermute | solution.py:541
  14.5 1.2 %collective-permute-start.1 = (f32[16,512]{1,0:T(8,128)S(1)}, f32[16,512]{1,0:T(8,128)S(1)}, u32[]{:S(2)}, u32[]{:S(2)}) collective-permute-start(f32[16,512]{1,0:T(8,128)S(1)} %get-tuple-element.23), channel_id=1, source_target_pairs={{8,0},{9,1},{10,2},{11,3},{12,4},{13,5},{14,6},{15,7},{16,8},{17,9... | collective-permute-start | bytes 98312 | tf_op jit(solution)/shard_map/ppermute | solution.py:539
  15.7 0.9 %collective-permute-start.4 = (f32[128,512]{1,0:T(8,128)S(1)}, f32[128,512]{1,0:T(8,128)}, u32[]{:S(2)}, u32[]{:S(2)}) collective-permute-start(f32[128,512]{1,0:T(8,128)S(1)} %get-tuple-element.32), channel_id=1, source_target_pairs={{0,8},{1,9},{2,10},{3,11},{4,12},{5,13},{6,14},{7,15},{8,16},{9,17... | collective-permute-start | bytes 786440 | tf_op jit(solution)/shard_map/ppermute | solution.py:536
  16.6 1.8 %all-to-all-done.heights = f32[32,3,4,128]{3,2,1,0:T(4,128)S(1)} async-done(((f32[32,3,4,128]{3,2,1,0:T(4,128)}), f32[32,3,4,128]{3,2,1,0:T(4,128)S(1)}, u32[]{:S(2)}, u32[]{:S(2)}) %all-to-all-start) | async-done | bytes 196640 | tf_op jit(solution)/shard_map/all_to_all | solution.py:542
  18.4 0.0 collective-permute-done.small_below.below
  18.4 1.4 %collective-permute-start.5 = (f32[128,512]{1,0:T(8,128)S(1)}, f32[128,512]{1,0:T(8,128)}, u32[]{:S(2)}, u32[]{:S(2)}) collective-permute-start(f32[128,512]{1,0:T(8,128)S(1)} %get-tuple-element.32), channel_id=1, source_target_pairs={{8,0},{9,1},{10,2},{11,3},{12,4},{13,5},{14,6},{15,7},{16,8},{17,9... | collective-permute-start | bytes 786440 | tf_op jit(solution)/shard_map/ppermute | solution.py:537
  19.8 4.4 %local.1 = (f32[3,512,128]{2,1,0:T(8,128)S(1)}, f32[208,1024]{1,0:T(8,128)S(1)}) custom-call(f32[64,1024]{1,0:T(8,128)} %theta_in.5, f32[64,1024]{1,0:T(8,128)} %salt_in.5, f32[16,1024]{1,0:T(8,128)S(1)} %get-tuple-element.27.small.own_in, f32[63,1024]{1,0:T(8,128)} %kappa_in.1, s32[8,128]{1,0:T(8,128)} %bitcast.9), custom_call_target="tpu_custom_call" | custom-call | flops 40000000000 | bytes 4000000 | tf_op jit(solution)/shard_map/local/pallas_call | solution.py:544
  24.2 0.0 collective-permute-done.1.small_above.above
  24.2 0.0 collective-permute-done.2.swap_in
  24.2 0.0 collective-permute-done.3.swap_out
  24.2 2.0 %surface_first.1 = f32[32,3,4,128]{3,2,1,0:T(4,128)} custom-call(f32[16,512]{1,0:T(8,128)S(1)} %collective-permute-done.small_below.below, f32[16,512]{1,0:T(8,128)S(1)} %collective-permute-done.1.small_above.above, f32[32,3,4,128]{3,2,1,0:T(4,128)S(1)} %all-to-all-done.heights, f32[16,1024]{1,0:T(8,128)S(1)} %get-tuple-element.27.small.own_in, ...), custom_call_target="tpu_custom_call" | custom-call | flops 1000 | bytes 1000 | tf_op jit(solution)/shard_map/surface_first/pallas_call | solution.py:567
  26.2 5.6 %all-to-all-start.1 = ((f32[32,3,4,128]{3,2,1,0:T(4,128)}), f32[32,3,4,128]{3,2,1,0:T(4,128)S(1)}, u32[]{:S(2)}, u32[]{:S(2)}) async-start(f32[32,3,4,128]{3,2,1,0:T(4,128)} %surface_first.1), calls=%async_computation.1 | async-start | bytes 393216 | tf_op jit(solution)/shard_map/all_to_all | solution.py:582
  31.9 0.0 collective-permute-done.4.below
  31.9 0.0 collective-permute-done.5.above
  31.9 8.6 %tracers.1 = (f32[64,1024]{1,0:T(8,128)}, f32[64,1024]{1,0:T(8,128)}) custom-call(f32[64,1024]{1,0:T(8,128)} %theta_in.5, f32[64,1024]{1,0:T(8,128)} %salt_in.5, f32[16,1024]{1,0:T(8,128)S(1)} %get-tuple-element.27.small.own_in, f32[16,512]{1,0:T(8,128)S(1)} %collective-permute-done.small_below.below, ...), custom_call_target="tpu_custom_call" | custom-call | flops 4000000000 | bytes 8000000 | tf_op jit(solution)/shard_map/tracers/pallas_call | solution.py:584
  40.5 0.1 all-to-all-done.1.heights
  40.6 1.7 %surface_last.1 = f32[8,128]{1,0:T(8,128)} custom-call(f32[16,512]{1,0:T(8,128)S(1)} %collective-permute-done.small_below.below, f32[16,512]{1,0:T(8,128)S(1)} %collective-permute-done.1.small_above.above, f32[32,3,4,128]{3,2,1,0:T(4,128)S(1)} %all-to-all-done.1.heights, f32[16,1024]{1,0:T(8,128)S(1)} %get-tuple-element.27.small.own_in, ...), custom_call_target="tpu_custom_call" | custom-call | flops 1000 | bytes 1000 | tf_op jit(solution)/shard_map/surface_last/pallas_call | solution.py:567
Async XLA Ops:
  2.3 16.1 %all-to-all-start = ((f32[32,3,4,128]{3,2,1,0:T(4,128)}), f32[32,3,4,128]{3,2,1,0:T(4,128)S(1)}, u32[]{:S(2)}, u32[]{:S(2)}) async-start(f32[32,3,4,128]{3,2,1,0:T(4,128)} %get-tuple-element.25), calls=%async_computation | async-start | bytes 393216 | tf_op jit(solution)/shard_map/all_to_all | solution.py:542
  12.0 6.4 %collective-permute-start = (f32[16,512]{1,0:T(8,128)S(1)}, f32[16,512]{1,0:T(8,128)S(1)}, u32[]{:S(2)}, u32[]{:S(2)}) collective-permute-start(f32[16,512]{1,0:T(8,128)S(1)} %get-tuple-element.23), channel_id=1, source_target_pairs={{0,8},{1,9},{2,10},{3,11},{4,12},{5,13},{6,14},{7,15},{8,16},{9,17... | collective-permute-start | bytes 98312 | tf_op jit(solution)/shard_map/ppermute | solution.py:538
  13.8 10.4 %collective-permute-start.2 = (f32[144,1024]{1,0:T(8,128)}, f32[144,1024]{1,0:T(8,128)S(1)}, u32[]{:S(2)}, u32[]{:S(2)}) collective-permute-start(f32[144,1024]{1,0:T(8,128)} %get-tuple-element.24), channel_id=1, source_target_pairs={{0,1},{1,0},{2,3},{3,2},{4,5},{5,4},{6,7},{7,6},{8,9},{9,8},{10,11... | collective-permute-start | bytes 1769480 | tf_op jit(solution)/shard_map/ppermute | solution.py:540
  13.8 10.4 %collective-permute-start.3 = (f32[144,1024]{1,0:T(8,128)}, f32[144,1024]{1,0:T(8,128)S(1)}, u32[]{:S(2)}, u32[]{:S(2)}) collective-permute-start(f32[144,1024]{1,0:T(8,128)} %get-tuple-element.24), channel_id=1, source_target_pairs={{1,2},{2,1},{3,4},{4,3},{5,6},{6,5},{9,10},{10,9},{11,12},{12,11},... | collective-permute-start | bytes 1769480 | tf_op jit(solution)/shard_map/ppermute | solution.py:541
  14.5 9.7 %collective-permute-start.1 = (f32[16,512]{1,0:T(8,128)S(1)}, f32[16,512]{1,0:T(8,128)S(1)}, u32[]{:S(2)}, u32[]{:S(2)}) collective-permute-start(f32[16,512]{1,0:T(8,128)S(1)} %get-tuple-element.23), channel_id=1, source_target_pairs={{8,0},{9,1},{10,2},{11,3},{12,4},{13,5},{14,6},{15,7},{16,8},{17,9... | collective-permute-start | bytes 98312 | tf_op jit(solution)/shard_map/ppermute | solution.py:539
  15.7 16.2 %collective-permute-start.4 = (f32[128,512]{1,0:T(8,128)S(1)}, f32[128,512]{1,0:T(8,128)}, u32[]{:S(2)}, u32[]{:S(2)}) collective-permute-start(f32[128,512]{1,0:T(8,128)S(1)} %get-tuple-element.32), channel_id=1, source_target_pairs={{0,8},{1,9},{2,10},{3,11},{4,12},{5,13},{6,14},{7,15},{8,16},{9,17... | collective-permute-start | bytes 786440 | tf_op jit(solution)/shard_map/ppermute | solution.py:536
  18.4 13.5 %collective-permute-start.5 = (f32[128,512]{1,0:T(8,128)S(1)}, f32[128,512]{1,0:T(8,128)}, u32[]{:S(2)}, u32[]{:S(2)}) collective-permute-start(f32[128,512]{1,0:T(8,128)S(1)} %get-tuple-element.32), channel_id=1, source_target_pairs={{8,0},{9,1},{10,2},{11,3},{12,4},{13,5},{14,6},{15,7},{16,8},{17,9... | collective-permute-start | bytes 786440 | tf_op jit(solution)/shard_map/ppermute | solution.py:537
  26.2 14.4 %all-to-all-start.1 = ((f32[32,3,4,128]{3,2,1,0:T(4,128)}), f32[32,3,4,128]{3,2,1,0:T(4,128)S(1)}, u32[]{:S(2)}, u32[]{:S(2)}) async-start(f32[32,3,4,128]{3,2,1,0:T(4,128)} %surface_first.1), calls=%async_computation.1 | async-start | bytes 393216 | tf_op jit(solution)/shard_map/all_to_all | solution.py:582

commit v7 on v6

--- a/solution.py
+++ b/solution.py
@@ -98,8 +98,8 @@
         arrivals[5 + c].wait()
         target = message.at[pl.ds(c * levels, levels), :]
         departures += copies([(tracer, target)], stored.at[pl.ds(c, 1)])
-    pick(theta, picked, levels // 8, 0)
-    pick(salt, picked, levels // 8, levels)
+        if c == 0:
+            pick(theta, picked, levels // 8, 0)
     for b in range(blocks):
         cols = slice(b * LANES, (b + 1) * LANES)
         term = 0.2 * theta[:, cols] - 0.15 * salt[:, cols]
@@ -108,6 +108,7 @@
         small[ROW_FORCING : ROW_FORCING + 1, cols] = total / math.sqrt(levels)
     rest = message.at[pl.ds(2 * levels, SMALL), :]
     departures += copies([(small, rest)], stored.at[pl.ds(2, 1)])
+    pick(salt, picked, levels // 8, levels)
     pick(small, picked_small, SMALL // 8, 0)
     for copy in departures:
         copy.wait()

time: 43.1 us -> 43.1 us (level)
  no operation moved by 1% of the time
where the time goes in v7:
time: 43.1 us; the launch traced here: 42.3 us
  Pallas kernels  20.8 us (48%)
  starting transfers between devices  18.9 us (44%)
  waiting for transfers between devices  1.89 us (4%)
  between operations  0.74 us (2%)
    pallas_call x1, Pallas kernels, body(): pl.pallas_call(tracer_kernel, out_shape=(jax.ShapeDtypeStruct((levels, ce...  8.61 us
    all_to_all x1, starting transfers between devices, body(): heights = lax.all_to_all(payload, AXES, 0, 0)  7.3 us
    all_to_all x1, starting transfers between devices, body(): heights2 = lax.all_to_all(subcycles(heights, False), AXES, 0, 0)  5.64 us
    pallas_call x1, Pallas kernels, body(): pl.pallas_call(local_kernel, out_shape=(jax.ShapeDtypeStruct((3, 8 * leve...  4.4 us
    pallas_call x2, Pallas kernels, subcycles(): pl.pallas_call(functools.partial(surface_kernel, last=last, shape=(region...  3.72 us
    pallas_call x1, Pallas kernels, body(): pl.pallas_call(pick_kernel, out_shape=(jax.ShapeDtypeStruct((SMALL, cells...  2.37 us
    ppermute x1, starting transfers between devices, body(): small_below = lax.ppermute(picked_small, AXES, upward)  1.82 us
    all_to_all x1, waiting for transfers between devices, body(): heights = lax.all_to_all(payload, AXES, 0, 0)  1.77 us
  transfers between devices with their start and end apart: 8, of which 2 were waited for; matrix products, arithmetic and copies ran while one was open for 0% of the time, Pallas kernels for 41%

profile of v7, /device:TPU:0, one launch (start us, length us, event | category | flops | bytes accessed | tf_op | source)
XLA Modules:
  0.0 42.3 jit_solution(14861302187741825467)
XLA Ops:
  0.6 1.7 %heights.1 = (f32[32,3,4,128]{3,2,1,0:T(4,128)}, s32[4,128]{1,0:T(4,128)S(1)}) custom-call(f32[8,128]{1,0:T(8,128)} %bitcast.4, s32[4,128]{1,0:T(4,128)} %bitcast.6), custom_call_target="tpu_custom_call" | custom-call | flops 1000 | bytes 1000 | tf_op jit(solution)/shard_map/heights/pallas_call | solution.py:497
  2.3 7.3 %all-to-all-start = ((f32[32,3,4,128]{3,2,1,0:T(4,128)}), f32[32,3,4,128]{3,2,1,0:T(4,128)S(1)}, u32[]{:S(2)}, u32[]{:S(2)}) async-start(f32[32,3,4,128]{3,2,1,0:T(4,128)} %get-tuple-element.25), calls=%async_computation | async-start | bytes 393216 | tf_op jit(solution)/shard_map/all_to_all | solution.py:543
  9.6 2.4 %pick.1 = (f32[16,1024]{1,0:T(8,128)S(1)}, f32[128,512]{1,0:T(8,128)S(1)}, f32[16,512]{1,0:T(8,128)S(1)}, f32[144,1024]{1,0:T(8,128)}) custom-call(f32[64,1024]{1,0:T(8,128)} %theta_in.5, f32[64,1024]{1,0:T(8,128)} %salt_in.5, s32[8,128]{1,0:T(8,128)} %bitcast.8, f32[8,128]{1,0:T(8,128)} %bitcast.5, s32[6,1024]{1,0:T(8,128)} %neighbors.1, ...), custom_call_target="tpu_custom_call" | custom-call | flops 2000000 | bytes 2000000 | tf_op jit(solution)/shard_map/pick/pallas_call | solution.py:507
  12.0 1.8 %collective-permute-start = (f32[16,512]{1,0:T(8,128)S(1)}, f32[16,512]{1,0:T(8,128)S(1)}, u32[]{:S(2)}, u32[]{:S(2)}) collective-permute-start(f32[16,512]{1,0:T(8,128)S(1)} %get-tuple-element.23), channel_id=1, source_target_pairs={{0,8},{1,9},{2,10},{3,11},{4,12},{5,13},{6,14},{7,15},{8,16},{9,17... | collective-permute-start | bytes 98312 | tf_op jit(solution)/shard_map/ppermute | solution.py:539
  13.8 0.0 collective-permute-start.2
  13.8 0.7 %collective-permute-start.3 = (f32[144,1024]{1,0:T(8,128)}, f32[144,1024]{1,0:T(8,128)S(1)}, u32[]{:S(2)}, u32[]{:S(2)}) collective-permute-start(f32[144,1024]{1,0:T(8,128)} %get-tuple-element.24), channel_id=1, source_target_pairs={{1,2},{2,1},{3,4},{4,3},{5,6},{6,5},{9,10},{10,9},{11,12},{12,11},... | collective-permute-start | bytes 1769480 | tf_op jit(solution)/shard_map/ppermute | solution.py:542
  14.5 1.2 %collective-permute-start.1 = (f32[16,512]{1,0:T(8,128)S(1)}, f32[16,512]{1,0:T(8,128)S(1)}, u32[]{:S(2)}, u32[]{:S(2)}) collective-permute-start(f32[16,512]{1,0:T(8,128)S(1)} %get-tuple-element.23), channel_id=1, source_target_pairs={{8,0},{9,1},{10,2},{11,3},{12,4},{13,5},{14,6},{15,7},{16,8},{17,9... | collective-permute-start | bytes 98312 | tf_op jit(solution)/shard_map/ppermute | solution.py:540
  15.7 0.9 %collective-permute-start.4 = (f32[128,512]{1,0:T(8,128)S(1)}, f32[128,512]{1,0:T(8,128)}, u32[]{:S(2)}, u32[]{:S(2)}) collective-permute-start(f32[128,512]{1,0:T(8,128)S(1)} %get-tuple-element.32), channel_id=1, source_target_pairs={{0,8},{1,9},{2,10},{3,11},{4,12},{5,13},{6,14},{7,15},{8,16},{9,17... | collective-permute-start | bytes 786440 | tf_op jit(solution)/shard_map/ppermute | solution.py:537
  16.6 1.8 %all-to-all-done.heights = f32[32,3,4,128]{3,2,1,0:T(4,128)S(1)} async-done(((f32[32,3,4,128]{3,2,1,0:T(4,128)}), f32[32,3,4,128]{3,2,1,0:T(4,128)S(1)}, u32[]{:S(2)}, u32[]{:S(2)}) %all-to-all-start) | async-done | bytes 196640 | tf_op jit(solution)/shard_map/all_to_all | solution.py:543
  18.4 0.0 collective-permute-done.small_below.below
  18.4 1.4 %collective-permute-start.5 = (f32[128,512]{1,0:T(8,128)S(1)}, f32[128,512]{1,0:T(8,128)}, u32[]{:S(2)}, u32[]{:S(2)}) collective-permute-start(f32[128,512]{1,0:T(8,128)S(1)} %get-tuple-element.32), channel_id=1, source_target_pairs={{8,0},{9,1},{10,2},{11,3},{12,4},{13,5},{14,6},{15,7},{16,8},{17,9... | collective-permute-start | bytes 786440 | tf_op jit(solution)/shard_map/ppermute | solution.py:538
  19.8 4.4 %local.1 = (f32[3,512,128]{2,1,0:T(8,128)S(1)}, f32[208,1024]{1,0:T(8,128)S(1)}) custom-call(f32[64,1024]{1,0:T(8,128)} %theta_in.5, f32[64,1024]{1,0:T(8,128)} %salt_in.5, f32[16,1024]{1,0:T(8,128)S(1)} %get-tuple-element.27.small.own_in, f32[63,1024]{1,0:T(8,128)} %kappa_in.1, s32[8,128]{1,0:T(8,128)} %bitcast.9), custom_call_target="tpu_custom_call" | custom-call | flops 40000000000 | bytes 4000000 | tf_op jit(solution)/shard_map/local/pallas_call | solution.py:545
  24.2 0.0 collective-permute-done.1.small_above.above
  24.2 0.0 collective-permute-done.2.swap_in
  24.2 0.0 collective-permute-done.3.swap_out
  24.2 2.0 %surface_first.1 = f32[32,3,4,128]{3,2,1,0:T(4,128)} custom-call(f32[16,512]{1,0:T(8,128)S(1)} %collective-permute-done.small_below.below, f32[16,512]{1,0:T(8,128)S(1)} %collective-permute-done.1.small_above.above, f32[32,3,4,128]{3,2,1,0:T(4,128)S(1)} %all-to-all-done.heights, f32[16,1024]{1,0:T(8,128)S(1)} %get-tuple-element.27.small.own_in, ...), custom_call_target="tpu_custom_call" | custom-call | flops 1000 | bytes 1000 | tf_op jit(solution)/shard_map/surface_first/pallas_call | solution.py:568
  26.2 5.6 %all-to-all-start.1 = ((f32[32,3,4,128]{3,2,1,0:T(4,128)}), f32[32,3,4,128]{3,2,1,0:T(4,128)S(1)}, u32[]{:S(2)}, u32[]{:S(2)}) async-start(f32[32,3,4,128]{3,2,1,0:T(4,128)} %surface_first.1), calls=%async_computation.1 | async-start | bytes 393216 | tf_op jit(solution)/shard_map/all_to_all | solution.py:583
  31.9 0.0 collective-permute-done.4.below
  31.9 0.0 collective-permute-done.5.above
  31.9 8.6 %tracers.1 = (f32[64,1024]{1,0:T(8,128)}, f32[64,1024]{1,0:T(8,128)}) custom-call(f32[64,1024]{1,0:T(8,128)} %theta_in.5, f32[64,1024]{1,0:T(8,128)} %salt_in.5, f32[16,1024]{1,0:T(8,128)S(1)} %get-tuple-element.27.small.own_in, f32[16,512]{1,0:T(8,128)S(1)} %collective-permute-done.small_below.below, ...), custom_call_target="tpu_custom_call" | custom-call | flops 4000000000 | bytes 8000000 | tf_op jit(solution)/shard_map/tracers/pallas_call | solution.py:585
  40.5 0.1 all-to-all-done.1.heights
  40.6 1.7 %surface_last.1 = f32[8,128]{1,0:T(8,128)} custom-call(f32[16,512]{1,0:T(8,128)S(1)} %collective-permute-done.small_below.below, f32[16,512]{1,0:T(8,128)S(1)} %collective-permute-done.1.small_above.above, f32[32,3,4,128]{3,2,1,0:T(4,128)S(1)} %all-to-all-done.1.heights, f32[16,1024]{1,0:T(8,128)S(1)} %get-tuple-element.27.small.own_in, ...), custom_call_target="tpu_custom_call" | custom-call | flops 1000 | bytes 1000 | tf_op jit(solution)/shard_map/surface_last/pallas_call | solution.py:568
Async XLA Ops:
  2.3 16.1 %all-to-all-start = ((f32[32,3,4,128]{3,2,1,0:T(4,128)}), f32[32,3,4,128]{3,2,1,0:T(4,128)S(1)}, u32[]{:S(2)}, u32[]{:S(2)}) async-start(f32[32,3,4,128]{3,2,1,0:T(4,128)} %get-tuple-element.25), calls=%async_computation | async-start | bytes 393216 | tf_op jit(solution)/shard_map/all_to_all | solution.py:543
  12.0 6.4 %collective-permute-start = (f32[16,512]{1,0:T(8,128)S(1)}, f32[16,512]{1,0:T(8,128)S(1)}, u32[]{:S(2)}, u32[]{:S(2)}) collective-permute-start(f32[16,512]{1,0:T(8,128)S(1)} %get-tuple-element.23), channel_id=1, source_target_pairs={{0,8},{1,9},{2,10},{3,11},{4,12},{5,13},{6,14},{7,15},{8,16},{9,17... | collective-permute-start | bytes 98312 | tf_op jit(solution)/shard_map/ppermute | solution.py:539
  13.8 10.4 %collective-permute-start.2 = (f32[144,1024]{1,0:T(8,128)}, f32[144,1024]{1,0:T(8,128)S(1)}, u32[]{:S(2)}, u32[]{:S(2)}) collective-permute-start(f32[144,1024]{1,0:T(8,128)} %get-tuple-element.24), channel_id=1, source_target_pairs={{0,1},{1,0},{2,3},{3,2},{4,5},{5,4},{6,7},{7,6},{8,9},{9,8},{10,11... | collective-permute-start | bytes 1769480 | tf_op jit(solution)/shard_map/ppermute | solution.py:541
  13.8 10.4 %collective-permute-start.3 = (f32[144,1024]{1,0:T(8,128)}, f32[144,1024]{1,0:T(8,128)S(1)}, u32[]{:S(2)}, u32[]{:S(2)}) collective-permute-start(f32[144,1024]{1,0:T(8,128)} %get-tuple-element.24), channel_id=1, source_target_pairs={{1,2},{2,1},{3,4},{4,3},{5,6},{6,5},{9,10},{10,9},{11,12},{12,11},... | collective-permute-start | bytes 1769480 | tf_op jit(solution)/shard_map/ppermute | solution.py:542
  14.5 9.7 %collective-permute-start.1 = (f32[16,512]{1,0:T(8,128)S(1)}, f32[16,512]{1,0:T(8,128)S(1)}, u32[]{:S(2)}, u32[]{:S(2)}) collective-permute-start(f32[16,512]{1,0:T(8,128)S(1)} %get-tuple-element.23), channel_id=1, source_target_pairs={{8,0},{9,1},{10,2},{11,3},{12,4},{13,5},{14,6},{15,7},{16,8},{17,9... | collective-permute-start | bytes 98312 | tf_op jit(solution)/shard_map/ppermute | solution.py:540
  15.7 16.2 %collective-permute-start.4 = (f32[128,512]{1,0:T(8,128)S(1)}, f32[128,512]{1,0:T(8,128)}, u32[]{:S(2)}, u32[]{:S(2)}) collective-permute-start(f32[128,512]{1,0:T(8,128)S(1)} %get-tuple-element.32), channel_id=1, source_target_pairs={{0,8},{1,9},{2,10},{3,11},{4,12},{5,13},{6,14},{7,15},{8,16},{9,17... | collective-permute-start | bytes 786440 | tf_op jit(solution)/shard_map/ppermute | solution.py:537
  18.4 13.5 %collective-permute-start.5 = (f32[128,512]{1,0:T(8,128)S(1)}, f32[128,512]{1,0:T(8,128)}, u32[]{:S(2)}, u32[]{:S(2)}) collective-permute-start(f32[128,512]{1,0:T(8,128)S(1)} %get-tuple-element.32), channel_id=1, source_target_pairs={{8,0},{9,1},{10,2},{11,3},{12,4},{13,5},{14,6},{15,7},{16,8},{17,9... | collective-permute-start | bytes 786440 | tf_op jit(solution)/shard_map/ppermute | solution.py:538
  26.2 14.4 %all-to-all-start.1 = ((f32[32,3,4,128]{3,2,1,0:T(4,128)}), f32[32,3,4,128]{3,2,1,0:T(4,128)S(1)}, u32[]{:S(2)}, u32[]{:S(2)}) async-start(f32[32,3,4,128]{3,2,1,0:T(4,128)} %surface_first.1), calls=%async_computation.1 | async-start | bytes 393216 | tf_op jit(solution)/shard_map/all_to_all | solution.py:583
